TPU v7x, 32 devices: a whole 2x2x4 slice. The times are simulated.
32 devices in a mesh: dap: 32 (over z, y, x, core).
Axes of the slice: x: 2, y: 2, z: 4, core: 2. Of those that a mesh axis runs over, the one named last changes fastest.
Arguments:
- homolog_stack: float32 [64, 64, 256], P('dap'), may hold values from -5 to 5
- couple_tensor: float32 [64, 64, 128], P('dap'), may hold values from -6 to 6
- homolog_presence: int32 [64, 64], P('dap'), may hold values from 0 to 1
- amino_presence: int32 [64], replicated, may hold values 0 or 1
- horizontal_standard_factor: float32 [256], replicated, may hold values from 0.5 to 1.5
- horizontal_asking_matrix: bfloat16 [256, 256], replicated, may hold values from -7 to 7
- horizontal_lookup_triple: bfloat16 [256, 768], replicated, may hold values from -0.375 to 0.375
- horizontal_final_matrix: bfloat16 [256, 256], replicated, may hold values from -0.375 to 0.375
- couple_offset_factor: float32 [128], replicated, may hold values from 0.5 to 1.5
- couple_offset_matrix: bfloat16 [128, 8], replicated, may hold values from -2 to 2
- vertical_standard_factor: float32 [256], replicated, may hold values from 0.5 to 1.5
- vertical_asking_matrix: bfloat16 [256, 256], replicated, may hold values from -7 to 7
- vertical_lookup_triple: bfloat16 [256, 768], replicated, may hold values from -0.375 to 0.375
- vertical_final_matrix: bfloat16 [256, 256], replicated, may hold values from -0.375 to 0.375
- tensor_average_factor: float32 [256], replicated, may hold values from 0.5 to 1.5
- tensor_average_mapping: bfloat16 [256, 64], replicated, may hold values from -0.375 to 0.375
- tensor_average_final: bfloat16 [1024, 128], replicated, may hold values from -0.375 to 0.375
- trio_entry_factors: float32 [2, 128], replicated, may hold values from 0.5 to 1.5
- trio_flank_mappings: bfloat16 [2, 128, 512], replicated, may hold values from -0.5 to 0.5
- trio_final_switches: bfloat16 [2, 128, 128], replicated, may hold values from -0.5 to 0.5
- trio_multiplied_factors: float32 [2, 128], replicated, may hold values from 0.5 to 1.5
- trio_final_matrices: bfloat16 [2, 128, 128], replicated, may hold values from -1 to 1
Outputs:
- msa_out: float32 [64, 64, 256], P(None, 'dap')
- pair_out: float32 [64, 64, 128], P('dap')
All inputs are finite; a program needn't handle non-finite values.
Results may differ from a plain program's by a relative error of at most 0.015.
Values may be sent and summed in bfloat16 or wider, within the bound.
No kernel may reach another device: no remote copies, remote signals or barrier semaphores. Data moves between devices by JAX's collectives and lax.ppermute only.
A program may use at most 64 MiB of HBM per device.

v0:
```python
import math

import jax
import jax.numpy as jnp
from jax import lax
from jax.sharding import PartitionSpec as P

FOCUS_NUMBER = 8
PER_FOCUS_WIDTH = 32
TENSOR_HIDDEN = 32
TRI_HID = 128


EPSILON = 1e-05
MASK_PENALTY_SCALE = 1000000000.0


def standardize_features(content_vectors, gain, axis):
    centred = content_vectors - jnp.mean(content_vectors, axis=axis, keepdims=True)
    spread = jnp.mean(centred * centred, axis=axis, keepdims=True)
    return centred * lax.rsqrt(spread + EPSILON) * gain


def triangle(
    pair_now, gain_in, proj_weight, gate_weight, gain_mid, final_weight, amino_presence, incoming
):
    hidden = TRI_HID
    row_count = pair_now.shape[0]
    my_index = lax.axis_index("dap")
    standardized_source = standardize_features(pair_now, gain_in, -1).astype(jnp.bfloat16)
    projected = jnp.einsum(
        "rkd,de->erk", standardized_source, proj_weight, preferred_element_type=jnp.float32
    )
    res_float = amino_presence.astype(jnp.float32)
    own_rows = lax.dynamic_slice_in_dim(res_float, my_index * row_count, row_count)
    pair_mask = own_rows[:, None] * res_float[None, :]
    left_side = (
        jax.nn.sigmoid(projected[hidden : 2 * hidden]) * projected[:hidden] * pair_mask[None]
    ).astype(jnp.bfloat16)
    right_side = (
        jax.nn.sigmoid(projected[3 * hidden :])
        * projected[2 * hidden : 3 * hidden]
        * pair_mask[None]
    ).astype(jnp.bfloat16)
    gating = jax.nn.sigmoid(
        jnp.dot(standardized_source, gate_weight, preferred_element_type=jnp.float32)
    )
    left_chan, right_chan = (
        lax.all_to_all(left_side, "dap", split_axis=0, concat_axis=1, tiled=True),
        lax.all_to_all(right_side, "dap", split_axis=0, concat_axis=1, tiled=True),
    )
    if incoming:
        product = jnp.einsum(
            "cki,ckj->cij", left_chan, right_chan, preferred_element_type=jnp.float32
        )
    else:
        product = jnp.einsum(
            "cik,cjk->cij", left_chan, right_chan, preferred_element_type=jnp.float32
        )
    product = product.astype(jnp.bfloat16)
    returned = lax.all_to_all(product, "dap", split_axis=1, concat_axis=0, tiled=True)
    product_normed = standardize_features(
        returned.astype(jnp.float32), gain_mid[:, None, None], 0
    ).astype(jnp.bfloat16)
    update = jnp.einsum(
        "crj,cd->rjd", product_normed, final_weight, preferred_element_type=jnp.float32
    )
    return pair_now + update * gating


def shards(
    homolog_stack,
    couple_tensor,
    homolog_presence,
    amino_presence,
    horizontal_standard_factor,
    horizontal_asking_matrix,
    horizontal_lookup_triple,
    horizontal_final_matrix,
    couple_offset_factor,
    couple_offset_matrix,
    vertical_standard_factor,
    vertical_asking_matrix,
    vertical_lookup_triple,
    vertical_final_matrix,
    tensor_average_factor,
    tensor_average_mapping,
    tensor_average_final,
    trio_entry_factors,
    trio_flank_mappings,
    trio_final_switches,
    trio_multiplied_factors,
    trio_final_matrices,
):
    nested_function = FOCUS_NUMBER * PER_FOCUS_WIDTH
    scaling = 1.0 / math.sqrt(PER_FOCUS_WIDTH)
    strand_portion = homolog_stack.shape[0]
    amino_total = homolog_stack.shape[1]
    row_count = couple_tensor.shape[0]
    pair_normed = standardize_features(couple_tensor, couple_offset_factor, -1).astype(jnp.bfloat16)
    bias_local = jnp.einsum(
        "rjc,ch->hrj", pair_normed, couple_offset_matrix, preferred_element_type=jnp.float32
    ).astype(jnp.bfloat16)
    standardized_source = standardize_features(
        homolog_stack, horizontal_standard_factor, -1
    ).astype(jnp.bfloat16)
    shaped = (strand_portion, amino_total, FOCUS_NUMBER, PER_FOCUS_WIDTH)
    queries = (
        (
            jnp.dot(
                standardized_source, horizontal_asking_matrix, preferred_element_type=jnp.float32
            )
            * scaling
        )
        .astype(jnp.bfloat16)
        .reshape(shaped)
    )
    others = jnp.dot(
        standardized_source, horizontal_lookup_triple, preferred_element_type=jnp.float32
    )
    keys_all = others[..., :nested_function].astype(jnp.bfloat16).reshape(shaped)
    content_entire = (
        others[..., nested_function : 2 * nested_function].astype(jnp.bfloat16).reshape(shaped)
    )
    sigmoid_switches = jax.nn.sigmoid(others[..., 2 * nested_function :])
    mask_penalty = MASK_PENALTY_SCALE * (homolog_presence.astype(jnp.float32) - 1.0)

    def attend(bias_piece):
        query_rows = bias_piece.shape[1]
        scores = jnp.einsum(
            "sihc,sjhc->shij", queries, keys_all, preferred_element_type=jnp.float32
        )
        scores = scores + bias_piece.astype(jnp.float32)[None] + mask_penalty[:, None, None, :]
        softmax_probabilities = jax.nn.softmax(scores, axis=-1).astype(jnp.bfloat16)
        mixed = jnp.einsum(
            "shij,sjhc->sihc",
            softmax_probabilities,
            content_entire,
            preferred_element_type=jnp.float32,
        )
        return mixed.reshape(strand_portion, query_rows, nested_function)

    bias_whole = lax.all_gather(bias_local, "dap", axis=1, tiled=True)
    block_rows = math.gcd(amino_total, 256)

    def one_block(block_index):
        return attend(bias_whole)

    blocks = lax.map(one_block, jnp.arange(amino_total // block_rows, dtype=jnp.int32))
    focused_content = jnp.moveaxis(blocks, 0, 1).reshape(
        strand_portion, amino_total, nested_function
    )
    homolog_stack_horizontal = homolog_stack + jnp.dot(
        (focused_content * sigmoid_switches).astype(jnp.bfloat16),
        horizontal_final_matrix,
        preferred_element_type=jnp.float32,
    )
    column_view, col_mask = (
        lax.all_to_all(
            homolog_stack_horizontal.astype(jnp.bfloat16),
            "dap",
            split_axis=1,
            concat_axis=0,
            tiled=True,
        ).astype(homolog_stack_horizontal.dtype),
        lax.all_to_all(
            homolog_presence.astype(jnp.float32).astype(jnp.bfloat16),
            "dap",
            split_axis=1,
            concat_axis=0,
            tiled=True,
        ).astype(jnp.float32),
    )
    seq_total = column_view.shape[0]
    col_shape = (seq_total, row_count, FOCUS_NUMBER, PER_FOCUS_WIDTH)
    standardized_source = standardize_features(column_view, vertical_standard_factor, -1).astype(
        jnp.bfloat16
    )
    col_queries = (
        (
            jnp.dot(standardized_source, vertical_asking_matrix, preferred_element_type=jnp.float32)
            * scaling
        )
        .astype(jnp.bfloat16)
        .reshape(col_shape)
    )
    col_others = jnp.dot(
        standardized_source, vertical_lookup_triple, preferred_element_type=jnp.float32
    )
    col_keys = col_others[..., :nested_function].astype(jnp.bfloat16).reshape(col_shape)
    col_values = (
        col_others[..., nested_function : 2 * nested_function]
        .astype(jnp.bfloat16)
        .reshape(col_shape)
    )
    col_gates = jax.nn.sigmoid(col_others[..., 2 * nested_function :])
    col_penalty = MASK_PENALTY_SCALE * (col_mask - 1.0)
    scores = jnp.einsum(
        "sihc,tihc->ihst", col_queries, col_keys, preferred_element_type=jnp.float32
    )
    scores = scores + jnp.transpose(col_penalty)[:, None, None, :]
    softmax_probabilities = jax.nn.softmax(scores, axis=-1).astype(jnp.bfloat16)
    col_mixed = jnp.einsum(
        "uovg,guox->vuox", softmax_probabilities, col_values, preferred_element_type=jnp.float32
    ).reshape(seq_total, row_count, nested_function)
    alignment_after_columns = column_view + jnp.dot(
        (col_mixed * col_gates).astype(jnp.bfloat16),
        vertical_final_matrix,
        preferred_element_type=jnp.float32,
    )
    standardized_source = standardize_features(
        alignment_after_columns, tensor_average_factor, -1
    ).astype(jnp.bfloat16)
    halves = jnp.dot(
        standardized_source, tensor_average_mapping, preferred_element_type=jnp.float32
    )
    left_proj = (halves[..., :TENSOR_HIDDEN] * col_mask[..., None]).astype(jnp.bfloat16)
    right_proj = (halves[..., TENSOR_HIDDEN:] * col_mask[..., None]).astype(jnp.bfloat16)
    right_whole, mask_whole = (
        lax.all_gather(right_proj, "dap", axis=1, tiled=True),
        lax.all_gather(col_mask.astype(jnp.bfloat16), "dap", axis=1, tiled=True),
    )
    outer = jnp.einsum("sra,sjb->rjab", left_proj, right_whole, preferred_element_type=jnp.float32)
    outer = outer.astype(jnp.bfloat16).reshape(
        row_count, amino_total, TENSOR_HIDDEN * TENSOR_HIDDEN
    )
    counts = jnp.dot(
        jnp.transpose(col_mask), mask_whole.astype(jnp.float32), precision=lax.Precision.HIGHEST
    )
    product = (
        jnp.dot(outer, tensor_average_final, preferred_element_type=jnp.float32)
        / jnp.maximum(counts, 1.0)[..., None]
    )
    pair_one = couple_tensor + product
    pair_two = triangle(
        pair_one,
        trio_entry_factors[0],
        trio_flank_mappings[0],
        trio_final_switches[0],
        trio_multiplied_factors[0],
        trio_final_matrices[0],
        amino_presence,
        False,
    )
    pair_after_incoming = triangle(
        pair_two,
        trio_entry_factors[1],
        trio_flank_mappings[1],
        trio_final_switches[1],
        trio_multiplied_factors[1],
        trio_final_matrices[1],
        amino_presence,
        True,
    )
    return (alignment_after_columns, pair_after_incoming)


def solution(mesh):
    placed = (
        P("dap", None, None),
        P("dap", None, None),
        P("dap", None),
        P(),
        P(),
        P(),
        P(),
        P(),
        P(),
        P(),
        P(),
        P(),
        P(),
        P(),
        P(),
        P(),
        P(),
        P(),
        P(),
        P(),
        P(),
        P(),
    )
    return jax.shard_map(
        shards,
        mesh=mesh,
        in_specs=placed,
        out_specs=(P(None, "dap", None), P("dap", None, None)),
        check_vma=False,
    )
```

profile of v0, /device:TPU:0, one launch (start us, length us, event | category | flops | bytes accessed | tf_op | source)
XLA Modules:
  0.0 221.2 jit_solution(10079408757036569126)
XLA Ops:
  0.7 0.8 convert_convert_fusion
  1.5 0.6 copy.137
  2.2 7.3 %all-to-all-start.1 = ((bf16[2,32,2]{2,0,1:T(2,128)(2,1)}), bf16[2,32,2]{2,0,1:T(2,128)(2,1)S(1)}, u32[]{:S(2)}, u32[]{:S(2)}) async-start(bf16[2,32,2]{2,0,1:T(2,128)(2,1)} %copy.137), calls=%async_computation.1 | async-start | bytes 32768 | tf_op jit(solution)/shard_map/all_to_all | solution.py:166
  9.5 0.7 add_multiply_fusion
  10.2 1.0 reduce_sum.163
  11.4 0.7 copy-done.10
  12.5 0.8 copy-done.6
  13.6 0.7 copy-done.2
  14.6 0.5 copy-done.18
  15.5 42.1 %all_gather.9 = bf16[8,64,64]{2,0,1:T(8,128)(2,1)S(1)} all-gather(bf16[8,2,64]{2,0,1:T(8,128)(2,1)S(1)} %fusion.22), channel_id=1, replica_groups=mesh['dap'=32] {'dap'}, dimensions={1}, use_global_device_ids=true | all-gather | bytes 67584 | tf_op jit(solution)/shard_map/all_gather | solution.py:143
  58.0 0.4 fusion.118
  58.9 0.5 copy-done.13
  59.5 0.7 copy-done.20
  60.5 0.7 copy.126
  61.2 2.6 %all-to-all-start = ((bf16[2,64,256]{2,0,1:T(2,128)(2,1)}), bf16[2,64,256]{2,0,1:T(2,128)(2,1)S(1)}, u32[]{:S(2)}, u32[]{:S(2)}) async-start(bf16[2,64,256]{2,0,1:T(2,128)(2,1)} %copy.126), calls=%async_computation | async-start | bytes 131072 | tf_op jit(solution)/shard_map/all_to_all | solution.py:159
  63.8 41.8 %all-gather = bf16[32,2,64]{2,1,0:T(2,128)(2,1)S(1)} all-gather(bf16[1,2,64]{2,1,0:T(2,128)(2,1)S(1)} %bitcast.220), channel_id=1, replica_groups=mesh['dap'=32] {'dap'}, dimensions={0}, use_global_device_ids=true | all-gather | bytes 8448 | tf_op jit(solution)/shard_map/all_gather | solution.py:221
  107.3 0.6 copy-done.11
  108.3 0.8 copy-done.7
  109.7 0.4 fusion.120
  110.6 0.8 copy-done.16
  111.9 0.6 copy-done.9
  112.8 38.1 %all_gather.10 = bf16[64,64,32]{0,2,1:T(8,128)(2,1)S(1)} all-gather(bf16[64,2,32]{0,2,1:T(8,128)(2,1)S(1)} %fusion.80), channel_id=1, replica_groups=mesh['dap'=32] {'dap'}, dimensions={1}, use_global_device_ids=true | all-gather | bytes 270336 | tf_op jit(solution)/shard_map/all_gather | solution.py:220
  150.9 0.6 fusion.6
  151.9 0.6 copy-done.4
  152.5 0.4 fusion.122
  153.0 0.4 copy-done.5
  153.9 0.7 reshape.256
  154.6 2.6 %all-to-all-start.2 = ((bf16[32,2,256]{2,1,0:T(2,128)(2,1)}), bf16[32,2,256]{2,1,0:T(2,128)(2,1)S(1)}, u32[]{:S(2)}, u32[]{:S(2)}) async-start(bf16[32,2,256]{2,1,0:T(2,128)(2,1)} %reshape.256), calls=%async_computation.2 | async-start | bytes 65536 | tf_op jit(solution)/shard_map/all_to_all | solution.py:49
  157.3 0.7 reshape.258
  158.0 6.4 %all-to-all-done.2 = bf16[32,2,256]{2,1,0:T(2,128)(2,1)S(1)} async-done(((bf16[32,2,256]{2,1,0:T(2,128)(2,1)}), bf16[32,2,256]{2,1,0:T(2,128)(2,1)S(1)}, u32[]{:S(2)}, u32[]{:S(2)}) %all-to-all-start.2) | async-done | bytes 32800 | tf_op jit(solution)/shard_map/all_to_all | solution.py:49
  164.4 2.6 %all-to-all-start.3 = ((bf16[32,2,256]{2,1,0:T(2,128)(2,1)}), bf16[32,2,256]{2,1,0:T(2,128)(2,1)S(1)}, u32[]{:S(2)}, u32[]{:S(2)}) async-start(bf16[32,2,256]{2,1,0:T(2,128)(2,1)} %reshape.258), calls=%async_computation.3 | async-start | bytes 65536 | tf_op jit(solution)/shard_map/all_to_all | solution.py:50
  167.2 7.0 %all-to-all-done.3 = bf16[32,2,256]{2,1,0:T(2,128)(2,1)S(1)} async-done(((bf16[32,2,256]{2,1,0:T(2,128)(2,1)}), bf16[32,2,256]{2,1,0:T(2,128)(2,1)S(1)}, u32[]{:S(2)}, u32[]{:S(2)}) %all-to-all-start.3) | async-done | bytes 32800 | tf_op jit(solution)/shard_map/all_to_all | solution.py:50
  174.7 0.7 reshape.260
  175.4 2.7 %all-to-all-start.4 = ((bf16[32,2,256]{2,1,0:T(2,128)(2,1)}), bf16[32,2,256]{2,1,0:T(2,128)(2,1)S(1)}, u32[]{:S(2)}, u32[]{:S(2)}) async-start(bf16[32,2,256]{2,1,0:T(2,128)(2,1)} %reshape.260), calls=%async_computation.4 | async-start | bytes 65536 | tf_op jit(solution)/shard_map/all_to_all | solution.py:61
  178.2 7.1 %all-to-all-done.4 = bf16[32,2,256]{2,1,0:T(2,128)(2,1)S(1)} async-done(((bf16[32,2,256]{2,1,0:T(2,128)(2,1)}), bf16[32,2,256]{2,1,0:T(2,128)(2,1)S(1)}, u32[]{:S(2)}, u32[]{:S(2)}) %all-to-all-start.4) | async-done | bytes 32800 | tf_op jit(solution)/shard_map/all_to_all | solution.py:61
  185.8 0.7 copy-done.8
  186.7 0.7 copy-done.17
  188.3 0.7 reshape.262
  189.0 2.6 %all-to-all-start.5 = ((bf16[32,2,256]{2,1,0:T(2,128)(2,1)}), bf16[32,2,256]{2,1,0:T(2,128)(2,1)S(1)}, u32[]{:S(2)}, u32[]{:S(2)}) async-start(bf16[32,2,256]{2,1,0:T(2,128)(2,1)} %reshape.262), calls=%async_computation.5 | async-start | bytes 65536 | tf_op jit(solution)/shard_map/all_to_all | solution.py:49
  191.7 0.7 reshape.264
  192.5 6.4 %all-to-all-done.5 = bf16[32,2,256]{2,1,0:T(2,128)(2,1)S(1)} async-done(((bf16[32,2,256]{2,1,0:T(2,128)(2,1)}), bf16[32,2,256]{2,1,0:T(2,128)(2,1)S(1)}, u32[]{:S(2)}, u32[]{:S(2)}) %all-to-all-start.5) | async-done | bytes 32800 | tf_op jit(solution)/shard_map/all_to_all | solution.py:49
  198.9 2.6 %all-to-all-start.6 = ((bf16[32,2,256]{2,1,0:T(2,128)(2,1)}), bf16[32,2,256]{2,1,0:T(2,128)(2,1)S(1)}, u32[]{:S(2)}, u32[]{:S(2)}) async-start(bf16[32,2,256]{2,1,0:T(2,128)(2,1)} %reshape.264), calls=%async_computation.6 | async-start | bytes 65536 | tf_op jit(solution)/shard_map/all_to_all | solution.py:50
  201.6 7.0 %all-to-all-done.6 = bf16[32,2,256]{2,1,0:T(2,128)(2,1)S(1)} async-done(((bf16[32,2,256]{2,1,0:T(2,128)(2,1)}), bf16[32,2,256]{2,1,0:T(2,128)(2,1)S(1)}, u32[]{:S(2)}, u32[]{:S(2)}) %all-to-all-start.6) | async-done | bytes 32800 | tf_op jit(solution)/shard_map/all_to_all | solution.py:50
  209.2 0.7 reshape.266
  209.9 2.6 %all-to-all-start.7 = ((bf16[32,2,256]{2,1,0:T(2,128)(2,1)}), bf16[32,2,256]{2,1,0:T(2,128)(2,1)S(1)}, u32[]{:S(2)}, u32[]{:S(2)}) async-start(bf16[32,2,256]{2,1,0:T(2,128)(2,1)} %reshape.266), calls=%async_computation.7 | async-start | bytes 65536 | tf_op jit(solution)/shard_map/all_to_all | solution.py:61
  212.6 0.8 copy.163
  213.3 6.4 %all-to-all-done.7 = bf16[32,2,256]{2,1,0:T(2,128)(2,1)S(1)} async-done(((bf16[32,2,256]{2,1,0:T(2,128)(2,1)}), bf16[32,2,256]{2,1,0:T(2,128)(2,1)S(1)}, u32[]{:S(2)}, u32[]{:S(2)}) %all-to-all-start.7) | async-done | bytes 32800 | tf_op jit(solution)/shard_map/all_to_all | solution.py:61
  220.3 0.9 fusion.15
  (135 shorter events, 11.6 us)
Async XLA Ops:
  0.6 10.8 %copy-start = (bf16[256,768]{1,0:T(8,128)(2,1)S(1)}, bf16[256,768]{1,0:T(8,128)(2,1)}, u32[]{:S(2)}) copy-start(bf16[256,768]{1,0:T(8,128)(2,1)} %param.28) | copy-start | bytes 1179652
  0.6 10.5 %copy-start.1 = (f32[2,64,256]{2,1,0:T(8,128)S(1)}, f32[2,64,256]{2,1,0:T(8,128)}, u32[]{:S(2)}) copy-start(f32[2,64,256]{2,1,0:T(8,128)} %param.22) | copy-start | bytes 393220
  2.2 59.0 %all-to-all-start.1 = ((bf16[2,32,2]{2,0,1:T(2,128)(2,1)}), bf16[2,32,2]{2,0,1:T(2,128)(2,1)S(1)}, u32[]{:S(2)}, u32[]{:S(2)}) async-start(bf16[2,32,2]{2,0,1:T(2,128)(2,1)} %copy.137), calls=%async_computation.1 | async-start | bytes 32768 | tf_op jit(solution)/shard_map/all_to_all | solution.py:166
  11.4 0.7 copy-start.10
  12.3 0.9 copy-start.6
  13.5 0.8 copy-start.2
  14.4 0.7 copy-start.18
  14.6 0.7 copy-start.19
  58.8 0.7 copy-start.13
  58.8 1.4 copy-start.15
  59.5 0.7 copy-start.20
  61.2 44.6 %all-to-all-start = ((bf16[2,64,256]{2,0,1:T(2,128)(2,1)}), bf16[2,64,256]{2,0,1:T(2,128)(2,1)S(1)}, u32[]{:S(2)}, u32[]{:S(2)}) async-start(bf16[2,64,256]{2,0,1:T(2,128)(2,1)} %copy.126), calls=%async_computation | async-start | bytes 131072 | tf_op jit(solution)/shard_map/all_to_all | solution.py:159
  106.3 1.0 copy-start.3
  107.2 0.7 copy-start.11
  108.2 0.9 copy-start.7
  110.5 0.9 copy-start.16
  111.7 0.8 copy-start.9
  111.9 0.7 copy-start.12
  151.5 1.0 copy-start.4
  152.5 0.9 copy-start.5
  154.6 9.8 %all-to-all-start.2 = ((bf16[32,2,256]{2,1,0:T(2,128)(2,1)}), bf16[32,2,256]{2,1,0:T(2,128)(2,1)S(1)}, u32[]{:S(2)}, u32[]{:S(2)}) async-start(bf16[32,2,256]{2,1,0:T(2,128)(2,1)} %reshape.256), calls=%async_computation.2 | async-start | bytes 65536 | tf_op jit(solution)/shard_map/all_to_all | solution.py:49
  164.4 9.8 %all-to-all-start.3 = ((bf16[32,2,256]{2,1,0:T(2,128)(2,1)}), bf16[32,2,256]{2,1,0:T(2,128)(2,1)S(1)}, u32[]{:S(2)}, u32[]{:S(2)}) async-start(bf16[32,2,256]{2,1,0:T(2,128)(2,1)} %reshape.258), calls=%async_computation.3 | async-start | bytes 65536 | tf_op jit(solution)/shard_map/all_to_all | solution.py:50
  175.4 2.7 %copy-start.14 = (f32[2,128]{1,0:T(2,128)S(1)}, f32[2,128]{1,0:T(2,128)}, u32[]{:S(2)}) copy-start(f32[2,128]{1,0:T(2,128)} %param.42) | copy-start | bytes 3076
  175.4 10.0 %all-to-all-start.4 = ((bf16[32,2,256]{2,1,0:T(2,128)(2,1)}), bf16[32,2,256]{2,1,0:T(2,128)(2,1)S(1)}, u32[]{:S(2)}, u32[]{:S(2)}) async-start(bf16[32,2,256]{2,1,0:T(2,128)(2,1)} %reshape.260), calls=%async_computation.4 | async-start | bytes 65536 | tf_op jit(solution)/shard_map/all_to_all | solution.py:61
  185.6 0.8 copy-start.8
  186.5 0.8 copy-start.17
  189.0 9.8 %all-to-all-start.5 = ((bf16[32,2,256]{2,1,0:T(2,128)(2,1)}), bf16[32,2,256]{2,1,0:T(2,128)(2,1)S(1)}, u32[]{:S(2)}, u32[]{:S(2)}) async-start(bf16[32,2,256]{2,1,0:T(2,128)(2,1)} %reshape.262), calls=%async_computation.5 | async-start | bytes 65536 | tf_op jit(solution)/shard_map/all_to_all | solution.py:49
  198.9 9.8 %all-to-all-start.6 = ((bf16[32,2,256]{2,1,0:T(2,128)(2,1)}), bf16[32,2,256]{2,1,0:T(2,128)(2,1)S(1)}, u32[]{:S(2)}, u32[]{:S(2)}) async-start(bf16[32,2,256]{2,1,0:T(2,128)(2,1)} %reshape.264), calls=%async_computation.6 | async-start | bytes 65536 | tf_op jit(solution)/shard_map/all_to_all | solution.py:50
  209.9 9.8 %all-to-all-start.7 = ((bf16[32,2,256]{2,1,0:T(2,128)(2,1)}), bf16[32,2,256]{2,1,0:T(2,128)(2,1)S(1)}, u32[]{:S(2)}, u32[]{:S(2)}) async-start(bf16[32,2,256]{2,1,0:T(2,128)(2,1)} %reshape.266), calls=%async_computation.7 | async-start | bytes 65536 | tf_op jit(solution)/shard_map/all_to_all | solution.py:61
where the time goes:
time: 222 us; the launch traced here: 221 us
  blocking collectives  122 us (55%)
  waiting for transfers between devices  40.4 us (18%)
  starting transfers between devices  25.4 us (11%)
  local copies, waits for them, and re-layouts  20.1 us (9%)
  matrix products  7.19 us (3%)
  other arithmetic  4.68 us (2%)
    all_gather x1, blocking collectives, shards(): bias_whole = lax.all_gather(bias_local, 'dap', axis=1, tiled=True)  42.1 us
    all_gather x1, blocking collectives, shards(): lax.all_gather(col_mask.astype(jnp.bfloat16), 'dap', axis=1, tiled=True)  41.8 us
    all_gather x1, blocking collectives, shards(): lax.all_gather(right_proj, 'dap', axis=1, tiled=True)  38.1 us
    unnamed x55, local copies, waits for them, and re-layouts  15 us
    all_to_all x2, waiting for transfers between devices, triangle(): lax.all_to_all(right_side, 'dap', split_axis=0, concat_axis=1, tiled=True)  14.1 us
    all_to_all x2, waiting for transfers between devices, triangle(): lax.all_to_all(product, 'dap', split_axis=1, concat_axis=0, tiled=True)  13.5 us
    all_to_all x2, waiting for transfers between devices, triangle(): lax.all_to_all(left_side, 'dap', split_axis=0, concat_axis=1, tiled=True)  12.8 us
    all_to_all x1, starting transfers between devices, shards(): lax.all_to_all(homolog_presence.astype(jnp.float32).astype(jnp.bfloat16),...  7.33 us
  transfers between devices with their start and end apart: 8, of which 6 were waited for; matrix products, arithmetic and copies ran while one was open for 4% of the time, Pallas kernels for 0%

commit v1 on v0

--- a/solution.py
+++ b/solution.py
@@ -19,6 +19,12 @@
     centred = content_vectors - jnp.mean(content_vectors, axis=axis, keepdims=True)
     spread = jnp.mean(centred * centred, axis=axis, keepdims=True)
     return centred * lax.rsqrt(spread + EPSILON) * gain
+
+
+def gather_blocks(block):
+    device_count = lax.axis_size("dap")
+    copies = jnp.broadcast_to(block[None], (device_count,) + block.shape)
+    return lax.all_to_all(copies, "dap", split_axis=0, concat_axis=0, tiled=True)
 
 
 def triangle(
@@ -45,10 +51,18 @@
     gating = jax.nn.sigmoid(
         jnp.dot(standardized_source, gate_weight, preferred_element_type=jnp.float32)
     )
-    left_chan, right_chan = (
-        lax.all_to_all(left_side, "dap", split_axis=0, concat_axis=1, tiled=True),
-        lax.all_to_all(right_side, "dap", split_axis=0, concat_axis=1, tiled=True),
-    )
+    device_count = lax.axis_size("dap")
+    per_device = hidden // device_count
+    both = jnp.stack(
+        [
+            left_side.reshape(device_count, per_device, row_count, -1),
+            right_side.reshape(device_count, per_device, row_count, -1),
+        ],
+        axis=1,
+    )
+    both = lax.all_to_all(both, "dap", split_axis=0, concat_axis=0, tiled=True)
+    both = jnp.moveaxis(both, 0, 2).reshape(2, per_device, device_count * row_count, -1)
+    left_chan, right_chan = both[0], both[1]
     if incoming:
         product = jnp.einsum(
             "cki,ckj->cij", left_chan, right_chan, preferred_element_type=jnp.float32
@@ -140,7 +154,9 @@
         )
         return mixed.reshape(strand_portion, query_rows, nested_function)
 
-    bias_whole = lax.all_gather(bias_local, "dap", axis=1, tiled=True)
+    bias_whole = jnp.moveaxis(gather_blocks(bias_local), 0, 1).reshape(
+        FOCUS_NUMBER, amino_total, amino_total
+    )
     block_rows = math.gcd(amino_total, 256)
 
     def one_block(block_index):
@@ -155,22 +171,19 @@
         horizontal_final_matrix,
         preferred_element_type=jnp.float32,
     )
-    column_view, col_mask = (
-        lax.all_to_all(
+    travelling = jnp.concatenate(
+        [
             homolog_stack_horizontal.astype(jnp.bfloat16),
-            "dap",
-            split_axis=1,
-            concat_axis=0,
-            tiled=True,
-        ).astype(homolog_stack_horizontal.dtype),
-        lax.all_to_all(
-            homolog_presence.astype(jnp.float32).astype(jnp.bfloat16),
-            "dap",
-            split_axis=1,
-            concat_axis=0,
-            tiled=True,
-        ).astype(jnp.float32),
-    )
+            jnp.broadcast_to(
+                homolog_presence.astype(jnp.bfloat16)[..., None],
+                (strand_portion, amino_total, 128),
+            ),
+        ],
+        axis=-1,
+    )
+    arrived = lax.all_to_all(travelling, "dap", split_axis=1, concat_axis=0, tiled=True)
+    column_view = arrived[..., :nested_function].astype(jnp.float32)
+    col_mask = arrived[..., nested_function].astype(jnp.float32)
     seq_total = column_view.shape[0]
     col_shape = (seq_total, row_count, FOCUS_NUMBER, PER_FOCUS_WIDTH)
     standardized_source = standardize_features(column_view, vertical_standard_factor, -1).astype(
@@ -216,10 +229,13 @@
     )
     left_proj = (halves[..., :TENSOR_HIDDEN] * col_mask[..., None]).astype(jnp.bfloat16)
     right_proj = (halves[..., TENSOR_HIDDEN:] * col_mask[..., None]).astype(jnp.bfloat16)
-    right_whole, mask_whole = (
-        lax.all_gather(right_proj, "dap", axis=1, tiled=True),
-        lax.all_gather(col_mask.astype(jnp.bfloat16), "dap", axis=1, tiled=True),
-    )
+    block = jnp.concatenate(
+        [right_proj, col_mask.astype(jnp.bfloat16)[..., None]], axis=-1
+    )
+    block = jnp.transpose(block, (1, 2, 0))
+    whole = gather_blocks(block).reshape(amino_total, TENSOR_HIDDEN + 1, seq_total)
+    right_whole = jnp.transpose(whole[:, :TENSOR_HIDDEN], (2, 0, 1))
+    mask_whole = jnp.transpose(whole[:, TENSOR_HIDDEN])
     outer = jnp.einsum("sra,sjb->rjab", left_proj, right_whole, preferred_element_type=jnp.float32)
     outer = outer.astype(jnp.bfloat16).reshape(
         row_count, amino_total, TENSOR_HIDDEN * TENSOR_HIDDEN

time: 222 us -> 101 us (0.45)
  blocking collectives: 122 us -> 28 us
  waiting for transfers between devices: 40.4 us -> 28.6 us
  starting transfers between devices: 25.4 us -> 15.2 us
  local copies, waits for them, and re-layouts: 20.1 us -> 17.5 us
    all_gather x3 -> x0, blocking collectives: 122 us -> none  [the longest x1 42.1 us: shards(): bias_whole = lax.all_gather(bias_local, 'dap', axis=1, tiled=True)]
    all_to_all x0 -> x3, blocking collectives: none -> 28 us  [the longest x2 18.5 us: triangle(): both = lax.all_to_all(both, 'dap', split_axis=0, concat_axis=0, tiled=True)]
    all_to_all x6 -> x2, waiting for transfers between devices: 26.9 us -> 15.1 us  [gather_blocks(): lax.all_to_all(copies, 'dap', split_axis=0, concat_axis=0, tiled=True)]
    all_to_all x6 -> x2, starting transfers between devices: 20.2 us -> 9.91 us  [gather_blocks(): lax.all_to_all(copies, 'dap', split_axis=0, concat_axis=0, tiled=True)]
    unnamed x55 -> x60, local copies, waits for them, and re-layouts: 15 us -> 13.7 us
  transfers between devices with their start and end apart: 8 -> 4, of which waited for: 6 -> 4; matrix products, arithmetic and copies ran while one was open for 4% -> 2% of each run, Pallas kernels for 0% -> 0%
where the time goes in v1:
time: 101 us
  waiting for transfers between devices  28.6 us (28%)
  blocking collectives  28 us (28%)
  local copies, waits for them, and re-layouts  17.5 us (17%)
  starting transfers between devices  15.2 us (15%)
  matrix products  6.79 us (7%)
  other arithmetic  3.24 us (3%)
  between operations  1.46 us (1%)
    all_to_all x2, blocking collectives, triangle(): both = lax.all_to_all(both, 'dap', split_axis=0, concat_axis=0, tiled=True)  18.5 us
    all_to_all x2, waiting for transfers between devices, gather_blocks(): lax.all_to_all(copies, 'dap', split_axis=0, concat_axis=0, tiled=True)  15.1 us
    unnamed x60, local copies, waits for them, and re-layouts  13.7 us
    all_to_all x2, waiting for transfers between devices, triangle(): lax.all_to_all(product, 'dap', split_axis=1, concat_axis=0, tiled=True)  13.5 us
    all_to_all x2, starting transfers between devices, gather_blocks(): lax.all_to_all(copies, 'dap', split_axis=0, concat_axis=0, tiled=True)  9.91 us
    all_to_all x1, blocking collectives, shards(): lax.all_to_all(travelling, 'dap', split_axis=1, concat_axis=0, tiled=True)  9.48 us
    all_to_all x2, starting transfers between devices, triangle(): lax.all_to_all(product, 'dap', split_axis=1, concat_axis=0, tiled=True)  5.27 us
  transfers between devices with their start and end apart: 4, of which 4 were waited for; matrix products, arithmetic and copies ran while one was open for 2% of the time, Pallas kernels for 0%

profile of v1, /device:TPU:0, one launch (start us, length us, event | category | flops | bytes accessed | tf_op | source)
XLA Modules:
  0.0 100.7 jit_solution(9206909129855813122)
XLA Ops:
  0.7 1.0 reduce_sum.165
  1.9 0.5 copy-done.20
  2.8 0.8 reshape.247
  3.6 7.3 %all-to-all-start = ((bf16[32,2,512]{2,1,0:T(2,128)(2,1)}), bf16[32,2,512]{2,1,0:T(2,128)(2,1)S(1)}, u32[]{:S(2)}, u32[]{:S(2)}) async-start(bf16[32,2,512]{2,1,0:T(2,128)(2,1)} %reshape.247), calls=%async_computation | async-start | bytes 131072 | tf_op jit(solution)/shard_map/all_to_all | solution.py:27
  11.3 0.6 copy-done.6
  12.3 0.3 fusion.126
  12.9 5.5 %all-to-all-done = bf16[32,2,512]{2,1,0:T(2,128)(2,1)S(1)} async-done(((bf16[32,2,512]{2,1,0:T(2,128)(2,1)}), bf16[32,2,512]{2,1,0:T(2,128)(2,1)S(1)}, u32[]{:S(2)}, u32[]{:S(2)}) %all-to-all-start) | async-done | bytes 65568 | tf_op jit(solution)/shard_map/all_to_all | solution.py:27
  18.7 0.4 fusion.127
  19.1 0.3 fusion.7
  19.3 0.2 fusion.29
  19.7 0.8 copy-done.15
  20.9 9.5 %all_to_all.56 = bf16[2,64,384]{2,0,1:T(2,128)(2,1)S(1)} all-to-all(bf16[2,64,384]{2,0,1:T(2,128)(2,1)S(1)} %copy.84), channel_id=1, replica_groups=mesh['dap'=32] {'dap'}, dimensions={1} | all-to-all | bytes 196608 | tf_op jit(solution)/shard_map/all_to_all | solution.py:184
  31.1 0.2 copy-done.16
  31.7 0.3 fusion.128
  32.2 0.4 fusion.129
  32.5 0.3 convolution_add_fusion
  33.1 0.2 fusion.30
  33.4 0.8 copy-done.17
  34.2 0.3 fusion.130
  34.7 0.6 copy-done.8
  35.6 0.3 broadcast_bitcast_fusion
  35.9 1.1 %reshape.249 = bf16[32,2,2112]{2,1,0:T(2,128)(2,1)} reshape(bf16[32,33,2,64]{3,2,1,0:T(2,128)(2,1)S(1)} %broadcast_bitcast_fusion) | data formatting | bytes 540672
  37.1 2.6 %all-to-all-start.2 = ((bf16[32,2,2112]{2,1,0:T(2,128)(2,1)}), bf16[32,2,2112]{2,1,0:T(2,128)(2,1)S(1)}, u32[]{:S(2)}, u32[]{:S(2)}) async-start(bf16[32,2,2112]{2,1,0:T(2,128)(2,1)} %reshape.249), calls=%async_computation.2 | async-start | bytes 557056 | tf_op jit(solution)/shard_map/all_to_all | solution.py:27
  39.7 0.6 copy-done.21
  40.5 0.6 copy-done.13
  41.1 9.6 %all-to-all-done.2 = bf16[32,2,2112]{2,1,0:T(2,128)(2,1)S(1)} async-done(((bf16[32,2,2112]{2,1,0:T(2,128)(2,1)}), bf16[32,2,2112]{2,1,0:T(2,128)(2,1)S(1)}, u32[]{:S(2)}, u32[]{:S(2)}) %all-to-all-start.2) | async-done | bytes 270368 | tf_op jit(solution)/shard_map/all_to_all | solution.py:27
  50.7 0.4 reshape.250
  51.1 0.6 copy.93
  51.9 0.3 copy.125
  52.1 0.3 fusion.6
  52.4 0.3 copy.95
  52.8 0.6 copy-done.4
  53.4 0.4 fusion.131
  54.0 0.4 copy-done.5
  55.1 9.4 %all_to_all.57 = bf16[32,2,512]{2,1,0:T(2,128)(2,1)S(1)} all-to-all(bf16[32,2,512]{2,1,0:T(2,128)(2,1)S(1)} %reshape.251), channel_id=1, replica_groups=mesh['dap'=32] {'dap'}, dimensions={0} | all-to-all | bytes 131072 | tf_op jit(solution)/shard_map/all_to_all | solution.py:63
  65.1 0.7 reshape.253
  65.8 2.7 %all-to-all-start.4 = ((bf16[32,2,256]{2,1,0:T(2,128)(2,1)}), bf16[32,2,256]{2,1,0:T(2,128)(2,1)S(1)}, u32[]{:S(2)}, u32[]{:S(2)}) async-start(bf16[32,2,256]{2,1,0:T(2,128)(2,1)} %reshape.253), calls=%async_computation.4 | async-start | bytes 65536 | tf_op jit(solution)/shard_map/all_to_all | solution.py:75
  68.7 7.1 %all-to-all-done.4 = bf16[32,2,256]{2,1,0:T(2,128)(2,1)S(1)} async-done(((bf16[32,2,256]{2,1,0:T(2,128)(2,1)}), bf16[32,2,256]{2,1,0:T(2,128)(2,1)S(1)}, u32[]{:S(2)}, u32[]{:S(2)}) %all-to-all-start.4) | async-done | bytes 32800 | tf_op jit(solution)/shard_map/all_to_all | solution.py:75
  76.2 0.7 copy-done.7
  77.1 0.7 copy-done.18
  77.7 0.3 fusion.132
  78.3 0.2 convolution_bitcast_fusion
  79.1 9.1 %all_to_all.58 = bf16[32,2,512]{2,1,0:T(2,128)(2,1)S(1)} all-to-all(bf16[32,2,512]{2,1,0:T(2,128)(2,1)S(1)} %reshape.255), channel_id=1, replica_groups=mesh['dap'=32] {'dap'}, dimensions={0} | all-to-all | bytes 131072 | tf_op jit(solution)/shard_map/all_to_all | solution.py:63
  88.8 0.7 reshape.257
  89.5 2.6 %all-to-all-start.6 = ((bf16[32,2,256]{2,1,0:T(2,128)(2,1)}), bf16[32,2,256]{2,1,0:T(2,128)(2,1)S(1)}, u32[]{:S(2)}, u32[]{:S(2)}) async-start(bf16[32,2,256]{2,1,0:T(2,128)(2,1)} %reshape.257), calls=%async_computation.6 | async-start | bytes 65536 | tf_op jit(solution)/shard_map/all_to_all | solution.py:75
  92.2 0.8 copy.114
  92.9 6.4 %all-to-all-done.6 = bf16[32,2,256]{2,1,0:T(2,128)(2,1)S(1)} async-done(((bf16[32,2,256]{2,1,0:T(2,128)(2,1)}), bf16[32,2,256]{2,1,0:T(2,128)(2,1)S(1)}, u32[]{:S(2)}, u32[]{:S(2)}) %all-to-all-start.6) | async-done | bytes 32800 | tf_op jit(solution)/shard_map/all_to_all | solution.py:75
  99.9 0.9 fusion.15
  (134 shorter events, 8.9 us)
Async XLA Ops:
  0.6 11.7 %copy-start = (bf16[256,768]{1,0:T(8,128)(2,1)S(1)}, bf16[256,768]{1,0:T(8,128)(2,1)}, u32[]{:S(2)}) copy-start(bf16[256,768]{1,0:T(8,128)(2,1)} %param.28) | copy-start | bytes 1179652
  0.6 1.0 %copy-start.2 = (f32[2,64,128]{2,1,0:T(8,128)S(1)}, f32[2,64,128]{2,1,0:T(8,128)}, u32[]{:S(2)}) copy-start(f32[2,64,128]{2,1,0:T(8,128)} %param.23) | copy-start | bytes 196612
  1.7 0.7 copy-start.20
  1.9 0.7 copy-start.19
  2.8 8.1 %copy-start.1 = (f32[2,64,256]{2,1,0:T(8,128)S(1)}, f32[2,64,256]{2,1,0:T(8,128)}, u32[]{:S(2)}) copy-start(f32[2,64,256]{2,1,0:T(8,128)} %param.22) | copy-start | bytes 393220
  3.6 7.3 %copy-start.12 = (s32[2,64]{1,0:T(2,128)S(1)}, s32[2,64]{1,0:T(2,128)}, u32[]{:S(2)}) copy-start(s32[2,64]{1,0:T(2,128)} %param.24) | copy-start | bytes 1540
  3.6 14.7 %all-to-all-start = ((bf16[32,2,512]{2,1,0:T(2,128)(2,1)}), bf16[32,2,512]{2,1,0:T(2,128)(2,1)S(1)}, u32[]{:S(2)}, u32[]{:S(2)}) async-start(bf16[32,2,512]{2,1,0:T(2,128)(2,1)} %reshape.247), calls=%async_computation | async-start | bytes 131072 | tf_op jit(solution)/shard_map/all_to_all | solution.py:27
  11.0 0.9 copy-start.6
  11.2 0.7 copy-start.9
  19.6 0.9 copy-start.15
  30.5 0.7 copy-start.10
  30.5 0.9 copy-start.16
  30.5 1.2 %copy-start.3 = (bf16[256,768]{1,0:T(8,128)(2,1)S(1)}, bf16[256,768]{1,0:T(8,128)(2,1)}, u32[]{:S(2)}) copy-start(bf16[256,768]{1,0:T(8,128)(2,1)} %param.34) | copy-start | bytes 1179652
  33.3 0.9 copy-start.17
  34.5 0.8 copy-start.8
  34.7 0.7 copy-start.11
  37.1 13.7 %all-to-all-start.2 = ((bf16[32,2,2112]{2,1,0:T(2,128)(2,1)}), bf16[32,2,2112]{2,1,0:T(2,128)(2,1)S(1)}, u32[]{:S(2)}, u32[]{:S(2)}) async-start(bf16[32,2,2112]{2,1,0:T(2,128)(2,1)} %reshape.249), calls=%async_computation.2 | async-start | bytes 557056 | tf_op jit(solution)/shard_map/all_to_all | solution.py:27
  39.6 0.7 copy-start.21
  40.4 0.7 copy-start.13
  52.4 1.0 copy-start.4
  53.4 0.9 copy-start.5
  65.8 2.7 %copy-start.14 = (f32[2,128]{1,0:T(2,128)S(1)}, f32[2,128]{1,0:T(2,128)}, u32[]{:S(2)}) copy-start(f32[2,128]{1,0:T(2,128)} %param.42) | copy-start | bytes 3076
  65.8 10.0 %all-to-all-start.4 = ((bf16[32,2,256]{2,1,0:T(2,128)(2,1)}), bf16[32,2,256]{2,1,0:T(2,128)(2,1)S(1)}, u32[]{:S(2)}, u32[]{:S(2)}) async-start(bf16[32,2,256]{2,1,0:T(2,128)(2,1)} %reshape.253), calls=%async_computation.4 | async-start | bytes 65536 | tf_op jit(solution)/shard_map/all_to_all | solution.py:75
  76.1 0.8 copy-start.7
  76.9 0.8 copy-start.18
  89.5 9.8 %all-to-all-start.6 = ((bf16[32,2,256]{2,1,0:T(2,128)(2,1)}), bf16[32,2,256]{2,1,0:T(2,128)(2,1)S(1)}, u32[]{:S(2)}, u32[]{:S(2)}) async-start(bf16[32,2,256]{2,1,0:T(2,128)(2,1)} %reshape.257), calls=%async_computation.6 | async-start | bytes 65536 | tf_op jit(solution)/shard_map/all_to_all | solution.py:75

commit v2 on v1

--- a/solution.py
+++ b/solution.py
@@ -3,6 +3,8 @@
 import jax
 import jax.numpy as jnp
 from jax import lax
+from jax.experimental import pallas as pl
+from jax.experimental.pallas import tpu as pltpu
 from jax.sharding import PartitionSpec as P
 
 FOCUS_NUMBER = 8
@@ -271,6 +273,621 @@
     return (alignment_after_columns, pair_after_incoming)
 
 
+def normed_rows(x, gain):
+    centred = x - jnp.mean(x, axis=-1, keepdims=True)
+    spread = jnp.mean(centred * centred, axis=-1, keepdims=True)
+    return centred * lax.rsqrt(spread + EPSILON) * gain
+
+
+def dot_nn(a, b):
+    return lax.dot_general(a, b, (((1,), (0,)), ((), ())), preferred_element_type=jnp.float32)
+
+
+def dot_nt(a, b):
+    return lax.dot_general(a, b, (((1,), (1,)), ((), ())), preferred_element_type=jnp.float32)
+
+
+def dot_tn(a, b):
+    return lax.dot_general(a, b, (((0,), (0,)), ((), ())), preferred_element_type=jnp.float32)
+
+
+def lane_iota(shape):
+    return lax.broadcasted_iota(jnp.int32, shape, len(shape) - 1)
+
+
+def vmem_call(body, outs, scratch=(), smem=(), count=0, cost=None, grant=20 << 20):
+    whole = pl.BlockSpec(memory_space=pltpu.VMEM)
+    scalar = pl.BlockSpec(memory_space=pltpu.SMEM)
+    return pl.pallas_call(
+        body,
+        out_shape=outs,
+        in_specs=[scalar if k in smem else whole for k in range(count)],
+        out_specs=jax.tree.map(lambda _: whole, outs),
+        scratch_shapes=list(scratch),
+        cost_estimate=cost,
+        compiler_params=pltpu.CompilerParams(vmem_limit_bytes=grant),
+    )
+
+
+def bias_body(pair_ref, gain_ref, weight_ref, present_ref, out_ref):
+    normed = normed_rows(pair_ref[...], gain_ref[...]).astype(jnp.bfloat16)
+    bias = dot_nt(weight_ref[...], normed)
+    present = present_ref[...].astype(jnp.float32)
+    mask_row = jnp.concatenate([present[0:1], present[1:2]], axis=1)
+    fill = jnp.zeros((out_ref.shape[1] - bias.shape[0] - 1, bias.shape[1]), jnp.float32)
+    block = jnp.concatenate([bias, mask_row, fill], axis=0).astype(jnp.bfloat16)
+    out_ref[...] = jnp.broadcast_to(block[None], out_ref.shape)
+
+
+def put_parts(ref, value):
+    lanes = ref.shape[2]
+    for part in range(ref.shape[0]):
+        ref[part] = value[:, part * lanes : (part + 1) * lanes]
+
+
+def rows_of(ref, rows):
+    return jnp.concatenate([ref[part, rows, :] for part in range(ref.shape[0])], axis=1)
+
+
+def project_body(x_ref, gain_ref, ask_ref, look_ref, q_ref, k_ref, v_ref, g_ref):
+    width = ask_ref.shape[1]
+    normed = normed_rows(x_ref[...], gain_ref[...]).astype(jnp.bfloat16)
+    scaling = 1.0 / math.sqrt(PER_FOCUS_WIDTH)
+    q = (dot_nn(normed, ask_ref[...]) * scaling).astype(jnp.bfloat16).astype(jnp.float32)
+    put_parts(q_ref, q)
+    others = dot_nn(normed, look_ref[...])
+    k_ref[...] = others[:, :width].astype(jnp.bfloat16)
+    v_ref[...] = others[:, width : 2 * width].astype(jnp.bfloat16)
+    put_parts(g_ref, jax.nn.sigmoid(others[:, 2 * width :]))
+
+
+def head_spread(q):
+    head_of = lane_iota(q.shape) // PER_FOCUS_WIDTH
+    return jnp.concatenate(
+        [jnp.where(head_of == h, q, 0.0) for h in range(FOCUS_NUMBER)], axis=0
+    ).astype(jnp.bfloat16)
+
+
+def attend_heads(q, k, v, offset):
+    scores = dot_nt(head_spread(q), k) + offset
+    scores = scores - jnp.max(scores, axis=-1, keepdims=True)
+    raised = jnp.exp(scores)
+    shares = (raised / jnp.sum(raised, axis=-1, keepdims=True)).astype(jnp.bfloat16)
+    mixed = dot_nn(shares, v)
+    rows = q.shape[0]
+    head_of = lane_iota(q.shape) // PER_FOCUS_WIDTH
+    total = jnp.where(head_of == 0, mixed[:rows], 0.0)
+    for h in range(1, FOCUS_NUMBER):
+        total = jnp.where(head_of == h, mixed[h * rows : (h + 1) * rows], total)
+    return total
+
+
+def row_body(blk_ref, x_ref, q_ref, k_ref, v_ref, g_ref, final_ref, present_ref, out_ref, wide, send, x_parts):
+    devices = blk_ref.shape[0]
+    put_parts(x_parts, x_ref[...])
+    per_block = blk_ref.shape[1]
+    half = wide.shape[1] // 2
+    per_seq = 2 * devices
+    wide[...] = blk_ref[...].astype(jnp.float32).reshape(wide.shape)
+    penalty = MASK_PENALTY_SCALE * (present_ref[...].astype(jnp.float32) - 1.0)
+    heads = [wide[pl.ds(h, devices, stride=per_block), :] for h in range(FOCUS_NUMBER)]
+    for s in range(2):
+        keys = k_ref[s * per_seq : (s + 1) * per_seq, :]
+        values = v_ref[s * per_seq : (s + 1) * per_seq, :]
+        for r in range(2):
+            rows = pl.ds(s * per_seq + r, devices, stride=2)
+            bias = jnp.concatenate([b[:, r * half : (r + 1) * half] for b in heads], axis=0)
+            mixed = attend_heads(rows_of(q_ref, rows), keys, values, bias + penalty[s : s + 1])
+            y = (mixed * rows_of(g_ref, rows)).astype(jnp.bfloat16)
+            updated = rows_of(x_parts, rows) + dot_nn(y, final_ref[...])
+            for part in range(updated.shape[1] // (2 * half)):
+                to = pl.ds((s * 2 + r) * 2 + part, devices, stride=out_ref.shape[1])
+                send[to, :] = updated[:, part * 2 * half : (part + 1) * 2 * half]
+    out_ref[...] = send[...].reshape(out_ref.shape).astype(jnp.bfloat16)
+
+
+def mask_block(blk_ref, wide):
+    wide[...] = blk_ref[...].astype(jnp.float32).reshape(wide.shape)
+    rows = pl.ds(FOCUS_NUMBER, blk_ref.shape[0], stride=blk_ref.shape[1])
+    return wide[rows, :].astype(jnp.bfloat16)
+
+
+def column_body(
+    arrived_ref, blk_ref, gain_ref, ask_ref, look_ref, final_ref, gain_out_ref, map_ref,
+    msa_ref, opm_ref, wide, wide_blk, x_all, msa,
+):
+    devices = arrived_ref.shape[0]
+    width = ask_ref.shape[1]
+    lanes = wide.shape[1]
+    half = lanes // 2
+    seqs = 2 * devices
+    me = lax.axis_index("dap")
+    wide[...] = arrived_ref[...].astype(jnp.float32).reshape(wide.shape)
+    for r in range(2):
+        for s in range(2):
+            base = (s * 2 + r) * 2
+            at = (r * 2 + s) * devices
+            for part in range(2):
+                x_all[at : at + devices, part * lanes : (part + 1) * lanes] = wide[
+                    pl.ds(base + part, devices, stride=8), :
+                ]
+    mask_lanes = mask_block(blk_ref, wide_blk)
+    row = lax.broadcasted_iota(jnp.int32, (8, lanes), 0)
+    wanted = (row % 2) * half + 2 * me + row // 2
+    pick = jnp.where((lane_iota((8, lanes)) == wanted) & (row < 4), 1.0, 0.0).astype(jnp.bfloat16)
+    picked = dot_nt(pick, mask_lanes)
+    present = [
+        jnp.concatenate([picked[2 * r : 2 * r + 1], picked[2 * r + 1 : 2 * r + 2]], axis=1)
+        for r in range(2)
+    ]
+    x = x_all[...]
+    normed = normed_rows(x, gain_ref[...]).astype(jnp.bfloat16)
+    scaling = 1.0 / math.sqrt(PER_FOCUS_WIDTH)
+    q = (dot_nn(normed, ask_ref[...]) * scaling).astype(jnp.bfloat16).astype(jnp.float32)
+    others = dot_nn(normed, look_ref[...])
+    keys = others[:, :width].astype(jnp.bfloat16)
+    values = others[:, width : 2 * width].astype(jnp.bfloat16)
+    gates = jax.nn.sigmoid(others[:, 2 * width :])
+    mixed = jnp.concatenate(
+        [
+            attend_heads(
+                q[r * seqs : (r + 1) * seqs],
+                keys[r * seqs : (r + 1) * seqs],
+                values[r * seqs : (r + 1) * seqs],
+                MASK_PENALTY_SCALE * (present[r] - 1.0),
+            )
+            for r in range(2)
+        ],
+        axis=0,
+    )
+    updated = x + dot_nn((mixed * gates).astype(jnp.bfloat16), final_ref[...])
+    for r in range(2):
+        for s in range(2):
+            at = (r * 2 + s) * devices
+            for part in range(2):
+                msa[r * 2 + part, pl.ds(s, devices, stride=2), :] = updated[
+                    at : at + devices, part * lanes : (part + 1) * lanes
+                ]
+    for part in range(4):
+        msa_ref[:, part * lanes : (part + 1) * lanes] = msa[part]
+    normed = normed_rows(updated, gain_out_ref[...]).astype(jnp.bfloat16)
+    sides = [
+        dot_nt(map_ref[...], normed[r * seqs : (r + 1) * seqs]) * present[r] for r in range(2)
+    ]
+    block = jnp.concatenate(sides, axis=1).astype(jnp.bfloat16)
+    opm_ref[...] = jnp.broadcast_to(block[None], opm_ref.shape)
+
+
+def gated(projected, q_at, g_at, width):
+    return jax.nn.sigmoid(projected[:, g_at : g_at + width]) * projected[:, q_at : q_at + width]
+
+
+def presence_down(amino_row, half, lanes):
+    square = lax.broadcasted_iota(jnp.int32, (half, half), 0) == lane_iota((half, half))
+    diagonal = jnp.where(square, amino_row.astype(jnp.float32), 0.0).astype(jnp.bfloat16)
+    return dot_nn(diagonal, jnp.ones((half, lanes), jnp.bfloat16))
+
+
+def gathered_at(chip, my_chip, chips):
+    apart = chip ^ my_chip
+    stages = chips.bit_length() - 1
+    place = jnp.int32(0)
+    for k in range(stages):
+        place = place | (((apart >> (stages - 1 - k)) & 1) << k)
+    return place
+
+
+def opm_body(
+    own_ref, oth_ref, blk_ref, near_ref, far_ref, fin_ref, amino_ref, amino_row_ref, gain_ref,
+    flank_ref, switch_ref,
+    pair_one_ref, left_ref, gate_ref, right_ref,
+    order, order16, outer, counts, mkeys, wide_blk,
+):
+    chips, both, lanes = own_ref.shape
+    hidden = both // 2
+    half = lanes // 2
+    channels = switch_ref.shape[0]
+    me = lax.axis_index("dap")
+    parity = lax.rem(me, 2)
+    my_chip = me // 2
+    own = own_ref[:, hidden:, :].astype(jnp.float32)
+    oth = oth_ref[:, hidden:, :].astype(jnp.float32)
+    flag = jnp.broadcast_to(parity, (1, 1, 1)) == 0
+    order16[0] = jnp.where(flag, own, oth).reshape(order16.shape[1:])
+    order16[1] = jnp.where(flag, oth, own).reshape(order16.shape[1:])
+    for b in range(hidden):
+        for p in range(2):
+            rows = order16[p, pl.ds(b, chips, stride=hidden), :]
+            for r in range(2):
+                order[pl.ds(b * half + 2 * p + r, chips, stride=4), :] = (
+                    pltpu.roll(rows, half, 1) if r else rows
+                )
+    rights = order[...].astype(jnp.bfloat16)[:, :half]
+    for r in range(2):
+        lhs = own_ref[:, :hidden, :].reshape(chips * hidden, lanes)[:, r * half : (r + 1) * half]
+        outer[r] = dot_nt(lhs, rights).astype(jnp.bfloat16).reshape(outer.shape[1:])
+    mask_rows = mask_block(blk_ref, wide_blk)
+    total = jnp.zeros((half, lanes), jnp.float32)
+    for s in range(2):
+        part = mask_rows[:, s * half : (s + 1) * half]
+        total = total + dot_tn(part, jnp.concatenate([part, part], axis=1))
+    counts[...] = 1.0 / jnp.maximum(total, 1.0)
+    mkeys[...] = presence_down(amino_row_ref[...], half, lanes)
+    gain = gain_ref[...]
+    low = lane_iota((channels, lanes)) < half
+    low_row = lane_iota((1, lanes)) < half
+    group = 4
+    near = near_ref.shape[0]
+
+    @pl.loop(0, chips // group)
+    def _(block):
+        pairs, keeps = [], []
+        for c in range(group):
+            chip = block * group + c
+            sides = []
+            for r in range(2):
+                strip = outer[r, chip]
+                sides.append(
+                    jnp.concatenate(
+                        [strip[:, g * lanes : (g + 1) * lanes] for g in range(hidden // 2)], axis=0
+                    )
+                )
+            res = dot_nn(fin_ref[...], jnp.concatenate(sides, axis=1))
+            a0, a1 = res[:channels, :lanes], res[:channels, lanes:]
+            b0, b1 = res[channels:, :lanes], res[channels:, lanes:]
+            turned = jnp.where(low, a0, b1) + pltpu.roll(jnp.where(low, a1, b0), half, 1)
+            i0 = 4 * chip + 2 * parity
+            share = jnp.where(low_row, counts[pl.ds(i0, 1), :], counts[pl.ds(i0 + 1, 1), :])
+            place = gathered_at(chip, my_chip, chips)
+            at = lax.rem(place, near)
+            couple = jnp.where(
+                jnp.broadcast_to(place, (1, 1)) < near,
+                near_ref[at].astype(jnp.float32),
+                far_ref[at].astype(jnp.float32),
+            )
+            pairs.append(jnp.transpose(turned * share) + couple)
+            for r in range(2):
+                keeps.append(mkeys[...] * amino_ref[i0 + r].astype(jnp.float32))
+        pair = jnp.concatenate(pairs, axis=0)
+        keep = jnp.concatenate(keeps, axis=0)
+        normed = normed_rows(pair, gain).astype(jnp.bfloat16)
+        projected = dot_nn(normed, flank_ref[...])
+        left = gated(projected, 0, channels, channels) * keep
+        right = gated(projected, 2 * channels, 3 * channels, channels) * keep
+        gate = jax.nn.sigmoid(dot_nn(normed, switch_ref[...]))
+        for c in range(group):
+            chip = block * group + c
+            rows = slice(c * lanes, (c + 1) * lanes)
+            pair_one_ref[chip] = pair[rows]
+            gate_ref[chip] = gate[rows]
+            left_ref[chip] = jnp.transpose(left[rows])
+            right_ref[chip] = jnp.transpose(right[rows]).astype(jnp.bfloat16)
+
+
+def outgoing_body(
+    pair_one_ref, left_ref, gate_ref, own_ref, oth_ref, amino_ref, amino_row_ref, gain_mid_ref,
+    final_ref, gain_ref, flank_ref,
+    two_ref, send_ref,
+    sides, prods, mkeys, pair_two, rows_out, cols,
+):
+    chips, channels, lanes = own_ref.shape
+    half = lanes // 2
+    me = lax.axis_index("dap")
+    parity = lax.rem(me, 2)
+    my_chip = me // 2
+    flag = jnp.broadcast_to(parity, (1, 1)) == 0
+
+    @pl.loop(0, chips)
+    def _(chip):
+        own = own_ref[chip].astype(jnp.float32)
+        oth = oth_ref[chip].astype(jnp.float32)
+        rows = pl.ds(pl.multiple_of(chip * channels, channels), channels)
+        sides[0, rows, :] = jnp.where(flag, own, oth)
+        sides[1, rows, :] = jnp.where(flag, oth, own)
+
+    low = lane_iota((chips, lanes)) < half
+
+    per_step = 32
+
+    @pl.loop(0, channels // per_step)
+    def _(octet):
+        results = []
+        for c in range(per_step):
+            at = pl.ds(octet * per_step + c, chips, stride=channels)
+            lhs = left_ref[at, :].astype(jnp.bfloat16)
+            pieces = [[], []]
+            for p in range(2):
+                rows = sides[p, at, :]
+                turned = pltpu.roll(rows, half, 1)
+                pieces[0] += [jnp.where(low, rows, 0.0), jnp.where(low, turned, 0.0)]
+                pieces[1] += [jnp.where(low, 0.0, turned), jnp.where(low, 0.0, rows)]
+            rhs = jnp.concatenate(pieces[0] + pieces[1], axis=0).astype(jnp.bfloat16)
+            results.append(dot_nt(lhs, rhs))
+        for c in range(per_step):
+            to = pl.ds(pl.multiple_of((octet * per_step + c) * chips, chips), chips)
+            prods[to, :] = results[c].astype(jnp.bfloat16).astype(jnp.float32)
+
+    mkeys[...] = presence_down(amino_row_ref[...], half, channels)
+    gain_mid = jnp.transpose(jnp.broadcast_to(gain_mid_ref[...], (channels, channels)))
+    final_t = jnp.transpose(final_ref[...].astype(jnp.float32)).astype(jnp.bfloat16)
+    gain = gain_ref[...]
+    flank_right = flank_ref[:, 2 * channels :]
+    flank_left = flank_ref[:, : 2 * channels]
+    octet = pl.multiple_of(8 * (my_chip // 2), 8)
+    group = 4
+    for block in range(chips // group):
+        changed = []
+        for c in range(group):
+            x = prods[pl.ds(block * group + c, channels, stride=chips), :]
+            centred = x - jnp.mean(x, axis=0, keepdims=True)
+            spread = jnp.mean(centred * centred, axis=0, keepdims=True)
+            changed.append((centred * lax.rsqrt(spread + EPSILON) * gain_mid).astype(jnp.bfloat16))
+        changed = dot_nn(final_t, jnp.concatenate(changed, axis=1))
+        for c in range(group):
+            part = jnp.transpose(changed[:, c * lanes : (c + 1) * lanes])
+            for k in range(8):
+                r, p, rj = k // 4, (k // 2) % 2, k % 2
+                rows_out[c, pl.ds(r * half + 2 * p + rj, chips, stride=4), :] = part[
+                    k * chips : (k + 1) * chips
+                ]
+        twos, keeps = [], []
+        for c in range(group):
+            chip = block * group + c
+            two = pair_one_ref[chip] + rows_out[c] * gate_ref[chip]
+            twos.append(two)
+            for r in range(2):
+                keeps.append(amino_ref[4 * chip + 2 * parity + r].astype(jnp.float32))
+        two = jnp.concatenate(twos, axis=0)
+        full = normed_rows(two, gain)
+        normed = full.astype(jnp.bfloat16)
+        keep = jnp.concatenate([mkeys[...] * m for m in keeps], axis=0)
+        going = (gated(dot_nn(normed, flank_right), 0, channels, channels) * keep).astype(jnp.bfloat16)
+        cols[...] = full
+        few = jnp.concatenate(
+            [cols[pl.ds(k * half + octet, 8), :] for k in range(2 * group)], axis=0
+        ).astype(jnp.bfloat16)
+        mine = mkeys[pl.ds(octet, 8), :]
+        keep = jnp.concatenate([mine * m for m in keeps], axis=0)
+        few = (gated(dot_nn(few, flank_left), 0, channels, channels) * keep).astype(jnp.bfloat16)
+        for c in range(group):
+            chip = block * group + c
+            pair_two[chip] = twos[c]
+            send_ref[chip, :lanes, :] = going[c * lanes : (c + 1) * lanes]
+            send_ref[chip, lanes:, :] = few[c * 16 : (c + 1) * 16]
+    two_ref[...] = pair_two[my_chip]
+
+
+def incoming_body(
+    own_ref, oth_ref, two_ref, couple_ref, gain_ref, switch_ref, gain_mid_ref, final_ref,
+    out_ref, right, left,
+):
+    chips, _, channels = own_ref.shape
+    lanes2 = out_ref.shape[0]
+    half = lanes2 // 2
+    me = lax.axis_index("dap")
+    first = 4 * lax.rem(me // 2, 2) + 2 * lax.rem(me, 2)
+    row = lax.broadcasted_iota(jnp.int32, (8, channels), 0)
+    totals = tuple(jnp.zeros((half, channels), jnp.float32) for _ in range(2))
+    for side_ref in (own_ref, oth_ref):
+
+        def step(chip, totals, side_ref=side_ref):
+            totals = list(totals)
+            tail = side_ref[chip, lanes2:, :].astype(jnp.float32)
+            for k in range(2):
+                there = side_ref[chip, k * half : (k + 1) * half, :].astype(jnp.float32)
+                for i in range(2):
+                    picked = jnp.where(row == first + i, tail[8 * k : 8 * k + 8], 0.0)
+                    one = jnp.sum(picked, axis=0, keepdims=True)
+                    totals[i] = totals[i] + one * there
+            return tuple(totals)
+
+        totals = lax.fori_loop(0, chips, step, totals)
+    prod = jnp.concatenate(totals, axis=0).astype(jnp.bfloat16).astype(jnp.float32)
+    changed = dot_nn(normed_rows(prod, gain_mid_ref[...]).astype(jnp.bfloat16), final_ref[...])
+    two = two_ref[...]
+    normed = normed_rows(two, gain_ref[...]).astype(jnp.bfloat16)
+    gate = jax.nn.sigmoid(dot_nn(normed, switch_ref[...]))
+    couple = couple_ref[...]
+    lost = couple - couple.astype(jnp.bfloat16).astype(jnp.float32)
+    out_ref[...] = two + lost + changed * gate
+
+
+def paired_shards(
+    homolog_stack,
+    couple_tensor,
+    homolog_presence,
+    amino_presence,
+    horizontal_standard_factor,
+    horizontal_asking_matrix,
+    horizontal_lookup_triple,
+    horizontal_final_matrix,
+    couple_offset_factor,
+    couple_offset_matrix,
+    vertical_standard_factor,
+    vertical_asking_matrix,
+    vertical_lookup_triple,
+    vertical_final_matrix,
+    tensor_average_factor,
+    tensor_average_mapping,
+    tensor_average_final,
+    trio_entry_factors,
+    trio_flank_mappings,
+    trio_final_switches,
+    trio_multiplied_factors,
+    trio_final_matrices,
+):
+    devices = lax.axis_size("dap")
+    chips = devices // 2
+    strands, aminos, features = homolog_stack.shape
+    rows, _, channels = couple_tensor.shape
+    lanes = rows * aminos
+    hidden = TENSOR_HIDDEN
+    f32, bf16 = jnp.float32, jnp.bfloat16
+    shape = jax.ShapeDtypeStruct
+    same_parity = [[2 * chip + p for chip in range(chips)] for p in range(2)]
+    swap = [(d, d ^ 1) for d in range(devices)]
+
+    def line(v):
+        return v.reshape(1, -1)
+
+    couple = couple_tensor.reshape(lanes, channels)
+    x = homolog_stack.reshape(strands * aminos, features)
+    block = vmem_call(
+        bias_body, shape((devices, 16, lanes), bf16), count=4
+    )(couple, line(couple_offset_factor), couple_offset_matrix.T, homolog_presence)
+    blocks = lax.all_to_all(block, "dap", split_axis=0, concat_axis=0, tiled=True)
+    q, k, v, g = vmem_call(
+        project_body,
+        (
+            shape((features // lanes, lanes, lanes), f32),
+            shape((lanes, features), bf16),
+            shape((lanes, features), bf16),
+            shape((features // lanes, lanes, lanes), f32),
+        ),
+        count=4,
+    )(x, line(horizontal_standard_factor), horizontal_asking_matrix, horizontal_lookup_triple)
+    near = couple.astype(bf16)[None]
+    stages = chips.bit_length() - 1
+    for stage in range(stages):
+        reach = devices >> (stage + 1)
+        far = lax.ppermute(near, "dap", [(d, d ^ reach) for d in range(devices)])
+        if stage < stages - 1:
+            near = jnp.concatenate([near, far], axis=0)
+    sent = vmem_call(
+        row_body,
+        shape((devices, 8, lanes), bf16),
+        scratch=[
+            pltpu.VMEM((devices * 16, lanes), f32),
+            pltpu.VMEM((devices * 8, lanes), f32),
+            pltpu.VMEM((features // lanes, lanes, lanes), f32),
+        ],
+        count=8,
+    )(blocks, x, q, k, v, g, horizontal_final_matrix, homolog_presence)
+    arrived = lax.all_to_all(sent, "dap", split_axis=0, concat_axis=0, tiled=True)
+    msa, opm = vmem_call(
+        column_body,
+        (shape((devices * strands, rows * features), f32), shape((chips, 2 * hidden, lanes), bf16)),
+        scratch=[
+            pltpu.VMEM((devices * 8, lanes), f32),
+            pltpu.VMEM((devices * 16, lanes), f32),
+            pltpu.VMEM((lanes, features), f32),
+            pltpu.VMEM((4, devices * strands, lanes), f32),
+        ],
+        count=8,
+    )(
+        arrived,
+        blocks,
+        line(vertical_standard_factor),
+        vertical_asking_matrix,
+        vertical_lookup_triple,
+        vertical_final_matrix,
+        line(tensor_average_factor),
+        tensor_average_mapping.T,
+    )
+    opm_own = lax.all_to_all(
+        opm, "dap", split_axis=0, concat_axis=0, tiled=True, axis_index_groups=same_parity
+    )
+    opm_oth = lax.ppermute(opm_own, "dap", swap)
+    final = jnp.transpose(
+        tensor_average_final.reshape(hidden, hidden // 2, 2, channels), (2, 3, 1, 0)
+    ).reshape(2 * channels, hidden * hidden // 2)
+    stack = (chips, lanes, channels)
+    amino_row = line(amino_presence)
+    pair_one, left, gate, right_own = vmem_call(
+        opm_body,
+        (shape(stack, f32), shape(stack, f32), shape(stack, f32), shape(stack, bf16)),
+        scratch=[
+            pltpu.VMEM((hidden * aminos, lanes), f32),
+            pltpu.VMEM((2, chips * hidden, lanes), f32),
+            pltpu.VMEM((2, chips, hidden, hidden * aminos), bf16),
+            pltpu.VMEM((aminos, lanes), f32),
+            pltpu.VMEM((aminos, channels), f32),
+            pltpu.VMEM((devices * 16, lanes), f32),
+        ],
+        smem=(6,),
+        count=11,
+    )(
+        opm_own,
+        opm_oth,
+        blocks,
+        near,
+        far,
+        final,
+        amino_presence,
+        amino_row,
+        line(trio_entry_factors[0]),
+        trio_flank_mappings[0],
+        trio_final_switches[0],
+    )
+    right_oth = lax.ppermute(right_own, "dap", swap)
+    two, going = vmem_call(
+        outgoing_body,
+        (shape((lanes, channels), f32), shape((chips, lanes + 16, channels), bf16)),
+        scratch=[
+            pltpu.VMEM((2, chips * channels, lanes), f32),
+            pltpu.VMEM((channels * chips, lanes), f32),
+            pltpu.VMEM((aminos, channels), f32),
+            pltpu.VMEM(stack, f32),
+            pltpu.VMEM((4, lanes, channels), f32),
+            pltpu.VMEM((4 * lanes, channels), f32),
+        ],
+        smem=(5,),
+        count=11,
+    )(
+        pair_one,
+        left.reshape(chips * channels, lanes),
+        gate,
+        right_own,
+        right_oth,
+        amino_presence,
+        amino_row,
+        line(trio_multiplied_factors[0]),
+        trio_final_matrices[0],
+        line(trio_entry_factors[1]),
+        trio_flank_mappings[1],
+    )
+    coming = lax.ppermute(going, "dap", swap)
+    pair_out = vmem_call(
+        incoming_body,
+        shape((lanes, channels), f32),
+        scratch=[pltpu.VMEM((8, channels), f32), pltpu.VMEM((8, channels), f32)],
+        count=8,
+    )(
+        going,
+        coming,
+        two,
+        couple,
+        line(trio_entry_factors[1]),
+        trio_final_switches[1],
+        line(trio_multiplied_factors[1]),
+        trio_final_matrices[1],
+    )
+    return (
+        msa.reshape(devices * strands, rows, features),
+        pair_out.reshape(rows, aminos, channels),
+    )
+
+
+def fits_pairs(homolog_stack, couple_tensor, devices):
+    strands, aminos, features = homolog_stack.shape
+    rows, _, channels = couple_tensor.shape
+    lanes = 128
+    return (
+        strands == rows == 2
+        and devices % 8 == 0
+        and devices & (devices - 1) == 0
+        and rows * aminos == lanes == channels
+        and aminos == 2 * devices
+        and features == 2 * lanes
+    )
+
+
+def either(*arrays):
+    if fits_pairs(arrays[0], arrays[1], lax.axis_size("dap")):
+        return paired_shards(*arrays)
+    return shards(*arrays)
+
+
 def solution(mesh):
     placed = (
         P("dap", None, None),
@@ -297,7 +914,7 @@
         P(),
     )
     return jax.shard_map(
-        shards,
+        either,
         mesh=mesh,
         in_specs=placed,
         out_specs=(P(None, "dap", None), P("dap", None, None)),

time: 101 us -> 74.7 us (0.74)
  blocking collectives: 28 us -> 0 us
  Pallas kernels: 0 us -> 21.8 us
  local copies, waits for them, and re-layouts: 17.5 us -> 7.13 us
  matrix products: 6.79 us -> 0 us
  starting transfers between devices: 15.2 us -> 21.9 us
  waiting for transfers between devices: 28.6 us -> 22.4 us
  other arithmetic: 3.24 us -> 0.06 us
    all_to_all x3 -> x0, blocking collectives: 28 us -> none  [the longest x2 18.5 us: triangle(): both = lax.all_to_all(both, 'dap', split_axis=0, concat_axis=0, tiled=True)]
    pallas_call x0 -> x7, Pallas kernels: none -> 21.8 us  [the longest x1 7.89 us: paired_shards(): vmem_call(opm_body, (shape(stack, f32), shape(stack, f32), shape(stack, f...]
    all_to_all x4 -> x3, waiting for transfers between devices: 28.6 us -> 10.5 us  [the longest x1 5.85 us: paired_shards(): lax.all_to_all(sent, 'dap', split_axis=0, concat_axis=0, tiled=True)]
    ppermute x0 -> x7, waiting for transfers between devices: none -> 11.8 us  [the longest x4 9.41 us: paired_shards(): far = lax.ppermute(near, 'dap', [(d, d ^ reach) for d in range(devices)])]
    ppermute x0 -> x7, starting transfers between devices: none -> 8.37 us  [the longest x4 8.1 us: paired_shards(): far = lax.ppermute(near, 'dap', [(d, d ^ reach) for d in range(devices)])]
    unnamed x60 -> x47, local copies, waits for them, and re-layouts: 13.7 us -> 5.98 us
    dot_general x23 -> x0, matrix products: 6.01 us -> none  [the longest x2 1.17 us: triangle(): jnp.dot(standardized_source, gate_weight, preferred_element_type=jnp.floa...]
    reduce_sum x13 -> x0, other arithmetic: 2.42 us -> none  [the longest x5 1.29 us: standardize_features(): jnp.mean(content_vectors, axis=axis, keepdims=True)]
  transfers between devices with their start and end apart: 4 -> 10, of which waited for: 4 -> 7; matrix products, arithmetic and copies ran while one was open for 2% -> 2% of each run, Pallas kernels for 0% -> 7%
where the time goes in v2:
time: 74.7 us; the launch traced here: 74.2 us
  waiting for transfers between devices  22.4 us (30%)
  starting transfers between devices  21.9 us (29%)
  Pallas kernels  21.8 us (29%)
  local copies, waits for them, and re-layouts  7.13 us (10%)
  between operations  0.89 us (1%)
    ppermute x4, waiting for transfers between devices, paired_shards(): far = lax.ppermute(near, 'dap', [(d, d ^ reach) for d in range(devices)])  9.41 us
    ppermute x4, starting transfers between devices, paired_shards(): far = lax.ppermute(near, 'dap', [(d, d ^ reach) for d in range(devices)])  8.1 us
    pallas_call x1, Pallas kernels, paired_shards(): vmem_call(opm_body, (shape(stack, f32), shape(stack, f32), shape(stack, f...  7.89 us
    all_to_all x1, starting transfers between devices, paired_shards(): lax.all_to_all(block, 'dap', split_axis=0, concat_axis=0, tiled=True)  7.33 us
    pallas_call x1, Pallas kernels, paired_shards(): vmem_call(outgoing_body, (shape((lanes, channels), f32), shape((chips, la...  6.28 us
    unnamed x47, local copies, waits for them, and re-layouts  5.98 us
    all_to_all x1, waiting for transfers between devices, paired_shards(): lax.all_to_all(sent, 'dap', split_axis=0, concat_axis=0, tiled=True)  5.85 us
    all_to_all x1, starting transfers between devices, paired_shards(): lax.all_to_all(opm, 'dap', split_axis=0, concat_axis=0, tiled=True, axis_...  3.53 us
  transfers between devices with their start and end apart: 10, of which 7 were waited for; matrix products, arithmetic and copies ran while one was open for 2% of the time, Pallas kernels for 7%

profile of v2, /device:TPU:0, one launch (start us, length us, event | category | flops | bytes accessed | tf_op | source)
XLA Modules:
  0.0 74.2 jit_solution(1288566578895214525)
XLA Ops:
  0.7 0.7 copy-done.12
  1.3 0.0 copy-done.11
  1.3 0.8 %copy-done = f32[2,64,128]{2,1,0:T(8,128)S(1)} copy-done((f32[2,64,128]{2,1,0:T(8,128)S(1)}, f32[2,64,128]{2,1,0:T(8,128)}, u32[]{:S(2)}) %copy-start) | copy-done | bytes 65560
  2.2 1.0 %shard_map.221 = bf16[32,16,128]{2,1,0:T(8,128)(2,1)} custom-call(f32[128,128]{1,0:T(8,128)S(1)} %bitcast.34, f32[1,128]{1,0:T(1,128)S(1)} %bitcast.45, bf16[8,128]{1,0:T(8,128)(2,1)S(1)} %bitcast.41, s32[2,64]{1,0:T(2,128)S(1)} %copy-done.11), custom_call_target="tpu_custom_call" | custom-call | tf_op jit(solution)/shard_map/pallas_call | solution.py:735
  3.2 7.3 %all-to-all-start = ((bf16[32,16,128]{2,1,0:T(8,128)(2,1)}), bf16[32,16,128]{2,1,0:T(8,128)(2,1)S(1)}, u32[]{:S(2)}, u32[]{:S(2)}) async-start(bf16[32,16,128]{2,1,0:T(8,128)(2,1)} %shard_map.221), calls=%async_computation | async-start | bytes 262144 | tf_op jit(solution)/shard_map/all_to_all | solution.py:738
  10.5 2.7 %collective-permute-start.1 = (bf16[1,128,128]{2,1,0:T(8,128)(2,1)S(1)}, bf16[1,128,128]{2,1,0:T(8,128)(2,1)S(1)}, u32[]{:S(2)}, u32[]{:S(2)}) collective-permute-start(bf16[1,128,128]{2,1,0:T(8,128)(2,1)S(1)} %bitcast.48), channel_id=1, source_target_pairs={{0,16},{1,17},{2,18},{3,19},{4,20},{5,21},{6,22},{7,23},{8,24},{9,... | collective-permute-start | bytes 98312 | tf_op jit(solution)/shard_map/ppermute | solution.py:753
  13.3 0.0 copy-done.5
  13.3 0.7 copy-done.13
  13.9 1.0 %copy-done.4 = bf16[256,768]{1,0:T(8,128)(2,1)S(1)} copy-done((bf16[256,768]{1,0:T(8,128)(2,1)S(1)}, bf16[256,768]{1,0:T(8,128)(2,1)}, u32[]{:S(2)}) %copy-start.4) | copy-done | bytes 393240
  14.9 0.4 shard_map.222
  15.3 3.5 %all-to-all-done.blk_ref = bf16[32,16,128]{2,1,0:T(8,128)(2,1)S(1)} async-done(((bf16[32,16,128]{2,1,0:T(8,128)(2,1)}), bf16[32,16,128]{2,1,0:T(8,128)(2,1)S(1)}, u32[]{:S(2)}, u32[]{:S(2)}) %all-to-all-start) | async-done | bytes 131104 | tf_op jit(solution)/shard_map/all_to_all | solution.py:738
  18.8 0.0 copy-done.8
  18.8 2.3 %shard_map.223 = bf16[32,8,128]{2,1,0:T(8,128)(2,1)} custom-call(bf16[32,16,128]{2,1,0:T(8,128)(2,1)S(1)} %all-to-all-done.blk_ref, f32[128,256]{1,0:T(8,128)S(1)} %bitcast.37, f32[2,128,128]{2,1,0:T(8,128)S(1)} %get-tuple-element.14.q_ref, bf16[128,256]{1,0:T(8,128)(2,1)S(1)} %get-tuple-element.15.k_ref, bf16[128,256]{1,0:T(8,128)(2,1)S(1)} %get-tuple-element.16.v_ref, ...), custom_call_target="tpu_custom_call" | custom-call | tf_op jit(solution)/shard_map/pallas_call | solution.py:756
  21.1 2.7 %all-to-all-start.1 = ((bf16[32,8,128]{2,1,0:T(8,128)(2,1)}), bf16[32,8,128]{2,1,0:T(8,128)(2,1)S(1)}, u32[]{:S(2)}, u32[]{:S(2)}) async-start(bf16[32,8,128]{2,1,0:T(8,128)(2,1)} %shard_map.223), calls=%async_computation.1 | async-start | bytes 131072 | tf_op jit(solution)/shard_map/all_to_all | solution.py:766
  23.9 0.0 collective-permute-done.1
  23.9 0.0 copy-start.15
  23.9 1.8 %collective-permute-start.2 = (bf16[2,128,128]{2,1,0:T(8,128)(2,1)S(1)}, bf16[2,128,128]{2,1,0:T(8,128)(2,1)S(1)}, u32[]{:S(2)}, u32[]{:S(2)}) collective-permute-start(bf16[2,128,128]{2,1,0:T(8,128)(2,1)S(1)} %pad_maximum_fusion.2), channel_id=1, source_target_pairs={{0,8},{1,9},{2,10},{3,11},{4,12},{5,13},{6,14},{7,15},{8,0},{9,1},... | collective-permute-start | bytes 196616 | tf_op jit(solution)/shard_map/ppermute | solution.py:753
  25.7 5.8 %all-to-all-done.1.arrived_ref = bf16[32,8,128]{2,1,0:T(8,128)(2,1)S(1)} async-done(((bf16[32,8,128]{2,1,0:T(8,128)(2,1)}), bf16[32,8,128]{2,1,0:T(8,128)(2,1)S(1)}, u32[]{:S(2)}, u32[]{:S(2)}) %all-to-all-start.1) | async-done | bytes 65568 | tf_op jit(solution)/shard_map/all_to_all | solution.py:766
  31.6 0.0 copy-done.9
  31.6 0.6 copy-done.14
  32.2 2.4 %shard_map.224 = (f32[64,512]{1,0:T(8,128)S(1)}, bf16[16,64,128]{2,1,0:T(8,128)(2,1)}) custom-call(bf16[32,8,128]{2,1,0:T(8,128)(2,1)S(1)} %all-to-all-done.1.arrived_ref, bf16[32,16,128]{2,1,0:T(8,128)(2,1)S(1)} %all-to-all-done.blk_ref, f32[1,256]{1,0:T(1,128)S(1)} %bitcast.43, bf16[256,256]{1,0:T(8,128)(2,1)S(1)} %copy-done.6, ...), custom_call_target="tpu_custom_call" | custom-call | tf_op jit(solution)/shard_map/pallas_call | solution.py:767
  34.6 3.5 %all-to-all-start.2 = ((bf16[16,64,128]{2,1,0:T(8,128)(2,1)}), bf16[16,64,128]{2,1,0:T(8,128)(2,1)S(1)}, u32[]{:S(2)}, u32[]{:S(2)}) async-start(bf16[16,64,128]{2,1,0:T(8,128)(2,1)} %get-tuple-element.19), calls=%async_computation.2 | async-start | bytes 524288 | tf_op jit(solution)/shard_map/all_to_all | solution.py:787
  38.2 0.0 copy-start.19
  38.2 0.0 collective-permute-done.2
  38.2 1.9 %collective-permute-start.3 = (bf16[4,128,128]{2,1,0:T(8,128)(2,1)S(1)}, bf16[4,128,128]{2,1,0:T(8,128)(2,1)S(1)}, u32[]{:S(2)}, u32[]{:S(2)}) collective-permute-start(bf16[4,128,128]{2,1,0:T(8,128)(2,1)S(1)} %pad_maximum_fusion.1), channel_id=1, source_target_pairs={{0,4},{1,5},{2,6},{3,7},{4,0},{5,1},{6,2},{7,3},{8,12},{9,13},{10,... | collective-permute-start | bytes 393224 | tf_op jit(solution)/shard_map/ppermute | solution.py:753
  40.1 0.0 copy-start.21
  40.1 0.0 copy-start.17
  40.1 5.6 %collective-permute-done.3 = bf16[4,128,128]{2,1,0:T(8,128)(2,1)S(1)} collective-permute-done((bf16[4,128,128]{2,1,0:T(8,128)(2,1)S(1)}, bf16[4,128,128]{2,1,0:T(8,128)(2,1)S(1)}, u32[]{:S(2)}, u32[]{:S(2)}) %collective-permute-start.3) | collective-permute-done | bytes 131104 | tf_op jit(solution)/shard_map/ppermute | solution.py:753
  45.8 1.7 %collective-permute-start.4 = (bf16[8,128,128]{2,1,0:T(8,128)(2,1)S(1)}, bf16[8,128,128]{2,1,0:T(8,128)(2,1)S(1)}, u32[]{:S(2)}, u32[]{:S(2)}) collective-permute-start(bf16[8,128,128]{2,1,0:T(8,128)(2,1)S(1)} %pad_maximum_fusion.near_ref), channel_id=1, source_target_pairs={{0,2},{1,3},{2,0},{3,1},{4,6},{5,7},{6,4},{7,5},{8,10},{9,11},{10,... | collective-permute-start | bytes 786440 | tf_op jit(solution)/shard_map/ppermute | solution.py:753
  47.5 1.2 %all-to-all-done.2.own_ref = bf16[16,64,128]{2,1,0:T(8,128)(2,1)S(1)} async-done(((bf16[16,64,128]{2,1,0:T(8,128)(2,1)}), bf16[16,64,128]{2,1,0:T(8,128)(2,1)S(1)}, u32[]{:S(2)}, u32[]{:S(2)}) %all-to-all-start.2) | async-done | bytes 262176 | tf_op jit(solution)/shard_map/all_to_all | solution.py:787
  48.6 0.0 collective-permute-start
  48.7 0.2 copy.25
  49.0 0.0 copy-start.18
  49.0 0.1 copy.26.fin_ref
  49.1 0.8 %copy-done.18 = bf16[2,128,512]{2,1,0:T(8,128)(2,1)S(1)} copy-done((bf16[2,128,512]{2,1,0:T(8,128)(2,1)S(1)}, bf16[2,128,512]{2,1,0:T(8,128)(2,1)}, u32[]{:S(2)}) %copy-start.18) | copy-done | bytes 262168
  49.9 3.8 %collective-permute-done.4.far_ref = bf16[8,128,128]{2,1,0:T(8,128)(2,1)S(1)} collective-permute-done((bf16[8,128,128]{2,1,0:T(8,128)(2,1)S(1)}, bf16[8,128,128]{2,1,0:T(8,128)(2,1)S(1)}, u32[]{:S(2)}, u32[]{:S(2)}) %collective-permute-start.4) | collective-permute-done | bytes 262176 | tf_op jit(solution)/shard_map/ppermute | solution.py:753
  53.7 0.0 collective-permute-done.oth_ref
  53.7 0.7 copy-done.10
  54.4 7.9 %shard_map.225 = (f32[16,128,128]{2,1,0:T(8,128)S(1)}, f32[16,128,128]{2,1,0:T(8,128)S(1)}, f32[16,128,128]{2,1,0:T(8,128)S(1)}, bf16[16,128,128]{2,1,0:T(8,128)(2,1)S(1)}) custom-call(bf16[16,64,128]{2,1,0:T(8,128)(2,1)S(1)} %all-to-all-done.2.own_ref, bf16[16,64,128]{2,1,0:T(8,128)(2,1)S(1)} %collective-permute-done.oth_ref, ...), custom_call_target="tpu_custom_call" | custom-call | tf_op jit(solution)/shard_map/pallas_call | solution.py:796
  62.3 0.0 copy-start.22
  62.3 0.1 collective-permute-start.5
  62.3 0.6 copy-done.22
  63.0 1.3 %collective-permute-done.5.oth_ref = bf16[16,128,128]{2,1,0:T(8,128)(2,1)S(1)} collective-permute-done((bf16[16,128,128]{2,1,0:T(8,128)(2,1)S(1)}, bf16[16,128,128]{2,1,0:T(8,128)(2,1)S(1)}, u32[]{:S(2)}, u32[]{:S(2)}) %collective-permute-start.5) | collective-permute-done | bytes 524320 | tf_op jit(solution)/shard_map/ppermute | solution.py:822
  64.2 6.3 %shard_map.226 = (f32[128,128]{1,0:T(8,128)S(1)}, bf16[16,144,128]{2,1,0:T(8,128)(2,1)S(1)}) custom-call(f32[16,128,128]{2,1,0:T(8,128)S(1)} %get-tuple-element.20.pair_one_ref, f32[2048,128]{1,0:T(8,128)S(1)} %bitcast.33, f32[16,128,128]{2,1,0:T(8,128)S(1)} %get-tuple-element.22.gate_ref, bf16[16,128,128]{2,1,0:T(8,128)(2,1)S(1)} %get-tuple-element.23.own_ref, ...), custom_call_target="tpu_custom_call" | custom-call | tf_op jit(solution)/shard_map/pallas_call | solution.py:823
  70.5 0.2 collective-permute-start.6
  70.7 0.7 reshape.57
  71.5 1.1 %collective-permute-done.6.oth_ref = bf16[16,144,128]{2,1,0:T(8,128)(2,1)S(1)} collective-permute-done((bf16[16,144,128]{2,1,0:T(8,128)(2,1)S(1)}, bf16[16,144,128]{2,1,0:T(8,128)(2,1)S(1)}, u32[]{:S(2)}, u32[]{:S(2)}) %collective-permute-start.6) | collective-permute-done | bytes 589856 | tf_op jit(solution)/shard_map/ppermute | solution.py:849
  72.6 1.6 %shard_map.227 = f32[128,128]{1,0:T(8,128)} custom-call(bf16[16,144,128]{2,1,0:T(8,128)(2,1)S(1)} %get-tuple-element.24.own_ref, bf16[16,144,128]{2,1,0:T(8,128)(2,1)S(1)} %collective-permute-done.6.oth_ref, f32[128,128]{1,0:T(8,128)S(1)} %get-tuple-element.25.two_ref, f32[128,128]{1,0:T(8,128)S(1)} %bitcast.35, f32[1,128]{1,0:T(1,128)S(1)} %get-tuple-element.34.gain_ref, ...), custom_call_target="tpu_custom_call" | custom-call | tf_op jit(solution)/shard_map/pallas_call | solution.py:850
  (38 shorter events, 0.2 us)
Async XLA Ops:
  0.6 0.7 copy-start.12
  0.6 0.7 copy-start.11
  0.7 0.7 copy-start.16
  1.3 0.8 %copy-start = (f32[2,64,128]{2,1,0:T(8,128)S(1)}, f32[2,64,128]{2,1,0:T(8,128)}, u32[]{:S(2)}) copy-start(f32[2,64,128]{2,1,0:T(8,128)} %param.23) | copy-start | bytes 196612
  3.1 7.3 %copy-start.1 = (f32[2,64,128]{2,1,0:T(8,128)S(1)}, f32[2,64,128]{2,1,0:T(8,128)}, u32[]{:S(2)}) copy-start(f32[2,64,128]{2,1,0:T(8,128)} %param.23) | copy-start | bytes 196612
  3.1 10.1 %copy-start.2 = (f32[2,64,256]{2,1,0:T(8,128)S(1)}, f32[2,64,256]{2,1,0:T(8,128)}, u32[]{:S(2)}) copy-start(f32[2,64,256]{2,1,0:T(8,128)} %param.22) | copy-start | bytes 393220
  3.2 10.1 %copy-start.5 = (bf16[256,256]{1,0:T(8,128)(2,1)S(1)}, bf16[256,256]{1,0:T(8,128)(2,1)}, u32[]{:S(2)}) copy-start(bf16[256,256]{1,0:T(8,128)(2,1)} %ask_ref.2) | copy-start | bytes 393220
  3.2 15.7 %all-to-all-start = ((bf16[32,16,128]{2,1,0:T(8,128)(2,1)}), bf16[32,16,128]{2,1,0:T(8,128)(2,1)S(1)}, u32[]{:S(2)}, u32[]{:S(2)}) async-start(bf16[32,16,128]{2,1,0:T(8,128)(2,1)} %shard_map.221), calls=%async_computation | async-start | bytes 262144 | tf_op jit(solution)/shard_map/all_to_all | solution.py:738
  10.5 13.3 %collective-permute-start.1 = (bf16[1,128,128]{2,1,0:T(8,128)(2,1)S(1)}, bf16[1,128,128]{2,1,0:T(8,128)(2,1)S(1)}, u32[]{:S(2)}, u32[]{:S(2)}) collective-permute-start(bf16[1,128,128]{2,1,0:T(8,128)(2,1)S(1)} %bitcast.48), channel_id=1, source_target_pairs={{0,16},{1,17},{2,18},{3,19},{4,20},{5,21},{6,22},{7,23},{8,24},{9,... | collective-permute-start | bytes 98312 | tf_op jit(solution)/shard_map/ppermute | solution.py:753
  13.3 0.7 copy-start.13
  13.9 1.0 %copy-start.4 = (bf16[256,768]{1,0:T(8,128)(2,1)S(1)}, bf16[256,768]{1,0:T(8,128)(2,1)}, u32[]{:S(2)}) copy-start(bf16[256,768]{1,0:T(8,128)(2,1)} %look_ref.2) | copy-start | bytes 1179652
  14.9 3.9 %copy-start.8 = (bf16[256,256]{1,0:T(8,128)(2,1)S(1)}, bf16[256,256]{1,0:T(8,128)(2,1)}, u32[]{:S(2)}) copy-start(bf16[256,256]{1,0:T(8,128)(2,1)} %final_ref.2) | copy-start | bytes 393220
  18.8 12.7 %copy-start.3 = (bf16[256,768]{1,0:T(8,128)(2,1)S(1)}, bf16[256,768]{1,0:T(8,128)(2,1)}, u32[]{:S(2)}) copy-start(bf16[256,768]{1,0:T(8,128)(2,1)} %look_ref.3) | copy-start | bytes 1179652
  18.8 12.7 %copy-start.9 = (bf16[256,64]{0,1:T(8,128)(2,1)S(1)}, bf16[256,64]{0,1:T(8,128)(2,1)}, u32[]{:S(2)}) copy-start(bf16[256,64]{0,1:T(8,128)(2,1)} %param.37) | copy-start | bytes 98308
  21.1 10.5 %copy-start.6 = (bf16[256,256]{1,0:T(8,128)(2,1)S(1)}, bf16[256,256]{1,0:T(8,128)(2,1)}, u32[]{:S(2)}) copy-start(bf16[256,256]{1,0:T(8,128)(2,1)} %ask_ref.3) | copy-start | bytes 393220
  21.1 10.5 %copy-start.7 = (bf16[256,256]{1,0:T(8,128)(2,1)S(1)}, bf16[256,256]{1,0:T(8,128)(2,1)}, u32[]{:S(2)}) copy-start(bf16[256,256]{1,0:T(8,128)(2,1)} %final_ref.3) | copy-start | bytes 393220
  21.1 10.4 %all-to-all-start.1 = ((bf16[32,8,128]{2,1,0:T(8,128)(2,1)}), bf16[32,8,128]{2,1,0:T(8,128)(2,1)S(1)}, u32[]{:S(2)}, u32[]{:S(2)}) async-start(bf16[32,8,128]{2,1,0:T(8,128)(2,1)} %shard_map.223), calls=%async_computation.1 | async-start | bytes 131072 | tf_op jit(solution)/shard_map/all_to_all | solution.py:766
  23.9 7.7 %copy-start.15 = (f32[256]{0:T(256)S(1)}, f32[256]{0:T(256)}, u32[]{:S(2)}) copy-start(f32[256]{0:T(256)} %param.36) | copy-start | bytes 3076
  23.9 14.3 %collective-permute-start.2 = (bf16[2,128,128]{2,1,0:T(8,128)(2,1)S(1)}, bf16[2,128,128]{2,1,0:T(8,128)(2,1)S(1)}, u32[]{:S(2)}, u32[]{:S(2)}) collective-permute-start(bf16[2,128,128]{2,1,0:T(8,128)(2,1)S(1)} %pad_maximum_fusion.2), channel_id=1, source_target_pairs={{0,8},{1,9},{2,10},{3,11},{4,12},{5,13},{6,14},{7,15},{8,0},{9,1},... | collective-permute-start | bytes 196616 | tf_op jit(solution)/shard_map/ppermute | solution.py:753
  31.6 0.7 copy-start.14
  34.6 14.0 %all-to-all-start.2 = ((bf16[16,64,128]{2,1,0:T(8,128)(2,1)}), bf16[16,64,128]{2,1,0:T(8,128)(2,1)S(1)}, u32[]{:S(2)}, u32[]{:S(2)}) async-start(bf16[16,64,128]{2,1,0:T(8,128)(2,1)} %get-tuple-element.19), calls=%async_computation.2 | async-start | bytes 524288 | tf_op jit(solution)/shard_map/all_to_all | solution.py:787
  38.2 1.9 %copy-start.19 = (bf16[2,128,128]{2,1,0:T(8,128)(2,1)S(1)}, bf16[2,128,128]{2,1,0:T(8,128)(2,1)}, u32[]{:S(2)}) copy-start(bf16[2,128,128]{2,1,0:T(8,128)(2,1)} %param.41) | copy-start | bytes 196612
  38.2 7.5 %collective-permute-start.3 = (bf16[4,128,128]{2,1,0:T(8,128)(2,1)S(1)}, bf16[4,128,128]{2,1,0:T(8,128)(2,1)S(1)}, u32[]{:S(2)}, u32[]{:S(2)}) collective-permute-start(bf16[4,128,128]{2,1,0:T(8,128)(2,1)S(1)} %pad_maximum_fusion.1), channel_id=1, source_target_pairs={{0,4},{1,5},{2,6},{3,7},{4,0},{5,1},{6,2},{7,3},{8,12},{9,13},{10,... | collective-permute-start | bytes 393224 | tf_op jit(solution)/shard_map/ppermute | solution.py:753
  40.1 8.5 %copy-start.21 = (f32[2,128]{1,0:T(2,128)S(1)}, f32[2,128]{1,0:T(2,128)}, u32[]{:S(2)}) copy-start(f32[2,128]{1,0:T(2,128)} %param.39) | copy-start | bytes 3076
  40.1 8.5 %copy-start.17 = (bf16[1024,128]{1,0:T(8,128)(2,1)S(1)}, bf16[1024,128]{1,0:T(8,128)(2,1)}, u32[]{:S(2)}) copy-start(bf16[1024,128]{1,0:T(8,128)(2,1)} %param.38) | copy-start | bytes 786436
  45.8 7.9 %collective-permute-start.4 = (bf16[8,128,128]{2,1,0:T(8,128)(2,1)S(1)}, bf16[8,128,128]{2,1,0:T(8,128)(2,1)S(1)}, u32[]{:S(2)}, u32[]{:S(2)}) collective-permute-start(bf16[8,128,128]{2,1,0:T(8,128)(2,1)S(1)} %pad_maximum_fusion.near_ref), channel_id=1, source_target_pairs={{0,2},{1,3},{2,0},{3,1},{4,6},{5,7},{6,4},{7,5},{8,10},{9,11},{10,... | collective-permute-start | bytes 786440 | tf_op jit(solution)/shard_map/ppermute | solution.py:753
  48.6 5.1 %collective-permute-start = (bf16[16,64,128]{2,1,0:T(8,128)(2,1)S(1)}, bf16[16,64,128]{2,1,0:T(8,128)(2,1)S(1)}, u32[]{:S(2)}, u32[]{:S(2)}) collective-permute-start(bf16[16,64,128]{2,1,0:T(8,128)(2,1)S(1)} %all-to-all-done.2.own_ref), channel_id=1, source_target_pairs={{0,1},{1,0},{2,3},{3,2},{4,5},{5,4},{6,7},{7,6},{8,9},{9,8},{10,11... | collective-permute-start | bytes 786440 | tf_op jit(solution)/shard_map/ppermute | solution.py:790
  49.0 1.0 %copy-start.18 = (bf16[2,128,512]{2,1,0:T(8,128)(2,1)S(1)}, bf16[2,128,512]{2,1,0:T(8,128)(2,1)}, u32[]{:S(2)}) copy-start(bf16[2,128,512]{2,1,0:T(8,128)(2,1)} %param.40) | copy-start | bytes 786436
  53.7 0.7 copy-start.10
  54.4 8.6 %copy-start.20 = (bf16[2,128,128]{2,1,0:T(8,128)(2,1)S(1)}, bf16[2,128,128]{2,1,0:T(8,128)(2,1)}, u32[]{:S(2)}) copy-start(bf16[2,128,128]{2,1,0:T(8,128)(2,1)} %param.43) | copy-start | bytes 196612
  62.3 0.7 copy-start.22
  62.3 2.0 %collective-permute-start.5 = (bf16[16,128,128]{2,1,0:T(8,128)(2,1)S(1)}, bf16[16,128,128]{2,1,0:T(8,128)(2,1)S(1)}, u32[]{:S(2)}, u32[]{:S(2)}) collective-permute-start(bf16[16,128,128]{2,1,0:T(8,128)(2,1)S(1)} %get-tuple-element.23.own_ref), channel_id=1, source_target_pairs={{0,1},{1,0},{2,3},{3,2},{4,5},{5,4},{6,7},{7,6},{8,9},{9,8},{10,11... | collective-permute-start | bytes 1572872 | tf_op jit(solution)/shard_map/ppermute | solution.py:822
  70.5 2.1 %collective-permute-start.6 = (bf16[16,144,128]{2,1,0:T(8,128)(2,1)S(1)}, bf16[16,144,128]{2,1,0:T(8,128)(2,1)S(1)}, u32[]{:S(2)}, u32[]{:S(2)}) collective-permute-start(bf16[16,144,128]{2,1,0:T(8,128)(2,1)S(1)} %get-tuple-element.24.own_ref), channel_id=1, source_target_pairs={{0,1},{1,0},{2,3},{3,2},{4,5},{5,4},{6,7},{7,6},{8,9},{9,8},{10,11... | collective-permute-start | bytes 1769480 | tf_op jit(solution)/shard_map/ppermute | solution.py:849

commit v3 on v2

--- a/solution.py
+++ b/solution.py
@@ -1,3 +1,4 @@
+import functools
 import math
 
 import jax
@@ -295,25 +296,43 @@
     return lax.broadcasted_iota(jnp.int32, shape, len(shape) - 1)
 
 
-def vmem_call(body, outs, scratch=(), smem=(), count=0, cost=None, grant=20 << 20):
+def vmem_call(body, outs, scratch=(), count=0, later=0, away=(), grant=20 << 20):
     whole = pl.BlockSpec(memory_space=pltpu.VMEM)
-    scalar = pl.BlockSpec(memory_space=pltpu.SMEM)
+    there = pl.BlockSpec(memory_space=pl.ANY)
+    hbm = pl.BlockSpec(memory_space=pltpu.HBM)
+
+    def reader(*refs):
+        body(*refs[:count], *refs[count + later :])
+
     return pl.pallas_call(
-        body,
+        reader,
         out_shape=outs,
-        in_specs=[scalar if k in smem else whole for k in range(count)],
+        in_specs=[hbm if k in away else whole for k in range(count)] + [there] * later,
         out_specs=jax.tree.map(lambda _: whole, outs),
         scratch_shapes=list(scratch),
-        cost_estimate=cost,
         compiler_params=pltpu.CompilerParams(vmem_limit_bytes=grant),
     )
 
 
-def bias_body(pair_ref, gain_ref, weight_ref, present_ref, out_ref):
-    normed = normed_rows(pair_ref[...], gain_ref[...]).astype(jnp.bfloat16)
-    bias = dot_nt(weight_ref[...], normed)
-    present = present_ref[...].astype(jnp.float32)
-    mask_row = jnp.concatenate([present[0:1], present[1:2]], axis=1)
+ROW_GAIN, COLUMN_GAIN, MEAN_GAIN, ENTRY_GAINS, MID_GAINS, PRESENCE = range(6)
+
+
+def bias_body(pair_at, gain_at, weight_at, present_at, out_ref, near_ref, pair, gain, weight, present, sems):
+    moves = [
+        pltpu.make_async_copy(there, here, sems.at[k])
+        for k, (there, here) in enumerate(
+            ((pair_at, pair), (gain_at, gain), (weight_at, weight), (present_at, present))
+        )
+    ]
+    for move in moves:
+        move.start()
+    for move in moves:
+        move.wait()
+    near_ref[0] = pair[...].astype(jnp.bfloat16)
+    normed = normed_rows(pair[...], gain[...]).astype(jnp.bfloat16)
+    bias = dot_nt(weight[...], normed)
+    here = present[...].astype(jnp.float32)
+    mask_row = jnp.concatenate([here[0:1], here[1:2]], axis=1)
     fill = jnp.zeros((out_ref.shape[1] - bias.shape[0] - 1, bias.shape[1]), jnp.float32)
     block = jnp.concatenate([bias, mask_row, fill], axis=0).astype(jnp.bfloat16)
     out_ref[...] = jnp.broadcast_to(block[None], out_ref.shape)
@@ -329,9 +348,9 @@
     return jnp.concatenate([ref[part, rows, :] for part in range(ref.shape[0])], axis=1)
 
 
-def project_body(x_ref, gain_ref, ask_ref, look_ref, q_ref, k_ref, v_ref, g_ref):
+def project_body(x_ref, small_ref, ask_ref, look_ref, q_ref, k_ref, v_ref, g_ref):
     width = ask_ref.shape[1]
-    normed = normed_rows(x_ref[...], gain_ref[...]).astype(jnp.bfloat16)
+    normed = normed_rows(x_ref[...], small_ref[ROW_GAIN : ROW_GAIN + 1]).astype(jnp.bfloat16)
     scaling = 1.0 / math.sqrt(PER_FOCUS_WIDTH)
     q = (dot_nn(normed, ask_ref[...]) * scaling).astype(jnp.bfloat16).astype(jnp.float32)
     put_parts(q_ref, q)
@@ -362,14 +381,15 @@
     return total
 
 
-def row_body(blk_ref, x_ref, q_ref, k_ref, v_ref, g_ref, final_ref, present_ref, out_ref, wide, send, x_parts):
+def row_body(blk_ref, x_ref, q_ref, k_ref, v_ref, g_ref, final_ref, out_ref, wide, send, x_parts):
     devices = blk_ref.shape[0]
     put_parts(x_parts, x_ref[...])
     per_block = blk_ref.shape[1]
     half = wide.shape[1] // 2
     per_seq = 2 * devices
     wide[...] = blk_ref[...].astype(jnp.float32).reshape(wide.shape)
-    penalty = MASK_PENALTY_SCALE * (present_ref[...].astype(jnp.float32) - 1.0)
+    mine = wide[pl.ds(lax.axis_index("dap") * per_block + FOCUS_NUMBER, 1), :]
+    penalty = MASK_PENALTY_SCALE * (mine - 1.0)
     heads = [wide[pl.ds(h, devices, stride=per_block), :] for h in range(FOCUS_NUMBER)]
     for s in range(2):
         keys = k_ref[s * per_seq : (s + 1) * per_seq, :]
@@ -377,7 +397,7 @@
         for r in range(2):
             rows = pl.ds(s * per_seq + r, devices, stride=2)
             bias = jnp.concatenate([b[:, r * half : (r + 1) * half] for b in heads], axis=0)
-            mixed = attend_heads(rows_of(q_ref, rows), keys, values, bias + penalty[s : s + 1])
+            mixed = attend_heads(rows_of(q_ref, rows), keys, values, bias + penalty[:, s * half : (s + 1) * half])
             y = (mixed * rows_of(g_ref, rows)).astype(jnp.bfloat16)
             updated = rows_of(x_parts, rows) + dot_nn(y, final_ref[...])
             for part in range(updated.shape[1] // (2 * half)):
@@ -393,7 +413,7 @@
 
 
 def column_body(
-    arrived_ref, blk_ref, gain_ref, ask_ref, look_ref, final_ref, gain_out_ref, map_ref,
+    arrived_ref, blk_ref, small_ref, ask_ref, look_ref, final_ref, map_ref,
     msa_ref, opm_ref, wide, wide_blk, x_all, msa,
 ):
     devices = arrived_ref.shape[0]
@@ -421,7 +441,7 @@
         for r in range(2)
     ]
     x = x_all[...]
-    normed = normed_rows(x, gain_ref[...]).astype(jnp.bfloat16)
+    normed = normed_rows(x, small_ref[COLUMN_GAIN : COLUMN_GAIN + 1]).astype(jnp.bfloat16)
     scaling = 1.0 / math.sqrt(PER_FOCUS_WIDTH)
     q = (dot_nn(normed, ask_ref[...]) * scaling).astype(jnp.bfloat16).astype(jnp.float32)
     others = dot_nn(normed, look_ref[...])
@@ -450,7 +470,7 @@
                 ]
     for part in range(4):
         msa_ref[:, part * lanes : (part + 1) * lanes] = msa[part]
-    normed = normed_rows(updated, gain_out_ref[...]).astype(jnp.bfloat16)
+    normed = normed_rows(updated, small_ref[MEAN_GAIN : MEAN_GAIN + 1]).astype(jnp.bfloat16)
     sides = [
         dot_nt(map_ref[...], normed[r * seqs : (r + 1) * seqs]) * present[r] for r in range(2)
     ]
@@ -468,33 +488,25 @@
     return dot_nn(diagonal, jnp.ones((half, lanes), jnp.bfloat16))
 
 
-def gathered_at(chip, my_chip, chips):
-    apart = chip ^ my_chip
-    stages = chips.bit_length() - 1
-    place = jnp.int32(0)
-    for k in range(stages):
-        place = place | (((apart >> (stages - 1 - k)) & 1) << k)
-    return place
-
-
-def opm_body(
-    own_ref, oth_ref, blk_ref, near_ref, far_ref, fin_ref, amino_ref, amino_row_ref, gain_ref,
-    flank_ref, switch_ref,
-    pair_one_ref, left_ref, gate_ref, right_ref,
-    order, order16, outer, counts, mkeys, wide_blk,
-):
-    chips, both, lanes = own_ref.shape
-    hidden = both // 2
+def opm_body(steps, own_ref, oth_ref, *refs):
+    couples, refs = refs[:steps], refs[steps:]
+    (
+        blk_ref, fin_ref, small_ref, flank_ref, switch_ref,
+        pair_one_ref, left_ref, gate_ref, right_ref,
+        order, order16, outer, counts, mkeys, wide_blk,
+    ) = refs
+    chips, lanes, channels = pair_one_ref.shape
+    hidden = outer.shape[2]
     half = lanes // 2
-    channels = switch_ref.shape[0]
     me = lax.axis_index("dap")
     parity = lax.rem(me, 2)
     my_chip = me // 2
-    own = own_ref[:, hidden:, :].astype(jnp.float32)
-    oth = oth_ref[:, hidden:, :].astype(jnp.float32)
-    flag = jnp.broadcast_to(parity, (1, 1, 1)) == 0
-    order16[0] = jnp.where(flag, own, oth).reshape(order16.shape[1:])
-    order16[1] = jnp.where(flag, oth, own).reshape(order16.shape[1:])
+    for k in range(steps):
+        for h in range(chips // steps):
+            pair_one_ref[my_chip ^ (h * steps + k)] = couples[k][h].astype(jnp.float32)
+    rows = (chips * hidden, lanes)
+    order16[parity] = own_ref[:, hidden:, :].astype(jnp.float32).reshape(rows)
+    order16[1 - parity] = oth_ref[:, hidden:, :].astype(jnp.float32).reshape(rows)
     for b in range(hidden):
         for p in range(2):
             rows = order16[p, pl.ds(b, chips, stride=hidden), :]
@@ -512,12 +524,11 @@
         part = mask_rows[:, s * half : (s + 1) * half]
         total = total + dot_tn(part, jnp.concatenate([part, part], axis=1))
     counts[...] = 1.0 / jnp.maximum(total, 1.0)
-    mkeys[...] = presence_down(amino_row_ref[...], half, lanes)
-    gain = gain_ref[...]
+    mkeys[...] = presence_down(small_ref[PRESENCE : PRESENCE + 1, :half], half, lanes)
+    gain = small_ref[ENTRY_GAINS : ENTRY_GAINS + 1, :channels]
     low = lane_iota((channels, lanes)) < half
     low_row = lane_iota((1, lanes)) < half
     group = 4
-    near = near_ref.shape[0]
 
     @pl.loop(0, chips // group)
     def _(block):
@@ -538,23 +549,16 @@
             turned = jnp.where(low, a0, b1) + pltpu.roll(jnp.where(low, a1, b0), half, 1)
             i0 = 4 * chip + 2 * parity
             share = jnp.where(low_row, counts[pl.ds(i0, 1), :], counts[pl.ds(i0 + 1, 1), :])
-            place = gathered_at(chip, my_chip, chips)
-            at = lax.rem(place, near)
-            couple = jnp.where(
-                jnp.broadcast_to(place, (1, 1)) < near,
-                near_ref[at].astype(jnp.float32),
-                far_ref[at].astype(jnp.float32),
-            )
-            pairs.append(jnp.transpose(turned * share) + couple)
+            pairs.append(jnp.transpose(turned * share) + pair_one_ref[chip])
             for r in range(2):
-                keeps.append(mkeys[...] * amino_ref[i0 + r].astype(jnp.float32))
+                keeps.append(mkeys[...] * mkeys[pl.ds(i0 + r, 1), :])
         pair = jnp.concatenate(pairs, axis=0)
         keep = jnp.concatenate(keeps, axis=0)
         normed = normed_rows(pair, gain).astype(jnp.bfloat16)
-        projected = dot_nn(normed, flank_ref[...])
+        projected = dot_nn(normed, flank_ref[0])
         left = gated(projected, 0, channels, channels) * keep
         right = gated(projected, 2 * channels, 3 * channels, channels) * keep
-        gate = jax.nn.sigmoid(dot_nn(normed, switch_ref[...]))
+        gate = jax.nn.sigmoid(dot_nn(normed, switch_ref[0]))
         for c in range(group):
             chip = block * group + c
             rows = slice(c * lanes, (c + 1) * lanes)
@@ -565,8 +569,7 @@
 
 
 def outgoing_body(
-    pair_one_ref, left_ref, gate_ref, own_ref, oth_ref, amino_ref, amino_row_ref, gain_mid_ref,
-    final_ref, gain_ref, flank_ref,
+    pair_one_ref, left_ref, gate_ref, own_ref, oth_ref, small_ref, final_ref, flank_ref,
     two_ref, send_ref,
     sides, prods, mkeys, pair_two, rows_out, cols,
 ):
@@ -607,12 +610,13 @@
             to = pl.ds(pl.multiple_of((octet * per_step + c) * chips, chips), chips)
             prods[to, :] = results[c].astype(jnp.bfloat16).astype(jnp.float32)
 
-    mkeys[...] = presence_down(amino_row_ref[...], half, channels)
-    gain_mid = jnp.transpose(jnp.broadcast_to(gain_mid_ref[...], (channels, channels)))
-    final_t = jnp.transpose(final_ref[...].astype(jnp.float32)).astype(jnp.bfloat16)
-    gain = gain_ref[...]
-    flank_right = flank_ref[:, 2 * channels :]
-    flank_left = flank_ref[:, : 2 * channels]
+    mkeys[...] = presence_down(small_ref[PRESENCE : PRESENCE + 1, :half], half, channels)
+    gain_mid = small_ref[MID_GAINS : MID_GAINS + 1, :channels]
+    gain_mid = jnp.transpose(jnp.broadcast_to(gain_mid, (channels, channels)))
+    final_t = jnp.transpose(final_ref[0].astype(jnp.float32)).astype(jnp.bfloat16)
+    gain = small_ref[ENTRY_GAINS : ENTRY_GAINS + 1, channels : 2 * channels]
+    flank_right = flank_ref[1, :, 2 * channels :]
+    flank_left = flank_ref[1, :, : 2 * channels]
     octet = pl.multiple_of(8 * (my_chip // 2), 8)
     group = 4
     for block in range(chips // group):
@@ -636,7 +640,7 @@
             two = pair_one_ref[chip] + rows_out[c] * gate_ref[chip]
             twos.append(two)
             for r in range(2):
-                keeps.append(amino_ref[4 * chip + 2 * parity + r].astype(jnp.float32))
+                keeps.append(mkeys[pl.ds(4 * chip + 2 * parity + r, 1), :])
         two = jnp.concatenate(twos, axis=0)
         full = normed_rows(two, gain)
         normed = full.astype(jnp.bfloat16)
@@ -658,13 +662,15 @@
 
 
 def incoming_body(
-    own_ref, oth_ref, two_ref, couple_ref, gain_ref, switch_ref, gain_mid_ref, final_ref,
-    out_ref, right, left,
+    own_ref, oth_ref, two_ref, couple_ref, small_ref, switch_ref, final_ref,
+    out_ref,
 ):
     chips, _, channels = own_ref.shape
     lanes2 = out_ref.shape[0]
     half = lanes2 // 2
     me = lax.axis_index("dap")
+    gain_mid = small_ref[MID_GAINS : MID_GAINS + 1, channels : 2 * channels]
+    gain = small_ref[ENTRY_GAINS : ENTRY_GAINS + 1, channels : 2 * channels]
     first = 4 * lax.rem(me // 2, 2) + 2 * lax.rem(me, 2)
     row = lax.broadcasted_iota(jnp.int32, (8, channels), 0)
     totals = tuple(jnp.zeros((half, channels), jnp.float32) for _ in range(2))
@@ -683,13 +689,26 @@
 
         totals = lax.fori_loop(0, chips, step, totals)
     prod = jnp.concatenate(totals, axis=0).astype(jnp.bfloat16).astype(jnp.float32)
-    changed = dot_nn(normed_rows(prod, gain_mid_ref[...]).astype(jnp.bfloat16), final_ref[...])
+    changed = dot_nn(normed_rows(prod, gain_mid).astype(jnp.bfloat16), final_ref[1])
     two = two_ref[...]
-    normed = normed_rows(two, gain_ref[...]).astype(jnp.bfloat16)
-    gate = jax.nn.sigmoid(dot_nn(normed, switch_ref[...]))
+    normed = normed_rows(two, gain).astype(jnp.bfloat16)
+    gate = jax.nn.sigmoid(dot_nn(normed, switch_ref[1]))
     couple = couple_ref[...]
     lost = couple - couple.astype(jnp.bfloat16).astype(jnp.float32)
     out_ref[...] = two + lost + changed * gate
+
+
+def gather_by_steps(block, chips):
+    bits = chips.bit_length() - 1
+    steps = 1 << (bits // 2)
+    devices = 2 * chips
+
+    def fetch(value, apart):
+        return lax.ppermute(value, "dap", [(d, d ^ (2 * apart)) for d in range(devices)])
+
+    parts = [fetch(block, h * steps) for h in range(1, chips // steps)]
+    near = jnp.concatenate([block] + parts, axis=0)
+    return near, [fetch(near, k) for k in range(1, steps)]
 
 
 def paired_shards(
@@ -721,6 +740,7 @@
     strands, aminos, features = homolog_stack.shape
     rows, _, channels = couple_tensor.shape
     lanes = rows * aminos
+    heads = FOCUS_NUMBER
     hidden = TENSOR_HIDDEN
     f32, bf16 = jnp.float32, jnp.bfloat16
     shape = jax.ShapeDtypeStruct
@@ -732,10 +752,36 @@
 
     couple = couple_tensor.reshape(lanes, channels)
     x = homolog_stack.reshape(strands * aminos, features)
-    block = vmem_call(
-        bias_body, shape((devices, 16, lanes), bf16), count=4
+    block, near = vmem_call(
+        bias_body,
+        (shape((devices, 16, lanes), bf16), shape((1, lanes, channels), bf16)),
+        scratch=[
+            pltpu.VMEM((lanes, channels), f32),
+            pltpu.VMEM((1, channels), f32),
+            pltpu.VMEM((heads, channels), bf16),
+            pltpu.VMEM((strands, aminos), jnp.int32),
+            pltpu.SemaphoreType.DMA((4,)),
+        ],
+        count=4,
+        away=range(4),
+        grant=60 << 20,
     )(couple, line(couple_offset_factor), couple_offset_matrix.T, homolog_presence)
     blocks = lax.all_to_all(block, "dap", split_axis=0, concat_axis=0, tiled=True)
+    small = jnp.concatenate(
+        [
+            line(horizontal_standard_factor),
+            line(vertical_standard_factor),
+            line(tensor_average_factor),
+            line(trio_entry_factors),
+            line(trio_multiplied_factors),
+            jnp.pad(line(amino_presence.astype(f32)), ((0, 0), (0, features - aminos))),
+            jnp.zeros((2, features), f32),
+        ],
+        axis=0,
+    )
+    final = jnp.transpose(
+        tensor_average_final.reshape(hidden, hidden // 2, 2, channels), (2, 3, 1, 0)
+    ).reshape(2 * channels, hidden * hidden // 2)
     q, k, v, g = vmem_call(
         project_body,
         (
@@ -745,14 +791,9 @@
             shape((features // lanes, lanes, lanes), f32),
         ),
         count=4,
-    )(x, line(horizontal_standard_factor), horizontal_asking_matrix, horizontal_lookup_triple)
-    near = couple.astype(bf16)[None]
-    stages = chips.bit_length() - 1
-    for stage in range(stages):
-        reach = devices >> (stage + 1)
-        far = lax.ppermute(near, "dap", [(d, d ^ reach) for d in range(devices)])
-        if stage < stages - 1:
-            near = jnp.concatenate([near, far], axis=0)
+    )(x, small, horizontal_asking_matrix, horizontal_lookup_triple)
+    near, fars = gather_by_steps(near, chips)
+    couples = [near, *fars]
     sent = vmem_call(
         row_body,
         shape((devices, 8, lanes), bf16),
@@ -761,8 +802,8 @@
             pltpu.VMEM((devices * 8, lanes), f32),
             pltpu.VMEM((features // lanes, lanes, lanes), f32),
         ],
-        count=8,
-    )(blocks, x, q, k, v, g, horizontal_final_matrix, homolog_presence)
+        count=7,
+    )(blocks, x, q, k, v, g, horizontal_final_matrix)
     arrived = lax.all_to_all(sent, "dap", split_axis=0, concat_axis=0, tiled=True)
     msa, opm = vmem_call(
         column_body,
@@ -773,28 +814,25 @@
             pltpu.VMEM((lanes, features), f32),
             pltpu.VMEM((4, devices * strands, lanes), f32),
         ],
-        count=8,
+        count=7,
+        later=1,
     )(
         arrived,
         blocks,
-        line(vertical_standard_factor),
+        small,
         vertical_asking_matrix,
         vertical_lookup_triple,
         vertical_final_matrix,
-        line(tensor_average_factor),
         tensor_average_mapping.T,
+        final,
     )
     opm_own = lax.all_to_all(
         opm, "dap", split_axis=0, concat_axis=0, tiled=True, axis_index_groups=same_parity
     )
     opm_oth = lax.ppermute(opm_own, "dap", swap)
-    final = jnp.transpose(
-        tensor_average_final.reshape(hidden, hidden // 2, 2, channels), (2, 3, 1, 0)
-    ).reshape(2 * channels, hidden * hidden // 2)
     stack = (chips, lanes, channels)
-    amino_row = line(amino_presence)
     pair_one, left, gate, right_own = vmem_call(
-        opm_body,
+        functools.partial(opm_body, len(couples)),
         (shape(stack, f32), shape(stack, f32), shape(stack, f32), shape(stack, bf16)),
         scratch=[
             pltpu.VMEM((hidden * aminos, lanes), f32),
@@ -804,20 +842,16 @@
             pltpu.VMEM((aminos, channels), f32),
             pltpu.VMEM((devices * 16, lanes), f32),
         ],
-        smem=(6,),
-        count=11,
+        count=len(couples) + 7,
     )(
         opm_own,
         opm_oth,
+        *couples,
         blocks,
-        near,
-        far,
         final,
-        amino_presence,
-        amino_row,
-        line(trio_entry_factors[0]),
-        trio_flank_mappings[0],
-        trio_final_switches[0],
+        small,
+        trio_flank_mappings,
+        trio_final_switches,
     )
     right_oth = lax.ppermute(right_own, "dap", swap)
     two, going = vmem_call(
@@ -831,37 +865,21 @@
             pltpu.VMEM((4, lanes, channels), f32),
             pltpu.VMEM((4 * lanes, channels), f32),
         ],
-        smem=(5,),
-        count=11,
+        count=8,
     )(
         pair_one,
         left.reshape(chips * channels, lanes),
         gate,
         right_own,
         right_oth,
-        amino_presence,
-        amino_row,
-        line(trio_multiplied_factors[0]),
-        trio_final_matrices[0],
-        line(trio_entry_factors[1]),
-        trio_flank_mappings[1],
+        small,
+        trio_final_matrices,
+        trio_flank_mappings,
     )
     coming = lax.ppermute(going, "dap", swap)
     pair_out = vmem_call(
-        incoming_body,
-        shape((lanes, channels), f32),
-        scratch=[pltpu.VMEM((8, channels), f32), pltpu.VMEM((8, channels), f32)],
-        count=8,
-    )(
-        going,
-        coming,
-        two,
-        couple,
-        line(trio_entry_factors[1]),
-        trio_final_switches[1],
-        line(trio_multiplied_factors[1]),
-        trio_final_matrices[1],
-    )
+        incoming_body, shape((lanes, channels), f32), count=7
+    )(going, coming, two, couple, small, trio_final_switches, trio_final_matrices)
     return (
         msa.reshape(devices * strands, rows, features),
         pair_out.reshape(rows, aminos, channels),

time: 74.7 us -> 77.3 us (1.035)
  waiting for transfers between devices: 22.4 us -> 29.4 us
  local copies, waits for them, and re-layouts: 7.13 us -> 2.97 us
    unnamed x47 -> x44, local copies, waits for them, and re-layouts: 5.98 us -> 1.82 us
    all_to_all x1, waiting for transfers between devices: 1.19 us -> 3.86 us  [paired_shards(): lax.all_to_all(opm, 'dap', split_axis=0, concat_axis=0, tiled=True, axis_...]
    all_to_all x1, waiting for transfers between devices: 3.51 us -> 6 us  [paired_shards(): lax.all_to_all(block, 'dap', split_axis=0, concat_axis=0, tiled=True)]
    all_to_all x1, waiting for transfers between devices: 5.85 us -> 6.91 us  [paired_shards(): lax.all_to_all(sent, 'dap', split_axis=0, concat_axis=0, tiled=True)]
    ppermute x4 -> x6, waiting for transfers between devices: 9.41 us -> 9.57 us  [fetch(): lax.ppermute(value, 'dap', [(d, d ^ 2 * apart) for d in range(devices)])]
    ppermute x4 -> x6, starting transfers between devices: 8.1 us -> 8.01 us  [fetch(): lax.ppermute(value, 'dap', [(d, d ^ 2 * apart) for d in range(devices)])]
  transfers between devices with their start and end apart: 10 -> 12, of which waited for: 7 -> 10; matrix products, arithmetic and copies ran while one was open for 2% -> 2% of each run, Pallas kernels for 7% -> 0%
where the time goes in v3:
time: 77.3 us; the launch traced here: 76.9 us
  waiting for transfers between devices  29.4 us (38%)
  Pallas kernels  21.8 us (28%)
  starting transfers between devices  21.8 us (28%)
  local copies, waits for them, and re-layouts  2.97 us (4%)
  between operations  0.92 us (1%)
    ppermute x6, waiting for transfers between devices, fetch(): lax.ppermute(value, 'dap', [(d, d ^ 2 * apart) for d in range(devices)])  9.57 us
    ppermute x6, starting transfers between devices, fetch(): lax.ppermute(value, 'dap', [(d, d ^ 2 * apart) for d in range(devices)])  8.01 us
    pallas_call x1, Pallas kernels, paired_shards(): vmem_call(functools.partial(opm_body, len(couples)), (shape(stack, f32),...  7.48 us
    all_to_all x1, starting transfers between devices, paired_shards(): lax.all_to_all(block, 'dap', split_axis=0, concat_axis=0, tiled=True)  7.33 us
    all_to_all x1, waiting for transfers between devices, paired_shards(): lax.all_to_all(sent, 'dap', split_axis=0, concat_axis=0, tiled=True)  6.91 us
    all_to_all x1, waiting for transfers between devices, paired_shards(): lax.all_to_all(block, 'dap', split_axis=0, concat_axis=0, tiled=True)  6 us
    pallas_call x1, Pallas kernels, paired_shards(): vmem_call(outgoing_body, (shape((lanes, channels), f32), shape((chips, la...  5.7 us
    all_to_all x1, waiting for transfers between devices, paired_shards(): lax.all_to_all(opm, 'dap', split_axis=0, concat_axis=0, tiled=True, axis_...  3.86 us
  transfers between devices with their start and end apart: 12, of which 10 were waited for; matrix products, arithmetic and copies ran while one was open for 2% of the time, Pallas kernels for 0%

profile of v3, /device:TPU:0, one launch (start us, length us, event | category | flops | bytes accessed | tf_op | source)
XLA Modules:
  0.0 76.9 jit_solution(18407412516325133984)
XLA Ops:
  0.6 1.9 %shard_map.221 = (bf16[32,16,128]{2,1,0:T(8,128)(2,1)}, bf16[1,128,128]{2,1,0:T(8,128)(2,1)}) custom-call(f32[128,128]{1,0:T(8,128)} %bitcast.26, f32[1,128]{1,0:T(1,128)} %bitcast.39, bf16[8,128]{1,0:T(8,128)(2,1)} %bitcast.33, s32[2,64]{1,0:T(2,128)} %refs_3_.3), custom_call_target="tpu_custom_call" | custom-call | tf_op jit(solution)/shard_map/pallas_call | solution.py:755
  2.5 0.0 copy-start.1
  2.5 0.0 copy-start.9
  2.5 7.3 %all-to-all-start = ((bf16[32,16,128]{2,1,0:T(8,128)(2,1)}), bf16[32,16,128]{2,1,0:T(8,128)(2,1)S(1)}, u32[]{:S(2)}, u32[]{:S(2)}) async-start(bf16[32,16,128]{2,1,0:T(8,128)(2,1)} %get-tuple-element.16), calls=%async_computation | async-start | bytes 262144 | tf_op jit(solution)/shard_map/all_to_all | solution.py:769
  9.9 0.0 copy-start.16
  9.9 0.0 copy-start.17
  9.9 0.0 copy-start.18
  9.9 0.0 copy-start.14
  10.0 0.0 copy-start.15
  10.0 0.6 copy-done.16
  10.6 0.0 copy-done.17
  10.6 0.0 copy-done.18
  10.6 0.0 copy-done.14
  10.6 0.0 copy-done.15
  10.7 0.0 copy-start.2
  10.7 1.0 %copy-done.2 = bf16[256,768]{1,0:T(8,128)(2,1)S(1)} copy-done((bf16[256,768]{1,0:T(8,128)(2,1)S(1)}, bf16[256,768]{1,0:T(8,128)(2,1)}, u32[]{:S(2)}) %copy-start.2) | copy-done | bytes 393240
  11.7 0.4 shard_map.222
  12.1 6.0 %all-to-all-done.refs_0_.refs_1_.refs_6_ = bf16[32,16,128]{2,1,0:T(8,128)(2,1)S(1)} async-done(((bf16[32,16,128]{2,1,0:T(8,128)(2,1)}), bf16[32,16,128]{2,1,0:T(8,128)(2,1)S(1)}, u32[]{:S(2)}, u32[]{:S(2)}) %all-to-all-start) | async-done | bytes 131104 | tf_op jit(solution)/shard_map/all_to_all | solution.py:769
  18.1 2.3 %shard_map.223 = bf16[32,8,128]{2,1,0:T(8,128)(2,1)} custom-call(bf16[32,16,128]{2,1,0:T(8,128)(2,1)S(1)} %all-to-all-done.refs_0_.refs_1_.refs_6_, f32[128,256]{1,0:T(8,128)S(1)} %bitcast.25, f32[2,128,128]{2,1,0:T(8,128)S(1)} %get-tuple-element.17.refs_2_, bf16[128,256]{1,0:T(8,128)(2,1)S(1)} %get-tuple-element.18.refs_3_, ...), custom_call_target="tpu_custom_call" | custom-call | tf_op jit(solution)/shard_map/pallas_call | solution.py:797
  20.4 2.6 %all-to-all-start.1 = ((bf16[32,8,128]{2,1,0:T(8,128)(2,1)}), bf16[32,8,128]{2,1,0:T(8,128)(2,1)S(1)}, u32[]{:S(2)}, u32[]{:S(2)}) async-start(bf16[32,8,128]{2,1,0:T(8,128)(2,1)} %shard_map.223), calls=%async_computation.1 | async-start | bytes 131072 | tf_op jit(solution)/shard_map/all_to_all | solution.py:807
  23.0 0.2 copy.25
  23.2 0.0 copy-start.8
  23.3 0.0 copy-start.3
  23.3 0.0 copy-start.7
  23.3 0.1 copy.26.refs_7_
  23.5 6.9 %all-to-all-done.1.refs_0_ = bf16[32,8,128]{2,1,0:T(8,128)(2,1)S(1)} async-done(((bf16[32,8,128]{2,1,0:T(8,128)(2,1)}), bf16[32,8,128]{2,1,0:T(8,128)(2,1)S(1)}, u32[]{:S(2)}, u32[]{:S(2)}) %all-to-all-start.1) | async-done | bytes 65568 | tf_op jit(solution)/shard_map/all_to_all | solution.py:807
  30.4 2.4 %shard_map.224 = (f32[64,512]{1,0:T(8,128)S(1)}, bf16[16,64,128]{2,1,0:T(8,128)(2,1)}) custom-call(bf16[32,8,128]{2,1,0:T(8,128)(2,1)S(1)} %all-to-all-done.1.refs_0_, bf16[32,16,128]{2,1,0:T(8,128)(2,1)S(1)} %all-to-all-done.refs_0_.refs_1_.refs_6_, f32[8,256]{1,0:T(8,128)S(1)} %concatenate.6.refs_1_.refs_2_.refs_8_.refs_5_.refs_4_, ...), custom_call_target="tpu_custom_call" | custom-call | tf_op jit(solution)/shard_map/pallas_call | solution.py:808
  32.8 3.7 %all-to-all-start.2 = ((bf16[16,64,128]{2,1,0:T(8,128)(2,1)}), bf16[16,64,128]{2,1,0:T(8,128)(2,1)S(1)}, u32[]{:S(2)}, u32[]{:S(2)}) async-start(bf16[16,64,128]{2,1,0:T(8,128)(2,1)} %get-tuple-element.22), calls=%async_computation.2 | async-start | bytes 524288 | tf_op jit(solution)/shard_map/all_to_all | solution.py:829
  36.5 0.0 copy-start
  36.5 3.7 %collective-permute-start.3 = (bf16[1,128,128]{2,1,0:T(8,128)(2,1)S(1)}, bf16[1,128,128]{2,1,0:T(8,128)(2,1)S(1)}, u32[]{:S(2)}, u32[]{:S(2)}) collective-permute-start(bf16[1,128,128]{2,1,0:T(8,128)(2,1)S(1)} %copy-done.13), channel_id=1, source_target_pairs={{0,24},{1,25},{2,26},{3,27},{4,28},{5,29},{6,30},{7,31},{8,16},{9,... | collective-permute-start | bytes 98312 | tf_op jit(solution)/shard_map/ppermute | solution.py:707
  40.2 0.7 collective-permute-start.1
  40.9 3.3 %collective-permute-done.1 = bf16[1,128,128]{2,1,0:T(8,128)(2,1)S(1)} collective-permute-done((bf16[1,128,128]{2,1,0:T(8,128)(2,1)S(1)}, bf16[1,128,128]{2,1,0:T(8,128)(2,1)S(1)}, u32[]{:S(2)}, u32[]{:S(2)}) %collective-permute-start.1) | collective-permute-done | bytes 32800 | tf_op jit(solution)/shard_map/ppermute | solution.py:707
  44.3 3.9 %all-to-all-done.2.refs_0_ = bf16[16,64,128]{2,1,0:T(8,128)(2,1)S(1)} async-done(((bf16[16,64,128]{2,1,0:T(8,128)(2,1)}), bf16[16,64,128]{2,1,0:T(8,128)(2,1)S(1)}, u32[]{:S(2)}, u32[]{:S(2)}) %all-to-all-start.2) | async-done | bytes 262176 | tf_op jit(solution)/shard_map/all_to_all | solution.py:829
  48.2 0.4 collective-permute-done.2
  48.6 2.4 %collective-permute-start.6 = (bf16[4,128,128]{2,1,0:T(8,128)(2,1)S(1)}, bf16[4,128,128]{2,1,0:T(8,128)(2,1)S(1)}, u32[]{:S(2)}, u32[]{:S(2)}) collective-permute-start(bf16[4,128,128]{2,1,0:T(8,128)(2,1)S(1)} %constant_dynamic-update-slice_fusion.refs_2_), channel_id=1, source_target_pairs={{0,6},{1,7},{2,4},{3,5},{4,2},{5,3},{6,0},{7,1},{8,14},{9,15},{10,... | collective-permute-start | bytes 393224 | tf_op jit(solution)/shard_map/ppermute | solution.py:707
  51.0 0.6 collective-permute-start.5
  51.6 0.6 collective-permute-start.4
  52.1 3.8 %collective-permute-done.6.refs_5_ = bf16[4,128,128]{2,1,0:T(8,128)(2,1)S(1)} collective-permute-done((bf16[4,128,128]{2,1,0:T(8,128)(2,1)S(1)}, bf16[4,128,128]{2,1,0:T(8,128)(2,1)S(1)}, u32[]{:S(2)}, u32[]{:S(2)}) %collective-permute-start.6) | collective-permute-done | bytes 131104 | tf_op jit(solution)/shard_map/ppermute | solution.py:707
  55.9 2.0 %collective-permute-done.5.refs_4_ = bf16[4,128,128]{2,1,0:T(8,128)(2,1)S(1)} collective-permute-done((bf16[4,128,128]{2,1,0:T(8,128)(2,1)S(1)}, bf16[4,128,128]{2,1,0:T(8,128)(2,1)S(1)}, u32[]{:S(2)}, u32[]{:S(2)}) %collective-permute-start.5) | collective-permute-done | bytes 131104 | tf_op jit(solution)/shard_map/ppermute | solution.py:707
  57.9 0.1 collective-permute-done.4.refs_3_
  58.0 7.5 %shard_map.225 = (f32[16,128,128]{2,1,0:T(8,128)S(1)}, f32[16,128,128]{2,1,0:T(8,128)S(1)}, f32[16,128,128]{2,1,0:T(8,128)S(1)}, bf16[16,128,128]{2,1,0:T(8,128)(2,1)S(1)}) custom-call(bf16[16,64,128]{2,1,0:T(8,128)(2,1)S(1)} %all-to-all-done.2.refs_0_, bf16[16,64,128]{2,1,0:T(8,128)(2,1)S(1)} %collective-permute-done.refs_1_, ...), custom_call_target="tpu_custom_call" | custom-call | tf_op jit(solution)/shard_map/pallas_call | solution.py:834
  65.5 0.1 collective-permute-start.7
  65.5 1.9 %collective-permute-done.7.refs_4_ = bf16[16,128,128]{2,1,0:T(8,128)(2,1)S(1)} collective-permute-done((bf16[16,128,128]{2,1,0:T(8,128)(2,1)S(1)}, bf16[16,128,128]{2,1,0:T(8,128)(2,1)S(1)}, u32[]{:S(2)}, u32[]{:S(2)}) %collective-permute-start.7) | collective-permute-done | bytes 524320 | tf_op jit(solution)/shard_map/ppermute | solution.py:856
  67.4 5.7 %shard_map.226 = (f32[128,128]{1,0:T(8,128)S(1)}, bf16[16,144,128]{2,1,0:T(8,128)(2,1)S(1)}) custom-call(f32[16,128,128]{2,1,0:T(8,128)S(1)} %get-tuple-element.24.refs_0_, f32[2048,128]{1,0:T(8,128)S(1)} %bitcast.23, f32[16,128,128]{2,1,0:T(8,128)S(1)} %get-tuple-element.26.refs_2_, bf16[16,128,128]{2,1,0:T(8,128)(2,1)S(1)} %get-tuple-element.27.refs_3_, ...), custom_call_target="tpu_custom_call" | custom-call | tf_op jit(solution)/shard_map/pallas_call | solution.py:857
  73.2 0.2 collective-permute-start.8
  73.4 0.7 reshape.57
  74.1 1.1 %collective-permute-done.8.refs_1_ = bf16[16,144,128]{2,1,0:T(8,128)(2,1)S(1)} collective-permute-done((bf16[16,144,128]{2,1,0:T(8,128)(2,1)S(1)}, bf16[16,144,128]{2,1,0:T(8,128)(2,1)S(1)}, u32[]{:S(2)}, u32[]{:S(2)}) %collective-permute-start.8) | collective-permute-done | bytes 589856 | tf_op jit(solution)/shard_map/ppermute | solution.py:879
  75.2 1.6 %shard_map.227 = f32[128,128]{1,0:T(8,128)} custom-call(bf16[16,144,128]{2,1,0:T(8,128)(2,1)S(1)} %get-tuple-element.28.refs_0_, bf16[16,144,128]{2,1,0:T(8,128)(2,1)S(1)} %collective-permute-done.8.refs_1_, f32[128,128]{1,0:T(8,128)S(1)} %get-tuple-element.29.refs_2_, f32[128,128]{1,0:T(8,128)S(1)} %bitcast.27, ...), custom_call_target="tpu_custom_call" | custom-call | tf_op jit(solution)/shard_map/pallas_call | solution.py:880
  (35 shorter events, 0.2 us)
Async XLA Ops:
  0.6 9.2 %copy-start.19 = (s32[64]{0:T(128)S(1)}, s32[64]{0:T(128)}, u32[]{:S(2)}) copy-start(s32[64]{0:T(128)} %param.25) | copy-start | bytes 772
  2.5 8.2 %copy-start.1 = (f32[2,64,256]{2,1,0:T(8,128)S(1)}, f32[2,64,256]{2,1,0:T(8,128)}, u32[]{:S(2)}) copy-start(f32[2,64,256]{2,1,0:T(8,128)} %param.22) | copy-start | bytes 393220
  2.5 8.2 %copy-start.9 = (bf16[256,256]{1,0:T(8,128)(2,1)S(1)}, bf16[256,256]{1,0:T(8,128)(2,1)}, u32[]{:S(2)}) copy-start(bf16[256,256]{1,0:T(8,128)(2,1)} %refs_2_.1) | copy-start | bytes 393220
  2.5 15.5 %all-to-all-start = ((bf16[32,16,128]{2,1,0:T(8,128)(2,1)}), bf16[32,16,128]{2,1,0:T(8,128)(2,1)S(1)}, u32[]{:S(2)}, u32[]{:S(2)}) async-start(bf16[32,16,128]{2,1,0:T(8,128)(2,1)} %get-tuple-element.16), calls=%async_computation | async-start | bytes 262144 | tf_op jit(solution)/shard_map/all_to_all | solution.py:769
  9.9 0.7 copy-start.16
  9.9 0.7 copy-start.17
  9.9 0.7 copy-start.18
  9.9 0.7 copy-start.14
  10.0 0.7 copy-start.15
  10.7 1.0 %copy-start.2 = (bf16[256,768]{1,0:T(8,128)(2,1)S(1)}, bf16[256,768]{1,0:T(8,128)(2,1)}, u32[]{:S(2)}) copy-start(bf16[256,768]{1,0:T(8,128)(2,1)} %refs_3_.4) | copy-start | bytes 1179652
  11.7 6.4 %copy-start.10 = (bf16[256,256]{1,0:T(8,128)(2,1)S(1)}, bf16[256,256]{1,0:T(8,128)(2,1)}, u32[]{:S(2)}) copy-start(bf16[256,256]{1,0:T(8,128)(2,1)} %refs_6_.3) | copy-start | bytes 393220
  18.1 4.9 %copy-start.12 = (bf16[1024,128]{1,0:T(8,128)(2,1)S(1)}, bf16[1024,128]{1,0:T(8,128)(2,1)}, u32[]{:S(2)}) copy-start(bf16[1024,128]{1,0:T(8,128)(2,1)} %param.38) | copy-start | bytes 786436
  20.4 10.0 %all-to-all-start.1 = ((bf16[32,8,128]{2,1,0:T(8,128)(2,1)}), bf16[32,8,128]{2,1,0:T(8,128)(2,1)S(1)}, u32[]{:S(2)}, u32[]{:S(2)}) async-start(bf16[32,8,128]{2,1,0:T(8,128)(2,1)} %shard_map.223), calls=%async_computation.1 | async-start | bytes 131072 | tf_op jit(solution)/shard_map/all_to_all | solution.py:807
  23.2 7.2 %copy-start.8 = (bf16[256,256]{1,0:T(8,128)(2,1)S(1)}, bf16[256,256]{1,0:T(8,128)(2,1)}, u32[]{:S(2)}) copy-start(bf16[256,256]{1,0:T(8,128)(2,1)} %refs_5_.2) | copy-start | bytes 393220
  23.2 7.1 %copy-start.11 = (bf16[256,64]{0,1:T(8,128)(2,1)S(1)}, bf16[256,64]{0,1:T(8,128)(2,1)}, u32[]{:S(2)}) copy-start(bf16[256,64]{0,1:T(8,128)(2,1)} %param.37) | copy-start | bytes 98308
  23.3 7.1 %copy-start.3 = (bf16[256,768]{1,0:T(8,128)(2,1)S(1)}, bf16[256,768]{1,0:T(8,128)(2,1)}, u32[]{:S(2)}) copy-start(bf16[256,768]{1,0:T(8,128)(2,1)} %refs_4_.1) | copy-start | bytes 1179652
  23.3 7.1 %copy-start.7 = (bf16[256,256]{1,0:T(8,128)(2,1)S(1)}, bf16[256,256]{1,0:T(8,128)(2,1)}, u32[]{:S(2)}) copy-start(bf16[256,256]{1,0:T(8,128)(2,1)} %refs_3_.5) | copy-start | bytes 393220
  32.8 3.7 %copy-start.13 = (bf16[1,128,128]{2,1,0:T(8,128)(2,1)S(1)}, bf16[1,128,128]{2,1,0:T(8,128)(2,1)}, u32[]{:S(2)}) copy-start(bf16[1,128,128]{2,1,0:T(8,128)(2,1)} %get-tuple-element.23) | copy-start | bytes 98308
  32.8 25.2 %copy-start.5 = (bf16[2,128,128]{2,1,0:T(8,128)(2,1)S(1)}, bf16[2,128,128]{2,1,0:T(8,128)(2,1)}, u32[]{:S(2)}) copy-start(bf16[2,128,128]{2,1,0:T(8,128)(2,1)} %refs_5_.3) | copy-start | bytes 196612
  32.8 15.4 %all-to-all-start.2 = ((bf16[16,64,128]{2,1,0:T(8,128)(2,1)}), bf16[16,64,128]{2,1,0:T(8,128)(2,1)S(1)}, u32[]{:S(2)}, u32[]{:S(2)}) async-start(bf16[16,64,128]{2,1,0:T(8,128)(2,1)} %get-tuple-element.22), calls=%async_computation.2 | async-start | bytes 524288 | tf_op jit(solution)/shard_map/all_to_all | solution.py:829
  36.5 21.5 %copy-start = (bf16[2,128,512]{2,1,0:T(8,128)(2,1)S(1)}, bf16[2,128,512]{2,1,0:T(8,128)(2,1)}, u32[]{:S(2)}) copy-start(bf16[2,128,512]{2,1,0:T(8,128)(2,1)} %refs_7_.1) | copy-start | bytes 786436
  36.5 12.1 %collective-permute-start.3 = (bf16[1,128,128]{2,1,0:T(8,128)(2,1)S(1)}, bf16[1,128,128]{2,1,0:T(8,128)(2,1)S(1)}, u32[]{:S(2)}, u32[]{:S(2)}) collective-permute-start(bf16[1,128,128]{2,1,0:T(8,128)(2,1)S(1)} %copy-done.13), channel_id=1, source_target_pairs={{0,24},{1,25},{2,26},{3,27},{4,28},{5,29},{6,30},{7,31},{8,16},{9,... | collective-permute-start | bytes 98312 | tf_op jit(solution)/shard_map/ppermute | solution.py:707
  40.2 8.3 %collective-permute-start.2 = (bf16[1,128,128]{2,1,0:T(8,128)(2,1)S(1)}, bf16[1,128,128]{2,1,0:T(8,128)(2,1)S(1)}, u32[]{:S(2)}, u32[]{:S(2)}) collective-permute-start(bf16[1,128,128]{2,1,0:T(8,128)(2,1)S(1)} %copy-done.13), channel_id=1, source_target_pairs={{0,16},{1,17},{2,18},{3,19},{4,20},{5,21},{6,22},{7,23},{8,24},{9,... | collective-permute-start | bytes 98312 | tf_op jit(solution)/shard_map/ppermute | solution.py:707
  40.2 4.1 %collective-permute-start.1 = (bf16[1,128,128]{2,1,0:T(8,128)(2,1)S(1)}, bf16[1,128,128]{2,1,0:T(8,128)(2,1)S(1)}, u32[]{:S(2)}, u32[]{:S(2)}) collective-permute-start(bf16[1,128,128]{2,1,0:T(8,128)(2,1)S(1)} %copy-done.13), channel_id=1, source_target_pairs={{0,8},{1,9},{2,10},{3,11},{4,12},{5,13},{6,14},{7,15},{8,0},{9,1},... | collective-permute-start | bytes 98312 | tf_op jit(solution)/shard_map/ppermute | solution.py:707
  48.2 9.8 %collective-permute-start = (bf16[16,64,128]{2,1,0:T(8,128)(2,1)S(1)}, bf16[16,64,128]{2,1,0:T(8,128)(2,1)S(1)}, u32[]{:S(2)}, u32[]{:S(2)}) collective-permute-start(bf16[16,64,128]{2,1,0:T(8,128)(2,1)S(1)} %all-to-all-done.2.refs_0_), channel_id=1, source_target_pairs={{0,1},{1,0},{2,3},{3,2},{4,5},{5,4},{6,7},{7,6},{8,9},{9,8},{10,11... | collective-permute-start | bytes 786440 | tf_op jit(solution)/shard_map/ppermute | solution.py:832
  48.6 18.9 %copy-start.4 = (bf16[2,128,128]{2,1,0:T(8,128)(2,1)S(1)}, bf16[2,128,128]{2,1,0:T(8,128)(2,1)}, u32[]{:S(2)}) copy-start(bf16[2,128,128]{2,1,0:T(8,128)(2,1)} %refs_6_.5) | copy-start | bytes 196612
  48.6 7.4 %collective-permute-start.6 = (bf16[4,128,128]{2,1,0:T(8,128)(2,1)S(1)}, bf16[4,128,128]{2,1,0:T(8,128)(2,1)S(1)}, u32[]{:S(2)}, u32[]{:S(2)}) collective-permute-start(bf16[4,128,128]{2,1,0:T(8,128)(2,1)S(1)} %constant_dynamic-update-slice_fusion.refs_2_), channel_id=1, source_target_pairs={{0,6},{1,7},{2,4},{3,5},{4,2},{5,3},{6,0},{7,1},{8,14},{9,15},{10,... | collective-permute-start | bytes 393224 | tf_op jit(solution)/shard_map/ppermute | solution.py:707
  51.0 6.9 %collective-permute-start.5 = (bf16[4,128,128]{2,1,0:T(8,128)(2,1)S(1)}, bf16[4,128,128]{2,1,0:T(8,128)(2,1)S(1)}, u32[]{:S(2)}, u32[]{:S(2)}) collective-permute-start(bf16[4,128,128]{2,1,0:T(8,128)(2,1)S(1)} %constant_dynamic-update-slice_fusion.refs_2_), channel_id=1, source_target_pairs={{0,4},{1,5},{2,6},{3,7},{4,0},{5,1},{6,2},{7,3},{8,12},{9,13},{10,... | collective-permute-start | bytes 393224 | tf_op jit(solution)/shard_map/ppermute | solution.py:707
  51.6 6.4 %collective-permute-start.4 = (bf16[4,128,128]{2,1,0:T(8,128)(2,1)S(1)}, bf16[4,128,128]{2,1,0:T(8,128)(2,1)S(1)}, u32[]{:S(2)}, u32[]{:S(2)}) collective-permute-start(bf16[4,128,128]{2,1,0:T(8,128)(2,1)S(1)} %constant_dynamic-update-slice_fusion.refs_2_), channel_id=1, source_target_pairs={{0,2},{1,3},{2,0},{3,1},{4,6},{5,7},{6,4},{7,5},{8,10},{9,11},{10,... | collective-permute-start | bytes 393224 | tf_op jit(solution)/shard_map/ppermute | solution.py:707
  65.5 2.0 %collective-permute-start.7 = (bf16[16,128,128]{2,1,0:T(8,128)(2,1)S(1)}, bf16[16,128,128]{2,1,0:T(8,128)(2,1)S(1)}, u32[]{:S(2)}, u32[]{:S(2)}) collective-permute-start(bf16[16,128,128]{2,1,0:T(8,128)(2,1)S(1)} %get-tuple-element.27.refs_3_), channel_id=1, source_target_pairs={{0,1},{1,0},{2,3},{3,2},{4,5},{5,4},{6,7},{7,6},{8,9},{9,8},{10,11... | collective-permute-start | bytes 1572872 | tf_op jit(solution)/shard_map/ppermute | solution.py:856
  73.2 2.1 %collective-permute-start.8 = (bf16[16,144,128]{2,1,0:T(8,128)(2,1)S(1)}, bf16[16,144,128]{2,1,0:T(8,128)(2,1)S(1)}, u32[]{:S(2)}, u32[]{:S(2)}) collective-permute-start(bf16[16,144,128]{2,1,0:T(8,128)(2,1)S(1)} %get-tuple-element.28.refs_0_), channel_id=1, source_target_pairs={{0,1},{1,0},{2,3},{3,2},{4,5},{5,4},{6,7},{7,6},{8,9},{9,8},{10,11... | collective-permute-start | bytes 1769480 | tf_op jit(solution)/shard_map/ppermute | solution.py:879
  73.4 1.9 %copy-start.6 = (f32[2,64,128]{2,1,0:T(8,128)S(1)}, f32[2,64,128]{2,1,0:T(8,128)}, u32[]{:S(2)}) copy-start(f32[2,64,128]{2,1,0:T(8,128)} %param.23) | copy-start | bytes 196612

commit v4 on v3

--- a/solution.py
+++ b/solution.py
@@ -491,8 +491,8 @@
 def opm_body(steps, own_ref, oth_ref, *refs):
     couples, refs = refs[:steps], refs[steps:]
     (
-        blk_ref, fin_ref, small_ref, flank_ref, switch_ref,
-        pair_one_ref, left_ref, gate_ref, right_ref,
+        blk_ref, fin_ref, small_ref, flank_ref,
+        pair_one_ref, normed_ref, right_ref,
         order, order16, outer, counts, mkeys, wide_blk,
     ) = refs
     chips, lanes, channels = pair_one_ref.shape
@@ -528,7 +528,7 @@
     gain = small_ref[ENTRY_GAINS : ENTRY_GAINS + 1, :channels]
     low = lane_iota((channels, lanes)) < half
     low_row = lane_iota((1, lanes)) < half
-    group = 4
+    group = 16
 
     @pl.loop(0, chips // group)
     def _(block):
@@ -555,17 +555,36 @@
         pair = jnp.concatenate(pairs, axis=0)
         keep = jnp.concatenate(keeps, axis=0)
         normed = normed_rows(pair, gain).astype(jnp.bfloat16)
-        projected = dot_nn(normed, flank_ref[0])
-        left = gated(projected, 0, channels, channels) * keep
-        right = gated(projected, 2 * channels, 3 * channels, channels) * keep
+        projected = dot_nn(normed, flank_ref[0, :, 2 * channels :])
+        right = gated(projected, 0, channels, channels) * keep
+        for c in range(group):
+            chip = block * group + c
+            rows = slice(c * lanes, (c + 1) * lanes)
+            pair_one_ref[chip] = pair[rows]
+            normed_ref[chip] = normed[rows]
+            right_ref[chip] = jnp.transpose(right[rows]).astype(jnp.bfloat16)
+
+
+def left_body(normed_ref, small_ref, flank_ref, switch_ref, left_ref, gate_ref, mkeys):
+    chips, lanes, channels = gate_ref.shape
+    half = lanes // 2
+    parity = lax.rem(lax.axis_index("dap"), 2)
+    mkeys[...] = presence_down(small_ref[PRESENCE : PRESENCE + 1, :half], half, lanes)
+    group = 8
+    for block in range(chips // group):
+        keeps = []
+        for c in range(group):
+            for r in range(2):
+                keeps.append(mkeys[...] * mkeys[pl.ds(4 * (block * group + c) + 2 * parity + r, 1), :])
+        normed = normed_ref[block * group : (block + 1) * group].reshape(group * lanes, channels)
+        projected = dot_nn(normed, flank_ref[0, :, : 2 * channels])
+        left = gated(projected, 0, channels, channels) * jnp.concatenate(keeps, axis=0)
         gate = jax.nn.sigmoid(dot_nn(normed, switch_ref[0]))
         for c in range(group):
             chip = block * group + c
             rows = slice(c * lanes, (c + 1) * lanes)
-            pair_one_ref[chip] = pair[rows]
             gate_ref[chip] = gate[rows]
-            left_ref[chip] = jnp.transpose(left[rows])
-            right_ref[chip] = jnp.transpose(right[rows]).astype(jnp.bfloat16)
+            left_ref[chip * channels : (chip + 1) * channels, :] = jnp.transpose(left[rows])
 
 
 def outgoing_body(
@@ -590,17 +609,27 @@
 
     low = lane_iota((chips, lanes)) < half
 
-    per_step = 32
+    per_step = 64
 
     @pl.loop(0, channels // per_step)
     def _(octet):
         results = []
+        stacked = []
+        for ref in (left_ref, sides.at[0], sides.at[1]):
+            stacked.append([])
+            for o in range(per_step // 8):
+                eight = jnp.stack(
+                    [
+                        ref[pl.ds(pl.multiple_of(chip * channels + octet * per_step + o * 8, 8), 8), :]
+                        for chip in range(chips)
+                    ]
+                )
+                stacked[-1].append(jnp.swapaxes(eight, 0, 1))
         for c in range(per_step):
-            at = pl.ds(octet * per_step + c, chips, stride=channels)
-            lhs = left_ref[at, :].astype(jnp.bfloat16)
+            lhs = stacked[0][c // 8][c % 8].astype(jnp.bfloat16)
             pieces = [[], []]
             for p in range(2):
-                rows = sides[p, at, :]
+                rows = stacked[1 + p][c // 8][c % 8]
                 turned = pltpu.roll(rows, half, 1)
                 pieces[0] += [jnp.where(low, rows, 0.0), jnp.where(low, turned, 0.0)]
                 pieces[1] += [jnp.where(low, 0.0, turned), jnp.where(low, 0.0, rows)]
@@ -618,7 +647,7 @@
     flank_right = flank_ref[1, :, 2 * channels :]
     flank_left = flank_ref[1, :, : 2 * channels]
     octet = pl.multiple_of(8 * (my_chip // 2), 8)
-    group = 4
+    group = 8
     for block in range(chips // group):
         changed = []
         for c in range(group):
@@ -631,13 +660,13 @@
             part = jnp.transpose(changed[:, c * lanes : (c + 1) * lanes])
             for k in range(8):
                 r, p, rj = k // 4, (k // 2) % 2, k % 2
-                rows_out[c, pl.ds(r * half + 2 * p + rj, chips, stride=4), :] = part[
+                rows_out[block * group + c, pl.ds(r * half + 2 * p + rj, chips, stride=4), :] = part[
                     k * chips : (k + 1) * chips
                 ]
         twos, keeps = [], []
         for c in range(group):
             chip = block * group + c
-            two = pair_one_ref[chip] + rows_out[c] * gate_ref[chip]
+            two = pair_one_ref[chip] + rows_out[chip] * gate_ref[chip]
             twos.append(two)
             for r in range(2):
                 keeps.append(mkeys[pl.ds(4 * chip + 2 * parity + r, 1), :])
@@ -646,9 +675,9 @@
         normed = full.astype(jnp.bfloat16)
         keep = jnp.concatenate([mkeys[...] * m for m in keeps], axis=0)
         going = (gated(dot_nn(normed, flank_right), 0, channels, channels) * keep).astype(jnp.bfloat16)
-        cols[...] = full
+        cols[block] = full
         few = jnp.concatenate(
-            [cols[pl.ds(k * half + octet, 8), :] for k in range(2 * group)], axis=0
+            [cols[block, pl.ds(k * half + octet, 8), :] for k in range(2 * group)], axis=0
         ).astype(jnp.bfloat16)
         mine = mkeys[pl.ds(octet, 8), :]
         keep = jnp.concatenate([mine * m for m in keeps], axis=0)
@@ -661,41 +690,52 @@
     two_ref[...] = pair_two[my_chip]
 
 
-def incoming_body(
-    own_ref, oth_ref, two_ref, couple_ref, small_ref, switch_ref, final_ref,
-    out_ref,
-):
-    chips, _, channels = own_ref.shape
-    lanes2 = out_ref.shape[0]
-    half = lanes2 // 2
+def add_products(side_ref, tails, totals):
+    chips = side_ref.shape[0]
+    half, _ = totals[0].shape
+    lanes = 2 * half
     me = lax.axis_index("dap")
-    gain_mid = small_ref[MID_GAINS : MID_GAINS + 1, channels : 2 * channels]
-    gain = small_ref[ENTRY_GAINS : ENTRY_GAINS + 1, channels : 2 * channels]
     first = 4 * lax.rem(me // 2, 2) + 2 * lax.rem(me, 2)
-    row = lax.broadcasted_iota(jnp.int32, (8, channels), 0)
-    totals = tuple(jnp.zeros((half, channels), jnp.float32) for _ in range(2))
-    for side_ref in (own_ref, oth_ref):
-
-        def step(chip, totals, side_ref=side_ref):
-            totals = list(totals)
-            tail = side_ref[chip, lanes2:, :].astype(jnp.float32)
+    tails[...] = side_ref[:, lanes:, :].astype(jnp.float32).reshape(tails.shape)
+    ahead = 4
+
+    def step(block, totals):
+        totals = list(totals)
+        for c in range(ahead):
+            chip = block * ahead + c
             for k in range(2):
                 there = side_ref[chip, k * half : (k + 1) * half, :].astype(jnp.float32)
                 for i in range(2):
-                    picked = jnp.where(row == first + i, tail[8 * k : 8 * k + 8], 0.0)
-                    one = jnp.sum(picked, axis=0, keepdims=True)
+                    one = tails[pl.ds(chip * 16 + 8 * k + first + i, 1), :]
                     totals[i] = totals[i] + one * there
-            return tuple(totals)
-
-        totals = lax.fori_loop(0, chips, step, totals)
-    prod = jnp.concatenate(totals, axis=0).astype(jnp.bfloat16).astype(jnp.float32)
+        return tuple(totals)
+
+    return lax.fori_loop(0, chips // ahead, step, tuple(totals))
+
+
+def incoming_own_body(own_ref, two_ref, couple_ref, small_ref, switch_ref, sums_ref, kept_ref, gate_ref, tails):
+    lanes, channels = two_ref.shape
+    half = lanes // 2
+    zero = jnp.zeros((half, channels), jnp.float32)
+    sums_ref[...] = jnp.concatenate(add_products(own_ref, tails, (zero, zero)), axis=0)
+    two = two_ref[...]
+    gain = small_ref[ENTRY_GAINS : ENTRY_GAINS + 1, channels : 2 * channels]
+    normed = normed_rows(two, gain).astype(jnp.bfloat16)
+    gate_ref[...] = jax.nn.sigmoid(dot_nn(normed, switch_ref[1]))
+    couple = couple_ref[...]
+    kept_ref[...] = two + (couple - couple.astype(jnp.bfloat16).astype(jnp.float32))
+
+
+def incoming_body(oth_ref, sums_ref, kept_ref, gate_ref, small_ref, final_ref, out_ref, tails):
+    lanes, channels = out_ref.shape
+    half = lanes // 2
+    prod = jnp.concatenate(
+        add_products(oth_ref, tails, (sums_ref[:half, :], sums_ref[half:, :])), axis=0
+    )
+    prod = prod.astype(jnp.bfloat16).astype(jnp.float32)
+    gain_mid = small_ref[MID_GAINS : MID_GAINS + 1, channels : 2 * channels]
     changed = dot_nn(normed_rows(prod, gain_mid).astype(jnp.bfloat16), final_ref[1])
-    two = two_ref[...]
-    normed = normed_rows(two, gain).astype(jnp.bfloat16)
-    gate = jax.nn.sigmoid(dot_nn(normed, switch_ref[1]))
-    couple = couple_ref[...]
-    lost = couple - couple.astype(jnp.bfloat16).astype(jnp.float32)
-    out_ref[...] = two + lost + changed * gate
+    out_ref[...] = kept_ref[...] + changed * gate_ref[...]
 
 
 def gather_by_steps(block, chips):
@@ -830,10 +870,11 @@
         opm, "dap", split_axis=0, concat_axis=0, tiled=True, axis_index_groups=same_parity
     )
     opm_oth = lax.ppermute(opm_own, "dap", swap)
+    msa = msa.reshape(devices * strands, rows, features)
     stack = (chips, lanes, channels)
-    pair_one, left, gate, right_own = vmem_call(
+    pair_one, normed, right_own = vmem_call(
         functools.partial(opm_body, len(couples)),
-        (shape(stack, f32), shape(stack, f32), shape(stack, f32), shape(stack, bf16)),
+        (shape(stack, f32), shape(stack, bf16), shape(stack, bf16)),
         scratch=[
             pltpu.VMEM((hidden * aminos, lanes), f32),
             pltpu.VMEM((2, chips * hidden, lanes), f32),
@@ -842,7 +883,8 @@
             pltpu.VMEM((aminos, channels), f32),
             pltpu.VMEM((devices * 16, lanes), f32),
         ],
-        count=len(couples) + 7,
+        count=len(couples) + 6,
+        later=1,
     )(
         opm_own,
         opm_oth,
@@ -851,9 +893,15 @@
         final,
         small,
         trio_flank_mappings,
-        trio_final_switches,
+        msa,
     )
     right_oth = lax.ppermute(right_own, "dap", swap)
+    left, gate = vmem_call(
+        left_body,
+        (shape((chips * channels, lanes), f32), shape(stack, f32)),
+        scratch=[pltpu.VMEM((aminos, channels), f32)],
+        count=4,
+    )(normed, small, trio_flank_mappings, trio_final_switches)
     two, going = vmem_call(
         outgoing_body,
         (shape((lanes, channels), f32), shape((chips, lanes + 16, channels), bf16)),
@@ -862,13 +910,13 @@
             pltpu.VMEM((channels * chips, lanes), f32),
             pltpu.VMEM((aminos, channels), f32),
             pltpu.VMEM(stack, f32),
-            pltpu.VMEM((4, lanes, channels), f32),
-            pltpu.VMEM((4 * lanes, channels), f32),
+            pltpu.VMEM(stack, f32),
+            pltpu.VMEM((chips // 8, 8 * lanes, channels), f32),
         ],
         count=8,
     )(
         pair_one,
-        left.reshape(chips * channels, lanes),
+        left,
         gate,
         right_own,
         right_oth,
@@ -877,13 +925,15 @@
         trio_flank_mappings,
     )
     coming = lax.ppermute(going, "dap", swap)
-    pair_out = vmem_call(
-        incoming_body, shape((lanes, channels), f32), count=7
-    )(going, coming, two, couple, small, trio_final_switches, trio_final_matrices)
-    return (
-        msa.reshape(devices * strands, rows, features),
-        pair_out.reshape(rows, aminos, channels),
-    )
+    own_rows = shape((lanes, channels), f32)
+    tails = [pltpu.VMEM((chips * 16, channels), f32)]
+    sums, kept, gate = vmem_call(
+        incoming_own_body, (own_rows,) * 3, scratch=tails, count=5
+    )(going, two, couple, small, trio_final_switches)
+    pair_out = vmem_call(incoming_body, own_rows, scratch=tails, count=6)(
+        coming, sums, kept, gate, small, trio_final_matrices
+    )
+    return msa, pair_out.reshape(rows, aminos, channels)
 
 
 def fits_pairs(homolog_stack, couple_tensor, devices):

time: 77.3 us -> 73.4 us (0.950)
  Pallas kernels: 21.8 us -> 19 us
  waiting for transfers between devices: 29.4 us -> 28.6 us
    pallas_call x1, Pallas kernels: 7.48 us -> 4.99 us  [paired_shards(): vmem_call(functools.partial(opm_body, len(couples)), (shape(stack, f32),...]
    pallas_call x1, Pallas kernels: 5.7 us -> 4.77 us  [paired_shards(): vmem_call(outgoing_body, (shape((lanes, channels), f32), shape((chips, la...]
    pallas_call x1 -> x3, Pallas kernels: 1.64 us -> 2.29 us  [the longest x1 1.13 us: paired_shards(): vmem_call(incoming_body, own_rows, scratch=tails, count=6)]
    unnamed x44 -> x46, local copies, waits for them, and re-layouts: 1.82 us -> 1.82 us
  transfers between devices with their start and end apart: 12 -> 12, of which waited for: 10 -> 10; matrix products, arithmetic and copies ran while one was open for 2% -> 1% of each run, Pallas kernels for 0% -> 2%
where the time goes in v4:
time: 73.4 us; the launch traced here: 72.9 us
  waiting for transfers between devices  28.6 us (39%)
  starting transfers between devices  22 us (30%)
  Pallas kernels  19 us (26%)
  local copies, waits for them, and re-layouts  2.33 us (3%)
  between operations  0.96 us (1%)
    ppermute x6, waiting for transfers between devices, fetch(): lax.ppermute(value, 'dap', [(d, d ^ 2 * apart) for d in range(devices)])  9.27 us
    ppermute x6, starting transfers between devices, fetch(): lax.ppermute(value, 'dap', [(d, d ^ 2 * apart) for d in range(devices)])  8.01 us
    all_to_all x1, starting transfers between devices, paired_shards(): lax.all_to_all(block, 'dap', split_axis=0, concat_axis=0, tiled=True)  7.33 us
    all_to_all x1, waiting for transfers between devices, paired_shards(): lax.all_to_all(sent, 'dap', split_axis=0, concat_axis=0, tiled=True)  6.91 us
    all_to_all x1, waiting for transfers between devices, paired_shards(): lax.all_to_all(block, 'dap', split_axis=0, concat_axis=0, tiled=True)  6 us
    pallas_call x1, Pallas kernels, paired_shards(): vmem_call(functools.partial(opm_body, len(couples)), (shape(stack, f32),...  4.99 us
    pallas_call x1, Pallas kernels, paired_shards(): vmem_call(outgoing_body, (shape((lanes, channels), f32), shape((chips, la...  4.77 us
    all_to_all x1, waiting for transfers between devices, paired_shards(): lax.all_to_all(opm, 'dap', split_axis=0, concat_axis=0, tiled=True, axis_...  3.86 us
  transfers between devices with their start and end apart: 12, of which 10 were waited for; matrix products, arithmetic and copies ran while one was open for 1% of the time, Pallas kernels for 2%

profile of v4, /device:TPU:0, one launch (start us, length us, event | category | flops | bytes accessed | tf_op | source)
XLA Modules:
  0.0 72.9 jit_solution(11105848550138323646)
XLA Ops:
  0.6 1.9 %shard_map.221 = (bf16[32,16,128]{2,1,0:T(8,128)(2,1)}, bf16[1,128,128]{2,1,0:T(8,128)(2,1)}) custom-call(f32[128,128]{1,0:T(8,128)} %bitcast.24, f32[1,128]{1,0:T(1,128)} %bitcast.37, bf16[8,128]{1,0:T(8,128)(2,1)} %bitcast.31, s32[2,64]{1,0:T(2,128)} %refs_3_.4), custom_call_target="tpu_custom_call" | custom-call | tf_op jit(solution)/shard_map/pallas_call | solution.py:795
  2.5 0.0 copy-start.2
  2.5 0.0 copy-start.10
  2.5 7.3 %all-to-all-start = ((bf16[32,16,128]{2,1,0:T(8,128)(2,1)}), bf16[32,16,128]{2,1,0:T(8,128)(2,1)S(1)}, u32[]{:S(2)}, u32[]{:S(2)}) async-start(bf16[32,16,128]{2,1,0:T(8,128)(2,1)} %get-tuple-element.20), calls=%async_computation | async-start | bytes 262144 | tf_op jit(solution)/shard_map/all_to_all | solution.py:809
  9.9 0.0 copy-start.17
  9.9 0.0 copy-start.18
  9.9 0.0 copy-start.19
  9.9 0.0 copy-start.15
  10.0 0.6 copy-done.17
  10.6 0.0 copy-done.18
  10.6 0.0 copy-done.19
  10.6 0.0 copy-done.15
  10.6 0.0 copy-done.16
  10.7 0.0 copy-start.3
  10.7 1.0 %copy-done.3 = bf16[256,768]{1,0:T(8,128)(2,1)S(1)} copy-done((bf16[256,768]{1,0:T(8,128)(2,1)S(1)}, bf16[256,768]{1,0:T(8,128)(2,1)}, u32[]{:S(2)}) %copy-start.3) | copy-done | bytes 393240
  11.7 0.4 shard_map.222
  12.1 6.0 %all-to-all-done.refs_0_.refs_1_.refs_6_ = bf16[32,16,128]{2,1,0:T(8,128)(2,1)S(1)} async-done(((bf16[32,16,128]{2,1,0:T(8,128)(2,1)}), bf16[32,16,128]{2,1,0:T(8,128)(2,1)S(1)}, u32[]{:S(2)}, u32[]{:S(2)}) %all-to-all-start) | async-done | bytes 131104 | tf_op jit(solution)/shard_map/all_to_all | solution.py:809
  18.1 2.3 %shard_map.223 = bf16[32,8,128]{2,1,0:T(8,128)(2,1)} custom-call(bf16[32,16,128]{2,1,0:T(8,128)(2,1)S(1)} %all-to-all-done.refs_0_.refs_1_.refs_6_, f32[128,256]{1,0:T(8,128)S(1)} %bitcast.23, f32[2,128,128]{2,1,0:T(8,128)S(1)} %get-tuple-element.21.refs_2_, bf16[128,256]{1,0:T(8,128)(2,1)S(1)} %get-tuple-element.22.refs_3_, ...), custom_call_target="tpu_custom_call" | custom-call | tf_op jit(solution)/shard_map/pallas_call | solution.py:837
  20.4 2.6 %all-to-all-start.1 = ((bf16[32,8,128]{2,1,0:T(8,128)(2,1)}), bf16[32,8,128]{2,1,0:T(8,128)(2,1)S(1)}, u32[]{:S(2)}, u32[]{:S(2)}) async-start(bf16[32,8,128]{2,1,0:T(8,128)(2,1)} %shard_map.223), calls=%async_computation.1 | async-start | bytes 131072 | tf_op jit(solution)/shard_map/all_to_all | solution.py:847
  23.0 0.2 copy.25
  23.3 0.0 copy-start.8
  23.3 0.1 copy.26.refs_7_
  23.5 6.9 %all-to-all-done.1.refs_0_ = bf16[32,8,128]{2,1,0:T(8,128)(2,1)S(1)} async-done(((bf16[32,8,128]{2,1,0:T(8,128)(2,1)}), bf16[32,8,128]{2,1,0:T(8,128)(2,1)S(1)}, u32[]{:S(2)}, u32[]{:S(2)}) %all-to-all-start.1) | async-done | bytes 65568 | tf_op jit(solution)/shard_map/all_to_all | solution.py:847
  30.4 2.4 %shard_map.224 = (f32[64,512]{1,0:T(8,128)S(1)}, bf16[16,64,128]{2,1,0:T(8,128)(2,1)}) custom-call(bf16[32,8,128]{2,1,0:T(8,128)(2,1)S(1)} %all-to-all-done.1.refs_0_, bf16[32,16,128]{2,1,0:T(8,128)(2,1)S(1)} %all-to-all-done.refs_0_.refs_1_.refs_6_, f32[8,256]{1,0:T(8,128)S(1)} %concatenate.6.refs_1_.refs_2_.refs_8_.refs_5_.refs_3_.refs_4_, ...), custom_call_target="tpu_custom_call" | custom-call | tf_op jit(solution)/shard_map/pallas_call | solution.py:848
  32.8 3.8 %all-to-all-start.2 = ((bf16[16,64,128]{2,1,0:T(8,128)(2,1)}), bf16[16,64,128]{2,1,0:T(8,128)(2,1)S(1)}, u32[]{:S(2)}, u32[]{:S(2)}) async-start(bf16[16,64,128]{2,1,0:T(8,128)(2,1)} %get-tuple-element.26), calls=%async_computation.2 | async-start | bytes 524288 | tf_op jit(solution)/shard_map/all_to_all | solution.py:869
  36.7 3.6 %collective-permute-start.3 = (bf16[1,128,128]{2,1,0:T(8,128)(2,1)S(1)}, bf16[1,128,128]{2,1,0:T(8,128)(2,1)S(1)}, u32[]{:S(2)}, u32[]{:S(2)}) collective-permute-start(bf16[1,128,128]{2,1,0:T(8,128)(2,1)S(1)} %copy-done.14), channel_id=1, source_target_pairs={{0,24},{1,25},{2,26},{3,27},{4,28},{5,29},{6,30},{7,31},{8,16},{9,... | collective-permute-start | bytes 98312 | tf_op jit(solution)/shard_map/ppermute | solution.py:747
  40.2 0.9 %collective-permute-start.1 = (bf16[1,128,128]{2,1,0:T(8,128)(2,1)S(1)}, bf16[1,128,128]{2,1,0:T(8,128)(2,1)S(1)}, u32[]{:S(2)}, u32[]{:S(2)}) collective-permute-start(bf16[1,128,128]{2,1,0:T(8,128)(2,1)S(1)} %copy-done.14), channel_id=1, source_target_pairs={{0,8},{1,9},{2,10},{3,11},{4,12},{5,13},{6,14},{7,15},{8,0},{9,1},... | collective-permute-start | bytes 98312 | tf_op jit(solution)/shard_map/ppermute | solution.py:747
  41.1 3.2 %collective-permute-done.1 = bf16[1,128,128]{2,1,0:T(8,128)(2,1)S(1)} collective-permute-done((bf16[1,128,128]{2,1,0:T(8,128)(2,1)S(1)}, bf16[1,128,128]{2,1,0:T(8,128)(2,1)S(1)}, u32[]{:S(2)}, u32[]{:S(2)}) %collective-permute-start.1) | collective-permute-done | bytes 32800 | tf_op jit(solution)/shard_map/ppermute | solution.py:747
  44.3 3.9 %all-to-all-done.2.refs_0_ = bf16[16,64,128]{2,1,0:T(8,128)(2,1)S(1)} async-done(((bf16[16,64,128]{2,1,0:T(8,128)(2,1)}), bf16[16,64,128]{2,1,0:T(8,128)(2,1)S(1)}, u32[]{:S(2)}, u32[]{:S(2)}) %all-to-all-start.2) | async-done | bytes 262176 | tf_op jit(solution)/shard_map/all_to_all | solution.py:869
  48.2 0.4 collective-permute-done.2
  48.6 2.4 %collective-permute-start.6 = (bf16[4,128,128]{2,1,0:T(8,128)(2,1)S(1)}, bf16[4,128,128]{2,1,0:T(8,128)(2,1)S(1)}, u32[]{:S(2)}, u32[]{:S(2)}) collective-permute-start(bf16[4,128,128]{2,1,0:T(8,128)(2,1)S(1)} %constant_dynamic-update-slice_fusion.refs_2_), channel_id=1, source_target_pairs={{0,6},{1,7},{2,4},{3,5},{4,2},{5,3},{6,0},{7,1},{8,14},{9,15},{10,... | collective-permute-start | bytes 393224 | tf_op jit(solution)/shard_map/ppermute | solution.py:747
  51.0 0.6 collective-permute-start.5
  51.6 0.6 collective-permute-start.4
  52.1 0.1 reshape.54.refs_10_
  52.2 0.0 copy-start.1
  52.2 0.0 copy-start.7
  52.2 3.7 %collective-permute-done.6.refs_5_ = bf16[4,128,128]{2,1,0:T(8,128)(2,1)S(1)} collective-permute-done((bf16[4,128,128]{2,1,0:T(8,128)(2,1)S(1)}, bf16[4,128,128]{2,1,0:T(8,128)(2,1)S(1)}, u32[]{:S(2)}, u32[]{:S(2)}) %collective-permute-start.6) | collective-permute-done | bytes 131104 | tf_op jit(solution)/shard_map/ppermute | solution.py:747
  55.9 2.0 %collective-permute-done.5.refs_4_ = bf16[4,128,128]{2,1,0:T(8,128)(2,1)S(1)} collective-permute-done((bf16[4,128,128]{2,1,0:T(8,128)(2,1)S(1)}, bf16[4,128,128]{2,1,0:T(8,128)(2,1)S(1)}, u32[]{:S(2)}, u32[]{:S(2)}) %collective-permute-start.5) | collective-permute-done | bytes 131104 | tf_op jit(solution)/shard_map/ppermute | solution.py:747
  57.9 0.1 collective-permute-done.4.refs_3_
  58.0 5.0 %shard_map.225 = (f32[16,128,128]{2,1,0:T(8,128)S(1)}, bf16[16,128,128]{2,1,0:T(8,128)(2,1)S(1)}, bf16[16,128,128]{2,1,0:T(8,128)(2,1)S(1)}) custom-call(bf16[16,64,128]{2,1,0:T(8,128)(2,1)S(1)} %all-to-all-done.2.refs_0_, bf16[16,64,128]{2,1,0:T(8,128)(2,1)S(1)} %collective-permute-done.refs_1_, ...), custom_call_target="tpu_custom_call" | custom-call | tf_op jit(solution)/shard_map/pallas_call | solution.py:875
  63.0 0.1 collective-permute-start.7
  63.1 0.7 shard_map.226
  63.7 1.2 %collective-permute-done.7.refs_4_ = bf16[16,128,128]{2,1,0:T(8,128)(2,1)S(1)} collective-permute-done((bf16[16,128,128]{2,1,0:T(8,128)(2,1)S(1)}, bf16[16,128,128]{2,1,0:T(8,128)(2,1)S(1)}, u32[]{:S(2)}, u32[]{:S(2)}) %collective-permute-start.7) | collective-permute-done | bytes 524320 | tf_op jit(solution)/shard_map/ppermute | solution.py:898
  64.9 4.8 %shard_map.227 = (f32[128,128]{1,0:T(8,128)S(1)}, bf16[16,144,128]{2,1,0:T(8,128)(2,1)S(1)}) custom-call(f32[16,128,128]{2,1,0:T(8,128)S(1)} %get-tuple-element.28.refs_0_, f32[2048,128]{1,0:T(8,128)S(1)} %get-tuple-element.30.refs_1_, f32[16,128,128]{2,1,0:T(8,128)S(1)} %get-tuple-element.31.refs_2_, bf16[16,128,128]{2,1,0:T(8,128)(2,1)S(1)} %get-tuple-element.32.refs_3_, ...), custom_call_target="tpu_custom_call" | custom-call | tf_op jit(solution)/shard_map/pallas_call | solution.py:905
  69.7 0.2 collective-permute-start.8
  69.9 0.5 shard_map.228
  70.4 1.4 %collective-permute-done.8.refs_0_ = bf16[16,144,128]{2,1,0:T(8,128)(2,1)S(1)} collective-permute-done((bf16[16,144,128]{2,1,0:T(8,128)(2,1)S(1)}, bf16[16,144,128]{2,1,0:T(8,128)(2,1)S(1)}, u32[]{:S(2)}, u32[]{:S(2)}) %collective-permute-start.8) | collective-permute-done | bytes 589856 | tf_op jit(solution)/shard_map/ppermute | solution.py:927
  71.8 1.1 %shard_map.229 = f32[128,128]{1,0:T(8,128)} custom-call(bf16[16,144,128]{2,1,0:T(8,128)(2,1)S(1)} %collective-permute-done.8.refs_0_, f32[128,128]{1,0:T(8,128)S(1)} %get-tuple-element.35.refs_1_, f32[128,128]{1,0:T(8,128)S(1)} %get-tuple-element.36.refs_2_, f32[128,128]{1,0:T(8,128)S(1)} %get-tuple-element.37.refs_3_, ...), custom_call_target="tpu_custom_call" | custom-call | tf_op jit(solution)/shard_map/pallas_call | solution.py:933
  (39 shorter events, 0.2 us)
Async XLA Ops:
  0.6 9.2 %copy-start.20 = (s32[64]{0:T(128)S(1)}, s32[64]{0:T(128)}, u32[]{:S(2)}) copy-start(s32[64]{0:T(128)} %param.25) | copy-start | bytes 772
  2.5 8.2 %copy-start.2 = (f32[2,64,256]{2,1,0:T(8,128)S(1)}, f32[2,64,256]{2,1,0:T(8,128)}, u32[]{:S(2)}) copy-start(f32[2,64,256]{2,1,0:T(8,128)} %param.22) | copy-start | bytes 393220
  2.5 8.2 %copy-start.10 = (bf16[256,256]{1,0:T(8,128)(2,1)S(1)}, bf16[256,256]{1,0:T(8,128)(2,1)}, u32[]{:S(2)}) copy-start(bf16[256,256]{1,0:T(8,128)(2,1)} %refs_2_.2) | copy-start | bytes 393220
  2.5 15.5 %all-to-all-start = ((bf16[32,16,128]{2,1,0:T(8,128)(2,1)}), bf16[32,16,128]{2,1,0:T(8,128)(2,1)S(1)}, u32[]{:S(2)}, u32[]{:S(2)}) async-start(bf16[32,16,128]{2,1,0:T(8,128)(2,1)} %get-tuple-element.20), calls=%async_computation | async-start | bytes 262144 | tf_op jit(solution)/shard_map/all_to_all | solution.py:809
  9.9 0.7 copy-start.17
  9.9 0.7 copy-start.18
  9.9 0.7 copy-start.19
  9.9 0.7 copy-start.15
  10.0 0.7 copy-start.16
  10.7 1.0 %copy-start.3 = (bf16[256,768]{1,0:T(8,128)(2,1)S(1)}, bf16[256,768]{1,0:T(8,128)(2,1)}, u32[]{:S(2)}) copy-start(bf16[256,768]{1,0:T(8,128)(2,1)} %refs_3_.5) | copy-start | bytes 1179652
  11.7 6.4 %copy-start.11 = (bf16[256,256]{1,0:T(8,128)(2,1)S(1)}, bf16[256,256]{1,0:T(8,128)(2,1)}, u32[]{:S(2)}) copy-start(bf16[256,256]{1,0:T(8,128)(2,1)} %refs_6_.2) | copy-start | bytes 393220
  18.1 4.9 %copy-start.13 = (bf16[1024,128]{1,0:T(8,128)(2,1)S(1)}, bf16[1024,128]{1,0:T(8,128)(2,1)}, u32[]{:S(2)}) copy-start(bf16[1024,128]{1,0:T(8,128)(2,1)} %param.38) | copy-start | bytes 786436
  20.4 10.0 %all-to-all-start.1 = ((bf16[32,8,128]{2,1,0:T(8,128)(2,1)}), bf16[32,8,128]{2,1,0:T(8,128)(2,1)S(1)}, u32[]{:S(2)}, u32[]{:S(2)}) async-start(bf16[32,8,128]{2,1,0:T(8,128)(2,1)} %shard_map.223), calls=%async_computation.1 | async-start | bytes 131072 | tf_op jit(solution)/shard_map/all_to_all | solution.py:847
  23.2 7.2 %copy-start.9 = (bf16[256,256]{1,0:T(8,128)(2,1)S(1)}, bf16[256,256]{1,0:T(8,128)(2,1)}, u32[]{:S(2)}) copy-start(bf16[256,256]{1,0:T(8,128)(2,1)} %refs_5_.2) | copy-start | bytes 393220
  23.2 7.1 %copy-start.12 = (bf16[256,64]{0,1:T(8,128)(2,1)S(1)}, bf16[256,64]{0,1:T(8,128)(2,1)}, u32[]{:S(2)}) copy-start(bf16[256,64]{0,1:T(8,128)(2,1)} %param.37) | copy-start | bytes 98308
  23.3 7.1 %copy-start.4 = (bf16[256,768]{1,0:T(8,128)(2,1)S(1)}, bf16[256,768]{1,0:T(8,128)(2,1)}, u32[]{:S(2)}) copy-start(bf16[256,768]{1,0:T(8,128)(2,1)} %refs_4_.2) | copy-start | bytes 1179652
  23.3 7.1 %copy-start.8 = (bf16[256,256]{1,0:T(8,128)(2,1)S(1)}, bf16[256,256]{1,0:T(8,128)(2,1)}, u32[]{:S(2)}) copy-start(bf16[256,256]{1,0:T(8,128)(2,1)} %refs_3_.6) | copy-start | bytes 393220
  32.8 3.9 %copy-start.14 = (bf16[1,128,128]{2,1,0:T(8,128)(2,1)S(1)}, bf16[1,128,128]{2,1,0:T(8,128)(2,1)}, u32[]{:S(2)}) copy-start(bf16[1,128,128]{2,1,0:T(8,128)(2,1)} %get-tuple-element.27) | copy-start | bytes 98308
  32.8 15.4 %all-to-all-start.2 = ((bf16[16,64,128]{2,1,0:T(8,128)(2,1)}), bf16[16,64,128]{2,1,0:T(8,128)(2,1)S(1)}, u32[]{:S(2)}, u32[]{:S(2)}) async-start(bf16[16,64,128]{2,1,0:T(8,128)(2,1)} %get-tuple-element.26), calls=%async_computation.2 | async-start | bytes 524288 | tf_op jit(solution)/shard_map/all_to_all | solution.py:869
  36.6 21.3 %copy-start = (bf16[2,128,512]{2,1,0:T(8,128)(2,1)S(1)}, bf16[2,128,512]{2,1,0:T(8,128)(2,1)}, u32[]{:S(2)}) copy-start(bf16[2,128,512]{2,1,0:T(8,128)(2,1)} %refs_7_.1) | copy-start | bytes 786436
  36.7 11.9 %collective-permute-start.3 = (bf16[1,128,128]{2,1,0:T(8,128)(2,1)S(1)}, bf16[1,128,128]{2,1,0:T(8,128)(2,1)S(1)}, u32[]{:S(2)}, u32[]{:S(2)}) collective-permute-start(bf16[1,128,128]{2,1,0:T(8,128)(2,1)S(1)} %copy-done.14), channel_id=1, source_target_pairs={{0,24},{1,25},{2,26},{3,27},{4,28},{5,29},{6,30},{7,31},{8,16},{9,... | collective-permute-start | bytes 98312 | tf_op jit(solution)/shard_map/ppermute | solution.py:747
  40.2 8.3 %collective-permute-start.2 = (bf16[1,128,128]{2,1,0:T(8,128)(2,1)S(1)}, bf16[1,128,128]{2,1,0:T(8,128)(2,1)S(1)}, u32[]{:S(2)}, u32[]{:S(2)}) collective-permute-start(bf16[1,128,128]{2,1,0:T(8,128)(2,1)S(1)} %copy-done.14), channel_id=1, source_target_pairs={{0,16},{1,17},{2,18},{3,19},{4,20},{5,21},{6,22},{7,23},{8,24},{9,... | collective-permute-start | bytes 98312 | tf_op jit(solution)/shard_map/ppermute | solution.py:747
  40.2 4.1 %collective-permute-start.1 = (bf16[1,128,128]{2,1,0:T(8,128)(2,1)S(1)}, bf16[1,128,128]{2,1,0:T(8,128)(2,1)S(1)}, u32[]{:S(2)}, u32[]{:S(2)}) collective-permute-start(bf16[1,128,128]{2,1,0:T(8,128)(2,1)S(1)} %copy-done.14), channel_id=1, source_target_pairs={{0,8},{1,9},{2,10},{3,11},{4,12},{5,13},{6,14},{7,15},{8,0},{9,1},... | collective-permute-start | bytes 98312 | tf_op jit(solution)/shard_map/ppermute | solution.py:747
  48.2 9.8 %collective-permute-start = (bf16[16,64,128]{2,1,0:T(8,128)(2,1)S(1)}, bf16[16,64,128]{2,1,0:T(8,128)(2,1)S(1)}, u32[]{:S(2)}, u32[]{:S(2)}) collective-permute-start(bf16[16,64,128]{2,1,0:T(8,128)(2,1)S(1)} %all-to-all-done.2.refs_0_), channel_id=1, source_target_pairs={{0,1},{1,0},{2,3},{3,2},{4,5},{5,4},{6,7},{7,6},{8,9},{9,8},{10,11... | collective-permute-start | bytes 786440 | tf_op jit(solution)/shard_map/ppermute | solution.py:872
  48.6 7.4 %collective-permute-start.6 = (bf16[4,128,128]{2,1,0:T(8,128)(2,1)S(1)}, bf16[4,128,128]{2,1,0:T(8,128)(2,1)S(1)}, u32[]{:S(2)}, u32[]{:S(2)}) collective-permute-start(bf16[4,128,128]{2,1,0:T(8,128)(2,1)S(1)} %constant_dynamic-update-slice_fusion.refs_2_), channel_id=1, source_target_pairs={{0,6},{1,7},{2,4},{3,5},{4,2},{5,3},{6,0},{7,1},{8,14},{9,15},{10,... | collective-permute-start | bytes 393224 | tf_op jit(solution)/shard_map/ppermute | solution.py:747
  51.0 6.9 %collective-permute-start.5 = (bf16[4,128,128]{2,1,0:T(8,128)(2,1)S(1)}, bf16[4,128,128]{2,1,0:T(8,128)(2,1)S(1)}, u32[]{:S(2)}, u32[]{:S(2)}) collective-permute-start(bf16[4,128,128]{2,1,0:T(8,128)(2,1)S(1)} %constant_dynamic-update-slice_fusion.refs_2_), channel_id=1, source_target_pairs={{0,4},{1,5},{2,6},{3,7},{4,0},{5,1},{6,2},{7,3},{8,12},{9,13},{10,... | collective-permute-start | bytes 393224 | tf_op jit(solution)/shard_map/ppermute | solution.py:747
  51.6 6.4 %collective-permute-start.4 = (bf16[4,128,128]{2,1,0:T(8,128)(2,1)S(1)}, bf16[4,128,128]{2,1,0:T(8,128)(2,1)S(1)}, u32[]{:S(2)}, u32[]{:S(2)}) collective-permute-start(bf16[4,128,128]{2,1,0:T(8,128)(2,1)S(1)} %constant_dynamic-update-slice_fusion.refs_2_), channel_id=1, source_target_pairs={{0,2},{1,3},{2,0},{3,1},{4,6},{5,7},{6,4},{7,5},{8,10},{9,11},{10,... | collective-permute-start | bytes 393224 | tf_op jit(solution)/shard_map/ppermute | solution.py:747
  52.2 10.8 %copy-start.1 = (f32[64,2,256]{2,1,0:T(2,128)}, f32[64,2,256]{2,1,0:T(2,128)S(1)}, u32[]{:S(2)}) copy-start(f32[64,2,256]{2,1,0:T(2,128)S(1)} %reshape.54.refs_10_) | copy-start | bytes 393220
  52.2 10.8 %copy-start.7 = (bf16[2,128,128]{2,1,0:T(8,128)(2,1)S(1)}, bf16[2,128,128]{2,1,0:T(8,128)(2,1)}, u32[]{:S(2)}) copy-start(bf16[2,128,128]{2,1,0:T(8,128)(2,1)} %refs_4_.3) | copy-start | bytes 196612
  63.0 2.0 %collective-permute-start.7 = (bf16[16,128,128]{2,1,0:T(8,128)(2,1)S(1)}, bf16[16,128,128]{2,1,0:T(8,128)(2,1)S(1)}, u32[]{:S(2)}, u32[]{:S(2)}) collective-permute-start(bf16[16,128,128]{2,1,0:T(8,128)(2,1)S(1)} %get-tuple-element.32.refs_3_), channel_id=1, source_target_pairs={{0,1},{1,0},{2,3},{3,2},{4,5},{5,4},{6,7},{7,6},{8,9},{9,8},{10,11... | collective-permute-start | bytes 1572872 | tf_op jit(solution)/shard_map/ppermute | solution.py:898
  63.1 1.9 %copy-start.5 = (bf16[2,128,128]{2,1,0:T(8,128)(2,1)S(1)}, bf16[2,128,128]{2,1,0:T(8,128)(2,1)}, u32[]{:S(2)}) copy-start(bf16[2,128,128]{2,1,0:T(8,128)(2,1)} %refs_5_.3) | copy-start | bytes 196612
  64.9 5.0 %copy-start.6 = (f32[2,64,128]{2,1,0:T(8,128)S(1)}, f32[2,64,128]{2,1,0:T(8,128)}, u32[]{:S(2)}) copy-start(f32[2,64,128]{2,1,0:T(8,128)} %param.23) | copy-start | bytes 196612
  69.7 2.1 %collective-permute-start.8 = (bf16[16,144,128]{2,1,0:T(8,128)(2,1)S(1)}, bf16[16,144,128]{2,1,0:T(8,128)(2,1)S(1)}, u32[]{:S(2)}, u32[]{:S(2)}) collective-permute-start(bf16[16,144,128]{2,1,0:T(8,128)(2,1)S(1)} %get-tuple-element.33.refs_0_), channel_id=1, source_target_pairs={{0,1},{1,0},{2,3},{3,2},{4,5},{5,4},{6,7},{7,6},{8,9},{9,8},{10,11... | collective-permute-start | bytes 1769480 | tf_op jit(solution)/shard_map/ppermute | solution.py:927

commit v5 on v4

--- a/solution.py
+++ b/solution.py
@@ -496,7 +496,7 @@
         order, order16, outer, counts, mkeys, wide_blk,
     ) = refs
     chips, lanes, channels = pair_one_ref.shape
-    hidden = outer.shape[2]
+    hidden = outer.shape[1]
     half = lanes // 2
     me = lax.axis_index("dap")
     parity = lax.rem(me, 2)
@@ -507,17 +507,23 @@
     rows = (chips * hidden, lanes)
     order16[parity] = own_ref[:, hidden:, :].astype(jnp.float32).reshape(rows)
     order16[1 - parity] = oth_ref[:, hidden:, :].astype(jnp.float32).reshape(rows)
+    early = lane_iota((chips, lanes)) < half
     for b in range(hidden):
         for p in range(2):
             rows = order16[p, pl.ds(b, chips, stride=hidden), :]
+            turned = pltpu.roll(rows, half, 1)
             for r in range(2):
-                order[pl.ds(b * half + 2 * p + r, chips, stride=4), :] = (
-                    pltpu.roll(rows, half, 1) if r else rows
-                )
-    rights = order[...].astype(jnp.bfloat16)[:, :half]
-    for r in range(2):
-        lhs = own_ref[:, :hidden, :].reshape(chips * hidden, lanes)[:, r * half : (r + 1) * half]
-        outer[r] = dot_nt(lhs, rights).astype(jnp.bfloat16).reshape(outer.shape[1:])
+                for rj in range(2):
+                    part = rows if r == rj else turned
+                    part = jnp.where(early, 0.0, part) if r else jnp.where(early, part, 0.0)
+                    order[pl.ds(b * lanes + r * half + 2 * p + rj, chips, stride=4), :] = part
+    rights = order[...].astype(jnp.bfloat16)
+    few = 4
+    for q in range(chips // few):
+        lhs = own_ref[q * few : (q + 1) * few, :hidden, :].reshape(few * hidden, lanes)
+        outer[q * few : (q + 1) * few] = (
+            dot_nt(lhs, rights).astype(jnp.bfloat16).reshape((few,) + outer.shape[1:])
+        )
     mask_rows = mask_block(blk_ref, wide_blk)
     total = jnp.zeros((half, lanes), jnp.float32)
     for s in range(2):
@@ -526,30 +532,29 @@
     counts[...] = 1.0 / jnp.maximum(total, 1.0)
     mkeys[...] = presence_down(small_ref[PRESENCE : PRESENCE + 1, :half], half, lanes)
     gain = small_ref[ENTRY_GAINS : ENTRY_GAINS + 1, :channels]
-    low = lane_iota((channels, lanes)) < half
     low_row = lane_iota((1, lanes)) < half
     group = 16
 
     @pl.loop(0, chips // group)
     def _(block):
         pairs, keeps = [], []
-        for c in range(group):
-            chip = block * group + c
+        made = []
+        for c in range(0, group, 2):
             sides = []
-            for r in range(2):
-                strip = outer[r, chip]
+            for chip in (block * group + c, block * group + c + 1):
+                strip = outer[chip]
                 sides.append(
                     jnp.concatenate(
-                        [strip[:, g * lanes : (g + 1) * lanes] for g in range(hidden // 2)], axis=0
+                        [strip[:, b * lanes : (b + 1) * lanes] for b in range(hidden)], axis=0
                     )
                 )
             res = dot_nn(fin_ref[...], jnp.concatenate(sides, axis=1))
-            a0, a1 = res[:channels, :lanes], res[:channels, lanes:]
-            b0, b1 = res[channels:, :lanes], res[channels:, lanes:]
-            turned = jnp.where(low, a0, b1) + pltpu.roll(jnp.where(low, a1, b0), half, 1)
+            made += [res[:, :lanes], res[:, lanes:]]
+        for c in range(group):
+            chip = block * group + c
             i0 = 4 * chip + 2 * parity
             share = jnp.where(low_row, counts[pl.ds(i0, 1), :], counts[pl.ds(i0 + 1, 1), :])
-            pairs.append(jnp.transpose(turned * share) + pair_one_ref[chip])
+            pairs.append(jnp.transpose(made[c] * share) + pair_one_ref[chip])
             for r in range(2):
                 keeps.append(mkeys[...] * mkeys[pl.ds(i0 + r, 1), :])
         pair = jnp.concatenate(pairs, axis=0)
@@ -612,32 +617,34 @@
     per_step = 64
 
     @pl.loop(0, channels // per_step)
-    def _(octet):
-        results = []
-        stacked = []
-        for ref in (left_ref, sides.at[0], sides.at[1]):
-            stacked.append([])
-            for o in range(per_step // 8):
-                eight = jnp.stack(
-                    [
-                        ref[pl.ds(pl.multiple_of(chip * channels + octet * per_step + o * 8, 8), 8), :]
-                        for chip in range(chips)
-                    ]
+    def _(step):
+        for o in range(per_step // 8):
+            base = step * per_step + o * 8
+            left, even, odd = (
+                jnp.swapaxes(
+                    jnp.stack(
+                        [
+                            ref[pl.ds(pl.multiple_of(chip * channels + base, 8), 8), :]
+                            for chip in range(chips)
+                        ]
+                    ),
+                    0,
+                    1,
                 )
-                stacked[-1].append(jnp.swapaxes(eight, 0, 1))
-        for c in range(per_step):
-            lhs = stacked[0][c // 8][c % 8].astype(jnp.bfloat16)
-            pieces = [[], []]
-            for p in range(2):
-                rows = stacked[1 + p][c // 8][c % 8]
-                turned = pltpu.roll(rows, half, 1)
-                pieces[0] += [jnp.where(low, rows, 0.0), jnp.where(low, turned, 0.0)]
-                pieces[1] += [jnp.where(low, 0.0, turned), jnp.where(low, 0.0, rows)]
-            rhs = jnp.concatenate(pieces[0] + pieces[1], axis=0).astype(jnp.bfloat16)
-            results.append(dot_nt(lhs, rhs))
-        for c in range(per_step):
-            to = pl.ds(pl.multiple_of((octet * per_step + c) * chips, chips), chips)
-            prods[to, :] = results[c].astype(jnp.bfloat16).astype(jnp.float32)
+                for ref in (left_ref, sides.at[0], sides.at[1])
+            )
+            for c in range(8):
+                lhs = jnp.concatenate(
+                    [jnp.where(low, left[c], 0.0), jnp.where(low, 0.0, left[c])], axis=0
+                )
+                rhs = jnp.concatenate(
+                    [even[c], pltpu.roll(even[c], half, 1), odd[c], pltpu.roll(odd[c], half, 1)],
+                    axis=0,
+                )
+                out = dot_nt(lhs.astype(jnp.bfloat16), rhs.astype(jnp.bfloat16))
+                out = jnp.concatenate([out[:chips], out[chips:]], axis=1)
+                to = pl.ds(base + c, chips, stride=channels)
+                prods[to, :] = out.astype(jnp.bfloat16).astype(jnp.float32)
 
     mkeys[...] = presence_down(small_ref[PRESENCE : PRESENCE + 1, :half], half, channels)
     gain_mid = small_ref[MID_GAINS : MID_GAINS + 1, :channels]
@@ -651,7 +658,7 @@
     for block in range(chips // group):
         changed = []
         for c in range(group):
-            x = prods[pl.ds(block * group + c, channels, stride=chips), :]
+            x = prods[(block * group + c) * channels : (block * group + c + 1) * channels, :]
             centred = x - jnp.mean(x, axis=0, keepdims=True)
             spread = jnp.mean(centred * centred, axis=0, keepdims=True)
             changed.append((centred * lax.rsqrt(spread + EPSILON) * gain_mid).astype(jnp.bfloat16))
@@ -659,7 +666,8 @@
         for c in range(group):
             part = jnp.transpose(changed[:, c * lanes : (c + 1) * lanes])
             for k in range(8):
-                r, p, rj = k // 4, (k // 2) % 2, k % 2
+                r, p = k // 4, (k // 2) % 2
+                rj = k % 2 if r == 0 else 1 - k % 2
                 rows_out[block * group + c, pl.ds(r * half + 2 * p + rj, chips, stride=4), :] = part[
                     k * chips : (k + 1) * chips
                 ]
@@ -820,8 +828,8 @@
         axis=0,
     )
     final = jnp.transpose(
-        tensor_average_final.reshape(hidden, hidden // 2, 2, channels), (2, 3, 1, 0)
-    ).reshape(2 * channels, hidden * hidden // 2)
+        tensor_average_final.reshape(hidden, hidden, channels), (2, 1, 0)
+    ).reshape(channels, hidden * hidden)
     q, k, v, g = vmem_call(
         project_body,
         (
@@ -876,9 +884,9 @@
         functools.partial(opm_body, len(couples)),
         (shape(stack, f32), shape(stack, bf16), shape(stack, bf16)),
         scratch=[
-            pltpu.VMEM((hidden * aminos, lanes), f32),
+            pltpu.VMEM((hidden * lanes, lanes), f32),
             pltpu.VMEM((2, chips * hidden, lanes), f32),
-            pltpu.VMEM((2, chips, hidden, hidden * aminos), bf16),
+            pltpu.VMEM((chips, hidden, hidden * lanes), bf16),
             pltpu.VMEM((aminos, lanes), f32),
             pltpu.VMEM((aminos, channels), f32),
             pltpu.VMEM((devices * 16, lanes), f32),

time: 73.4 us -> 71.3 us (0.971)
  Pallas kernels: 19 us -> 16.9 us
    pallas_call x1, Pallas kernels: 4.99 us -> 3.57 us  [paired_shards(): vmem_call(functools.partial(opm_body, len(couples)), (shape(stack, f32),...]
    unnamed x46 -> x45, local copies, waits for them, and re-layouts: 1.82 us -> 1.79 us
where the time goes in v5:
time: 71.3 us; the launch traced here: 70.8 us
  waiting for transfers between devices  29 us (41%)
  starting transfers between devices  21.8 us (31%)
  Pallas kernels  16.9 us (24%)
  local copies, waits for them, and re-layouts  2.17 us (3%)
  between operations  0.96 us (1%)
    ppermute x6, waiting for transfers between devices, fetch(): lax.ppermute(value, 'dap', [(d, d ^ 2 * apart) for d in range(devices)])  9.45 us
    ppermute x6, starting transfers between devices, fetch(): lax.ppermute(value, 'dap', [(d, d ^ 2 * apart) for d in range(devices)])  8.01 us
    all_to_all x1, starting transfers between devices, paired_shards(): lax.all_to_all(block, 'dap', split_axis=0, concat_axis=0, tiled=True)  7.33 us
    all_to_all x1, waiting for transfers between devices, paired_shards(): lax.all_to_all(sent, 'dap', split_axis=0, concat_axis=0, tiled=True)  7.08 us
    all_to_all x1, waiting for transfers between devices, paired_shards(): lax.all_to_all(block, 'dap', split_axis=0, concat_axis=0, tiled=True)  6 us
    pallas_call x1, Pallas kernels, paired_shards(): vmem_call(outgoing_body, (shape((lanes, channels), f32), shape((chips, la...  4.11 us
    all_to_all x1, waiting for transfers between devices, paired_shards(): lax.all_to_all(opm, 'dap', split_axis=0, concat_axis=0, tiled=True, axis_...  3.86 us
    all_to_all x1, starting transfers between devices, paired_shards(): lax.all_to_all(opm, 'dap', split_axis=0, concat_axis=0, tiled=True, axis_...  3.66 us
  transfers between devices with their start and end apart: 12, of which 10 were waited for; matrix products, arithmetic and copies ran while one was open for 1% of the time, Pallas kernels for 2%

profile of v5, /device:TPU:0, one launch (start us, length us, event | category | flops | bytes accessed | tf_op | source)
XLA Modules:
  0.0 70.8 jit_solution(12757343709725180262)
XLA Ops:
  0.6 1.9 %shard_map.221 = (bf16[32,16,128]{2,1,0:T(8,128)(2,1)}, bf16[1,128,128]{2,1,0:T(8,128)(2,1)}) custom-call(f32[128,128]{1,0:T(8,128)} %bitcast.19, f32[1,128]{1,0:T(1,128)} %bitcast.31, bf16[8,128]{1,0:T(8,128)(2,1)} %bitcast.25, s32[2,64]{1,0:T(2,128)} %refs_3_.4), custom_call_target="tpu_custom_call" | custom-call | tf_op jit(solution)/shard_map/pallas_call | solution.py:803
  2.5 0.0 copy-start.2
  2.5 0.0 copy-start.10
  2.5 7.3 %all-to-all-start = ((bf16[32,16,128]{2,1,0:T(8,128)(2,1)}), bf16[32,16,128]{2,1,0:T(8,128)(2,1)S(1)}, u32[]{:S(2)}, u32[]{:S(2)}) async-start(bf16[32,16,128]{2,1,0:T(8,128)(2,1)} %get-tuple-element.20), calls=%async_computation | async-start | bytes 262144 | tf_op jit(solution)/shard_map/all_to_all | solution.py:817
  9.9 0.0 copy-start.17
  9.9 0.0 copy-start.18
  9.9 0.0 copy-start.19
  9.9 0.0 copy-start.15
  10.0 0.6 copy-done.17
  10.6 0.0 copy-done.18
  10.6 0.0 copy-done.19
  10.6 0.0 copy-done.15
  10.6 0.0 copy-done.16
  10.7 1.0 %copy-done.3 = bf16[256,768]{1,0:T(8,128)(2,1)S(1)} copy-done((bf16[256,768]{1,0:T(8,128)(2,1)S(1)}, bf16[256,768]{1,0:T(8,128)(2,1)}, u32[]{:S(2)}) %copy-start.3) | copy-done | bytes 393240
  11.7 0.4 shard_map.222
  12.1 6.0 %all-to-all-done.refs_0_.refs_1_.refs_6_ = bf16[32,16,128]{2,1,0:T(8,128)(2,1)S(1)} async-done(((bf16[32,16,128]{2,1,0:T(8,128)(2,1)}), bf16[32,16,128]{2,1,0:T(8,128)(2,1)S(1)}, u32[]{:S(2)}, u32[]{:S(2)}) %all-to-all-start) | async-done | bytes 131104 | tf_op jit(solution)/shard_map/all_to_all | solution.py:817
  18.1 2.3 %shard_map.223 = bf16[32,8,128]{2,1,0:T(8,128)(2,1)} custom-call(bf16[32,16,128]{2,1,0:T(8,128)(2,1)S(1)} %all-to-all-done.refs_0_.refs_1_.refs_6_, f32[128,256]{1,0:T(8,128)S(1)} %bitcast.18, f32[2,128,128]{2,1,0:T(8,128)S(1)} %get-tuple-element.21.refs_2_, bf16[128,256]{1,0:T(8,128)(2,1)S(1)} %get-tuple-element.22.refs_3_, ...), custom_call_target="tpu_custom_call" | custom-call | tf_op jit(solution)/shard_map/pallas_call | solution.py:845
  20.4 2.6 %all-to-all-start.1 = ((bf16[32,8,128]{2,1,0:T(8,128)(2,1)}), bf16[32,8,128]{2,1,0:T(8,128)(2,1)S(1)}, u32[]{:S(2)}, u32[]{:S(2)}) async-start(bf16[32,8,128]{2,1,0:T(8,128)(2,1)} %shard_map.223), calls=%async_computation.1 | async-start | bytes 131072 | tf_op jit(solution)/shard_map/all_to_all | solution.py:855
  23.0 0.0 copy-start.9
  23.0 0.0 copy-start.12
  23.0 0.1 copy.27
  23.1 0.1 copy.28.refs_7_
  23.3 7.1 %all-to-all-done.1.refs_0_ = bf16[32,8,128]{2,1,0:T(8,128)(2,1)S(1)} async-done(((bf16[32,8,128]{2,1,0:T(8,128)(2,1)}), bf16[32,8,128]{2,1,0:T(8,128)(2,1)S(1)}, u32[]{:S(2)}, u32[]{:S(2)}) %all-to-all-start.1) | async-done | bytes 65568 | tf_op jit(solution)/shard_map/all_to_all | solution.py:855
  30.4 2.4 %shard_map.224 = (f32[64,512]{1,0:T(8,128)S(1)}, bf16[16,64,128]{2,1,0:T(8,128)(2,1)}) custom-call(bf16[32,8,128]{2,1,0:T(8,128)(2,1)S(1)} %all-to-all-done.1.refs_0_, bf16[32,16,128]{2,1,0:T(8,128)(2,1)S(1)} %all-to-all-done.refs_0_.refs_1_.refs_6_, f32[8,256]{1,0:T(8,128)S(1)} %concatenate.6.refs_1_.refs_2_.refs_8_.refs_5_.refs_3_.refs_4_, ...), custom_call_target="tpu_custom_call" | custom-call | tf_op jit(solution)/shard_map/pallas_call | solution.py:856
  32.8 3.7 %all-to-all-start.2 = ((bf16[16,64,128]{2,1,0:T(8,128)(2,1)}), bf16[16,64,128]{2,1,0:T(8,128)(2,1)S(1)}, u32[]{:S(2)}, u32[]{:S(2)}) async-start(bf16[16,64,128]{2,1,0:T(8,128)(2,1)} %get-tuple-element.26), calls=%async_computation.2 | async-start | bytes 524288 | tf_op jit(solution)/shard_map/all_to_all | solution.py:877
  36.5 3.7 %collective-permute-start.3 = (bf16[1,128,128]{2,1,0:T(8,128)(2,1)S(1)}, bf16[1,128,128]{2,1,0:T(8,128)(2,1)S(1)}, u32[]{:S(2)}, u32[]{:S(2)}) collective-permute-start(bf16[1,128,128]{2,1,0:T(8,128)(2,1)S(1)} %copy-done.14), channel_id=1, source_target_pairs={{0,24},{1,25},{2,26},{3,27},{4,28},{5,29},{6,30},{7,31},{8,16},{9,... | collective-permute-start | bytes 98312 | tf_op jit(solution)/shard_map/ppermute | solution.py:755
  40.2 0.7 %collective-permute-start.1 = (bf16[1,128,128]{2,1,0:T(8,128)(2,1)S(1)}, bf16[1,128,128]{2,1,0:T(8,128)(2,1)S(1)}, u32[]{:S(2)}, u32[]{:S(2)}) collective-permute-start(bf16[1,128,128]{2,1,0:T(8,128)(2,1)S(1)} %copy-done.14), channel_id=1, source_target_pairs={{0,8},{1,9},{2,10},{3,11},{4,12},{5,13},{6,14},{7,15},{8,0},{9,1},... | collective-permute-start | bytes 98312 | tf_op jit(solution)/shard_map/ppermute | solution.py:755
  40.9 3.3 %collective-permute-done.1 = bf16[1,128,128]{2,1,0:T(8,128)(2,1)S(1)} collective-permute-done((bf16[1,128,128]{2,1,0:T(8,128)(2,1)S(1)}, bf16[1,128,128]{2,1,0:T(8,128)(2,1)S(1)}, u32[]{:S(2)}, u32[]{:S(2)}) %collective-permute-start.1) | collective-permute-done | bytes 32800 | tf_op jit(solution)/shard_map/ppermute | solution.py:755
  44.3 3.9 %all-to-all-done.2.refs_0_ = bf16[16,64,128]{2,1,0:T(8,128)(2,1)S(1)} async-done(((bf16[16,64,128]{2,1,0:T(8,128)(2,1)}), bf16[16,64,128]{2,1,0:T(8,128)(2,1)S(1)}, u32[]{:S(2)}, u32[]{:S(2)}) %all-to-all-start.2) | async-done | bytes 262176 | tf_op jit(solution)/shard_map/all_to_all | solution.py:877
  48.2 0.4 collective-permute-done.2
  48.6 2.4 %collective-permute-start.6 = (bf16[4,128,128]{2,1,0:T(8,128)(2,1)S(1)}, bf16[4,128,128]{2,1,0:T(8,128)(2,1)S(1)}, u32[]{:S(2)}, u32[]{:S(2)}) collective-permute-start(bf16[4,128,128]{2,1,0:T(8,128)(2,1)S(1)} %constant_dynamic-update-slice_fusion.refs_2_), channel_id=1, source_target_pairs={{0,6},{1,7},{2,4},{3,5},{4,2},{5,3},{6,0},{7,1},{8,14},{9,15},{10,... | collective-permute-start | bytes 393224 | tf_op jit(solution)/shard_map/ppermute | solution.py:755
  51.0 0.6 collective-permute-start.5
  51.6 0.6 collective-permute-start.4
  52.1 0.1 reshape.54.refs_10_
  52.2 0.0 copy-start.1
  52.2 0.0 copy-start.7
  52.2 3.7 %collective-permute-done.6.refs_5_ = bf16[4,128,128]{2,1,0:T(8,128)(2,1)S(1)} collective-permute-done((bf16[4,128,128]{2,1,0:T(8,128)(2,1)S(1)}, bf16[4,128,128]{2,1,0:T(8,128)(2,1)S(1)}, u32[]{:S(2)}, u32[]{:S(2)}) %collective-permute-start.6) | collective-permute-done | bytes 131104 | tf_op jit(solution)/shard_map/ppermute | solution.py:755
  55.9 2.0 %collective-permute-done.5.refs_4_ = bf16[4,128,128]{2,1,0:T(8,128)(2,1)S(1)} collective-permute-done((bf16[4,128,128]{2,1,0:T(8,128)(2,1)S(1)}, bf16[4,128,128]{2,1,0:T(8,128)(2,1)S(1)}, u32[]{:S(2)}, u32[]{:S(2)}) %collective-permute-start.5) | collective-permute-done | bytes 131104 | tf_op jit(solution)/shard_map/ppermute | solution.py:755
  57.9 0.1 collective-permute-done.4.refs_3_
  58.0 3.6 %shard_map.225 = (f32[16,128,128]{2,1,0:T(8,128)S(1)}, bf16[16,128,128]{2,1,0:T(8,128)(2,1)S(1)}, bf16[16,128,128]{2,1,0:T(8,128)(2,1)S(1)}) custom-call(bf16[16,64,128]{2,1,0:T(8,128)(2,1)S(1)} %all-to-all-done.2.refs_0_, bf16[16,64,128]{2,1,0:T(8,128)(2,1)S(1)} %collective-permute-done.refs_1_, ...), custom_call_target="tpu_custom_call" | custom-call | tf_op jit(solution)/shard_map/pallas_call | solution.py:883
  61.5 0.1 collective-permute-start.7
  61.6 0.7 shard_map.226
  62.3 1.2 %collective-permute-done.7.refs_4_ = bf16[16,128,128]{2,1,0:T(8,128)(2,1)S(1)} collective-permute-done((bf16[16,128,128]{2,1,0:T(8,128)(2,1)S(1)}, bf16[16,128,128]{2,1,0:T(8,128)(2,1)S(1)}, u32[]{:S(2)}, u32[]{:S(2)}) %collective-permute-start.7) | collective-permute-done | bytes 524320 | tf_op jit(solution)/shard_map/ppermute | solution.py:906
  63.5 4.1 %shard_map.227 = (f32[128,128]{1,0:T(8,128)S(1)}, bf16[16,144,128]{2,1,0:T(8,128)(2,1)S(1)}) custom-call(f32[16,128,128]{2,1,0:T(8,128)S(1)} %get-tuple-element.28.refs_0_, f32[2048,128]{1,0:T(8,128)S(1)} %get-tuple-element.30.refs_1_, f32[16,128,128]{2,1,0:T(8,128)S(1)} %get-tuple-element.31.refs_2_, bf16[16,128,128]{2,1,0:T(8,128)(2,1)S(1)} %get-tuple-element.32.refs_3_, ...), custom_call_target="tpu_custom_call" | custom-call | tf_op jit(solution)/shard_map/pallas_call | solution.py:913
  67.6 0.2 collective-permute-start.8
  67.8 0.5 shard_map.228
  68.3 1.4 %collective-permute-done.8.refs_0_ = bf16[16,144,128]{2,1,0:T(8,128)(2,1)S(1)} collective-permute-done((bf16[16,144,128]{2,1,0:T(8,128)(2,1)S(1)}, bf16[16,144,128]{2,1,0:T(8,128)(2,1)S(1)}, u32[]{:S(2)}, u32[]{:S(2)}) %collective-permute-start.8) | collective-permute-done | bytes 589856 | tf_op jit(solution)/shard_map/ppermute | solution.py:935
  69.7 1.1 %shard_map.229 = f32[128,128]{1,0:T(8,128)} custom-call(bf16[16,144,128]{2,1,0:T(8,128)(2,1)S(1)} %collective-permute-done.8.refs_0_, f32[128,128]{1,0:T(8,128)S(1)} %get-tuple-element.35.refs_1_, f32[128,128]{1,0:T(8,128)S(1)} %get-tuple-element.36.refs_2_, f32[128,128]{1,0:T(8,128)S(1)} %get-tuple-element.37.refs_3_, ...), custom_call_target="tpu_custom_call" | custom-call | tf_op jit(solution)/shard_map/pallas_call | solution.py:941
  (38 shorter events, 0.1 us)
Async XLA Ops:
  0.6 9.2 %copy-start.20 = (s32[64]{0:T(128)S(1)}, s32[64]{0:T(128)}, u32[]{:S(2)}) copy-start(s32[64]{0:T(128)} %param.25) | copy-start | bytes 772
  2.5 8.2 %copy-start.2 = (f32[2,64,256]{2,1,0:T(8,128)S(1)}, f32[2,64,256]{2,1,0:T(8,128)}, u32[]{:S(2)}) copy-start(f32[2,64,256]{2,1,0:T(8,128)} %param.22) | copy-start | bytes 393220
  2.5 8.2 %copy-start.10 = (bf16[256,256]{1,0:T(8,128)(2,1)S(1)}, bf16[256,256]{1,0:T(8,128)(2,1)}, u32[]{:S(2)}) copy-start(bf16[256,256]{1,0:T(8,128)(2,1)} %refs_2_.2) | copy-start | bytes 393220
  2.5 15.5 %all-to-all-start = ((bf16[32,16,128]{2,1,0:T(8,128)(2,1)}), bf16[32,16,128]{2,1,0:T(8,128)(2,1)S(1)}, u32[]{:S(2)}, u32[]{:S(2)}) async-start(bf16[32,16,128]{2,1,0:T(8,128)(2,1)} %get-tuple-element.20), calls=%async_computation | async-start | bytes 262144 | tf_op jit(solution)/shard_map/all_to_all | solution.py:817
  9.9 0.7 copy-start.17
  9.9 0.7 copy-start.18
  9.9 0.7 copy-start.19
  9.9 0.7 copy-start.15
  10.0 0.7 copy-start.16
  10.7 1.0 %copy-start.3 = (bf16[256,768]{1,0:T(8,128)(2,1)S(1)}, bf16[256,768]{1,0:T(8,128)(2,1)}, u32[]{:S(2)}) copy-start(bf16[256,768]{1,0:T(8,128)(2,1)} %refs_3_.5) | copy-start | bytes 1179652
  11.7 6.4 %copy-start.11 = (bf16[256,256]{1,0:T(8,128)(2,1)S(1)}, bf16[256,256]{1,0:T(8,128)(2,1)}, u32[]{:S(2)}) copy-start(bf16[256,256]{1,0:T(8,128)(2,1)} %refs_6_.2) | copy-start | bytes 393220
  18.1 4.9 %copy-start.13 = (bf16[1024,128]{1,0:T(8,128)(2,1)S(1)}, bf16[1024,128]{1,0:T(8,128)(2,1)}, u32[]{:S(2)}) copy-start(bf16[1024,128]{1,0:T(8,128)(2,1)} %param.38) | copy-start | bytes 786436
  20.4 10.0 %all-to-all-start.1 = ((bf16[32,8,128]{2,1,0:T(8,128)(2,1)}), bf16[32,8,128]{2,1,0:T(8,128)(2,1)S(1)}, u32[]{:S(2)}, u32[]{:S(2)}) async-start(bf16[32,8,128]{2,1,0:T(8,128)(2,1)} %shard_map.223), calls=%async_computation.1 | async-start | bytes 131072 | tf_op jit(solution)/shard_map/all_to_all | solution.py:855
  23.0 7.4 %copy-start.9 = (bf16[256,256]{1,0:T(8,128)(2,1)S(1)}, bf16[256,256]{1,0:T(8,128)(2,1)}, u32[]{:S(2)}) copy-start(bf16[256,256]{1,0:T(8,128)(2,1)} %refs_5_.2) | copy-start | bytes 393220
  23.0 7.4 %copy-start.12 = (bf16[256,64]{0,1:T(8,128)(2,1)S(1)}, bf16[256,64]{0,1:T(8,128)(2,1)}, u32[]{:S(2)}) copy-start(bf16[256,64]{0,1:T(8,128)(2,1)} %param.37) | copy-start | bytes 98308
  23.1 7.3 %copy-start.4 = (bf16[256,768]{1,0:T(8,128)(2,1)S(1)}, bf16[256,768]{1,0:T(8,128)(2,1)}, u32[]{:S(2)}) copy-start(bf16[256,768]{1,0:T(8,128)(2,1)} %refs_4_.2) | copy-start | bytes 1179652
  23.1 7.3 %copy-start.8 = (bf16[256,256]{1,0:T(8,128)(2,1)S(1)}, bf16[256,256]{1,0:T(8,128)(2,1)}, u32[]{:S(2)}) copy-start(bf16[256,256]{1,0:T(8,128)(2,1)} %refs_3_.6) | copy-start | bytes 393220
  32.8 3.7 %copy-start.14 = (bf16[1,128,128]{2,1,0:T(8,128)(2,1)S(1)}, bf16[1,128,128]{2,1,0:T(8,128)(2,1)}, u32[]{:S(2)}) copy-start(bf16[1,128,128]{2,1,0:T(8,128)(2,1)} %get-tuple-element.27) | copy-start | bytes 98308
  32.8 15.4 %all-to-all-start.2 = ((bf16[16,64,128]{2,1,0:T(8,128)(2,1)}), bf16[16,64,128]{2,1,0:T(8,128)(2,1)S(1)}, u32[]{:S(2)}, u32[]{:S(2)}) async-start(bf16[16,64,128]{2,1,0:T(8,128)(2,1)} %get-tuple-element.26), calls=%async_computation.2 | async-start | bytes 524288 | tf_op jit(solution)/shard_map/all_to_all | solution.py:877
  36.5 21.5 %copy-start = (bf16[2,128,512]{2,1,0:T(8,128)(2,1)S(1)}, bf16[2,128,512]{2,1,0:T(8,128)(2,1)}, u32[]{:S(2)}) copy-start(bf16[2,128,512]{2,1,0:T(8,128)(2,1)} %refs_7_.1) | copy-start | bytes 786436
  36.5 12.1 %collective-permute-start.3 = (bf16[1,128,128]{2,1,0:T(8,128)(2,1)S(1)}, bf16[1,128,128]{2,1,0:T(8,128)(2,1)S(1)}, u32[]{:S(2)}, u32[]{:S(2)}) collective-permute-start(bf16[1,128,128]{2,1,0:T(8,128)(2,1)S(1)} %copy-done.14), channel_id=1, source_target_pairs={{0,24},{1,25},{2,26},{3,27},{4,28},{5,29},{6,30},{7,31},{8,16},{9,... | collective-permute-start | bytes 98312 | tf_op jit(solution)/shard_map/ppermute | solution.py:755
  40.2 8.3 %collective-permute-start.2 = (bf16[1,128,128]{2,1,0:T(8,128)(2,1)S(1)}, bf16[1,128,128]{2,1,0:T(8,128)(2,1)S(1)}, u32[]{:S(2)}, u32[]{:S(2)}) collective-permute-start(bf16[1,128,128]{2,1,0:T(8,128)(2,1)S(1)} %copy-done.14), channel_id=1, source_target_pairs={{0,16},{1,17},{2,18},{3,19},{4,20},{5,21},{6,22},{7,23},{8,24},{9,... | collective-permute-start | bytes 98312 | tf_op jit(solution)/shard_map/ppermute | solution.py:755
  40.2 4.1 %collective-permute-start.1 = (bf16[1,128,128]{2,1,0:T(8,128)(2,1)S(1)}, bf16[1,128,128]{2,1,0:T(8,128)(2,1)S(1)}, u32[]{:S(2)}, u32[]{:S(2)}) collective-permute-start(bf16[1,128,128]{2,1,0:T(8,128)(2,1)S(1)} %copy-done.14), channel_id=1, source_target_pairs={{0,8},{1,9},{2,10},{3,11},{4,12},{5,13},{6,14},{7,15},{8,0},{9,1},... | collective-permute-start | bytes 98312 | tf_op jit(solution)/shard_map/ppermute | solution.py:755
  48.2 9.8 %collective-permute-start = (bf16[16,64,128]{2,1,0:T(8,128)(2,1)S(1)}, bf16[16,64,128]{2,1,0:T(8,128)(2,1)S(1)}, u32[]{:S(2)}, u32[]{:S(2)}) collective-permute-start(bf16[16,64,128]{2,1,0:T(8,128)(2,1)S(1)} %all-to-all-done.2.refs_0_), channel_id=1, source_target_pairs={{0,1},{1,0},{2,3},{3,2},{4,5},{5,4},{6,7},{7,6},{8,9},{9,8},{10,11... | collective-permute-start | bytes 786440 | tf_op jit(solution)/shard_map/ppermute | solution.py:880
  48.6 7.4 %collective-permute-start.6 = (bf16[4,128,128]{2,1,0:T(8,128)(2,1)S(1)}, bf16[4,128,128]{2,1,0:T(8,128)(2,1)S(1)}, u32[]{:S(2)}, u32[]{:S(2)}) collective-permute-start(bf16[4,128,128]{2,1,0:T(8,128)(2,1)S(1)} %constant_dynamic-update-slice_fusion.refs_2_), channel_id=1, source_target_pairs={{0,6},{1,7},{2,4},{3,5},{4,2},{5,3},{6,0},{7,1},{8,14},{9,15},{10,... | collective-permute-start | bytes 393224 | tf_op jit(solution)/shard_map/ppermute | solution.py:755
  51.0 6.9 %collective-permute-start.5 = (bf16[4,128,128]{2,1,0:T(8,128)(2,1)S(1)}, bf16[4,128,128]{2,1,0:T(8,128)(2,1)S(1)}, u32[]{:S(2)}, u32[]{:S(2)}) collective-permute-start(bf16[4,128,128]{2,1,0:T(8,128)(2,1)S(1)} %constant_dynamic-update-slice_fusion.refs_2_), channel_id=1, source_target_pairs={{0,4},{1,5},{2,6},{3,7},{4,0},{5,1},{6,2},{7,3},{8,12},{9,13},{10,... | collective-permute-start | bytes 393224 | tf_op jit(solution)/shard_map/ppermute | solution.py:755
  51.6 6.4 %collective-permute-start.4 = (bf16[4,128,128]{2,1,0:T(8,128)(2,1)S(1)}, bf16[4,128,128]{2,1,0:T(8,128)(2,1)S(1)}, u32[]{:S(2)}, u32[]{:S(2)}) collective-permute-start(bf16[4,128,128]{2,1,0:T(8,128)(2,1)S(1)} %constant_dynamic-update-slice_fusion.refs_2_), channel_id=1, source_target_pairs={{0,2},{1,3},{2,0},{3,1},{4,6},{5,7},{6,4},{7,5},{8,10},{9,11},{10,... | collective-permute-start | bytes 393224 | tf_op jit(solution)/shard_map/ppermute | solution.py:755
  52.2 9.3 %copy-start.1 = (f32[64,2,256]{2,1,0:T(2,128)}, f32[64,2,256]{2,1,0:T(2,128)S(1)}, u32[]{:S(2)}) copy-start(f32[64,2,256]{2,1,0:T(2,128)S(1)} %reshape.54.refs_10_) | copy-start | bytes 393220
  52.2 9.4 %copy-start.7 = (bf16[2,128,128]{2,1,0:T(8,128)(2,1)S(1)}, bf16[2,128,128]{2,1,0:T(8,128)(2,1)}, u32[]{:S(2)}) copy-start(bf16[2,128,128]{2,1,0:T(8,128)(2,1)} %refs_4_.3) | copy-start | bytes 196612
  61.5 2.0 %collective-permute-start.7 = (bf16[16,128,128]{2,1,0:T(8,128)(2,1)S(1)}, bf16[16,128,128]{2,1,0:T(8,128)(2,1)S(1)}, u32[]{:S(2)}, u32[]{:S(2)}) collective-permute-start(bf16[16,128,128]{2,1,0:T(8,128)(2,1)S(1)} %get-tuple-element.32.refs_3_), channel_id=1, source_target_pairs={{0,1},{1,0},{2,3},{3,2},{4,5},{5,4},{6,7},{7,6},{8,9},{9,8},{10,11... | collective-permute-start | bytes 1572872 | tf_op jit(solution)/shard_map/ppermute | solution.py:906
  61.6 1.9 %copy-start.5 = (bf16[2,128,128]{2,1,0:T(8,128)(2,1)S(1)}, bf16[2,128,128]{2,1,0:T(8,128)(2,1)}, u32[]{:S(2)}) copy-start(bf16[2,128,128]{2,1,0:T(8,128)(2,1)} %refs_5_.3) | copy-start | bytes 196612
  63.5 4.3 %copy-start.6 = (f32[2,64,128]{2,1,0:T(8,128)S(1)}, f32[2,64,128]{2,1,0:T(8,128)}, u32[]{:S(2)}) copy-start(f32[2,64,128]{2,1,0:T(8,128)} %param.23) | copy-start | bytes 196612
  67.6 2.1 %collective-permute-start.8 = (bf16[16,144,128]{2,1,0:T(8,128)(2,1)S(1)}, bf16[16,144,128]{2,1,0:T(8,128)(2,1)S(1)}, u32[]{:S(2)}, u32[]{:S(2)}) collective-permute-start(bf16[16,144,128]{2,1,0:T(8,128)(2,1)S(1)} %get-tuple-element.33.refs_0_), channel_id=1, source_target_pairs={{0,1},{1,0},{2,3},{3,2},{4,5},{5,4},{6,7},{7,6},{8,9},{9,8},{10,11... | collective-permute-start | bytes 1769480 | tf_op jit(solution)/shard_map/ppermute | solution.py:935

commit v6 on v5

--- a/solution.py
+++ b/solution.py
@@ -570,7 +570,22 @@
             right_ref[chip] = jnp.transpose(right[rows]).astype(jnp.bfloat16)
 
 
-def left_body(normed_ref, small_ref, flank_ref, switch_ref, left_ref, gate_ref, mkeys):
+def by_channel(ref, base, chips, channels):
+    rows = [
+        ref[pl.ds(pl.multiple_of(chip * channels + base, 8), 8), :] for chip in range(chips)
+    ]
+    return jnp.swapaxes(jnp.stack(rows), 0, 1)
+
+
+def both_turns(rows):
+    return jnp.concatenate([rows, pltpu.roll(rows, rows.shape[1] // 2, 1)], axis=0)
+
+
+def left_body(
+    normed_ref, own_ref, small_ref, flank_ref, switch_ref,
+    lhs_ref, rhs_ref, gate_ref,
+    left_ref, side, mkeys,
+):
     chips, lanes, channels = gate_ref.shape
     half = lanes // 2
     parity = lax.rem(lax.axis_index("dap"), 2)
@@ -590,58 +605,50 @@
             rows = slice(c * lanes, (c + 1) * lanes)
             gate_ref[chip] = gate[rows]
             left_ref[chip * channels : (chip + 1) * channels, :] = jnp.transpose(left[rows])
+            side[chip * channels : (chip + 1) * channels, :] = own_ref[chip].astype(jnp.float32)
+    low = lane_iota((chips, lanes)) < half
+    per_step = 64
+
+    @pl.loop(0, channels // per_step)
+    def _(step):
+        for o in range(per_step // 8):
+            base = step * per_step + o * 8
+            left = by_channel(left_ref, base, chips, channels)
+            own = by_channel(side, base, chips, channels)
+            for c in range(8):
+                lhs = jnp.concatenate(
+                    [jnp.where(low, left[c], 0.0), jnp.where(low, 0.0, left[c])], axis=0
+                )
+                to = pl.ds(pl.multiple_of((base + c) * 2 * chips, 2 * chips), 2 * chips)
+                lhs_ref[to, :] = lhs.astype(jnp.bfloat16)
+                rhs_ref[to, :] = both_turns(own[c]).astype(jnp.bfloat16)
 
 
 def outgoing_body(
-    pair_one_ref, left_ref, gate_ref, own_ref, oth_ref, small_ref, final_ref, flank_ref,
+    pair_one_ref, lhs_ref, rhs_ref, gate_ref, oth_ref, small_ref, final_ref, flank_ref,
     two_ref, send_ref,
-    sides, prods, mkeys, pair_two, rows_out, cols,
+    side, prods, mkeys, pair_two, rows_out, cols,
 ):
-    chips, channels, lanes = own_ref.shape
+    chips, channels, lanes = oth_ref.shape
     half = lanes // 2
     me = lax.axis_index("dap")
     parity = lax.rem(me, 2)
     my_chip = me // 2
-    flag = jnp.broadcast_to(parity, (1, 1)) == 0
-
-    @pl.loop(0, chips)
-    def _(chip):
-        own = own_ref[chip].astype(jnp.float32)
-        oth = oth_ref[chip].astype(jnp.float32)
-        rows = pl.ds(pl.multiple_of(chip * channels, channels), channels)
-        sides[0, rows, :] = jnp.where(flag, own, oth)
-        sides[1, rows, :] = jnp.where(flag, oth, own)
-
-    low = lane_iota((chips, lanes)) < half
-
+
+    side[...] = oth_ref[...].astype(jnp.float32).reshape(side.shape)
     per_step = 64
 
     @pl.loop(0, channels // per_step)
     def _(step):
         for o in range(per_step // 8):
             base = step * per_step + o * 8
-            left, even, odd = (
-                jnp.swapaxes(
-                    jnp.stack(
-                        [
-                            ref[pl.ds(pl.multiple_of(chip * channels + base, 8), 8), :]
-                            for chip in range(chips)
-                        ]
-                    ),
-                    0,
-                    1,
+            oth = by_channel(side, base, chips, channels)
+            for c in range(8):
+                at = pl.ds(pl.multiple_of((base + c) * 2 * chips, 2 * chips), 2 * chips)
+                rhs = jnp.concatenate(
+                    [rhs_ref[at, :], both_turns(oth[c]).astype(jnp.bfloat16)], axis=0
                 )
-                for ref in (left_ref, sides.at[0], sides.at[1])
-            )
-            for c in range(8):
-                lhs = jnp.concatenate(
-                    [jnp.where(low, left[c], 0.0), jnp.where(low, 0.0, left[c])], axis=0
-                )
-                rhs = jnp.concatenate(
-                    [even[c], pltpu.roll(even[c], half, 1), odd[c], pltpu.roll(odd[c], half, 1)],
-                    axis=0,
-                )
-                out = dot_nt(lhs.astype(jnp.bfloat16), rhs.astype(jnp.bfloat16))
+                out = dot_nt(lhs_ref[at, :], rhs)
                 out = jnp.concatenate([out[:chips], out[chips:]], axis=1)
                 to = pl.ds(base + c, chips, stride=channels)
                 prods[to, :] = out.astype(jnp.bfloat16).astype(jnp.float32)
@@ -654,7 +661,7 @@
     flank_right = flank_ref[1, :, 2 * channels :]
     flank_left = flank_ref[1, :, : 2 * channels]
     octet = pl.multiple_of(8 * (my_chip // 2), 8)
-    group = 8
+    group = 16
     for block in range(chips // group):
         changed = []
         for c in range(group):
@@ -666,7 +673,8 @@
         for c in range(group):
             part = jnp.transpose(changed[:, c * lanes : (c + 1) * lanes])
             for k in range(8):
-                r, p = k // 4, (k // 2) % 2
+                r = k // 4
+                p = 1 - parity if (k // 2) % 2 else parity
                 rj = k % 2 if r == 0 else 1 - k % 2
                 rows_out[block * group + c, pl.ds(r * half + 2 * p + rj, chips, stride=4), :] = part[
                     k * chips : (k + 1) * chips
@@ -754,8 +762,9 @@
     def fetch(value, apart):
         return lax.ppermute(value, "dap", [(d, d ^ (2 * apart)) for d in range(devices)])
 
-    parts = [fetch(block, h * steps) for h in range(1, chips // steps)]
-    near = jnp.concatenate([block] + parts, axis=0)
+    near = block
+    while near.shape[0] < chips // steps:
+        near = jnp.concatenate([near, fetch(near, near.shape[0] * steps)], axis=0)
     return near, [fetch(near, k) for k in range(1, steps)]
 
 
@@ -904,29 +913,34 @@
         msa,
     )
     right_oth = lax.ppermute(right_own, "dap", swap)
-    left, gate = vmem_call(
+    by_channels = shape((channels * 2 * chips, lanes), bf16)
+    lhs, rhs, gate = vmem_call(
         left_body,
-        (shape((chips * channels, lanes), f32), shape(stack, f32)),
-        scratch=[pltpu.VMEM((aminos, channels), f32)],
-        count=4,
-    )(normed, small, trio_flank_mappings, trio_final_switches)
+        (by_channels, by_channels, shape(stack, f32)),
+        scratch=[
+            pltpu.VMEM((chips * channels, lanes), f32),
+            pltpu.VMEM((chips * channels, lanes), f32),
+            pltpu.VMEM((aminos, channels), f32),
+        ],
+        count=5,
+    )(normed, right_own, small, trio_flank_mappings, trio_final_switches)
     two, going = vmem_call(
         outgoing_body,
         (shape((lanes, channels), f32), shape((chips, lanes + 16, channels), bf16)),
         scratch=[
-            pltpu.VMEM((2, chips * channels, lanes), f32),
+            pltpu.VMEM((chips * channels, lanes), f32),
             pltpu.VMEM((channels * chips, lanes), f32),
             pltpu.VMEM((aminos, channels), f32),
             pltpu.VMEM(stack, f32),
             pltpu.VMEM(stack, f32),
-            pltpu.VMEM((chips // 8, 8 * lanes, channels), f32),
+            pltpu.VMEM((chips // 16, 16 * lanes, channels), f32),
         ],
         count=8,
     )(
         pair_one,
-        left,
+        lhs,
+        rhs,
         gate,
-        right_own,
         right_oth,
         small,
         trio_final_matrices,

time: 71.3 us -> 71.4 us (level)
  waiting for transfers between devices: 29 us -> 28.1 us
  starting transfers between devices: 21.8 us -> 22.6 us
    all_to_all x1, waiting for transfers between devices: 3.86 us -> 0.21 us  [paired_shards(): lax.all_to_all(opm, 'dap', split_axis=0, concat_axis=0, tiled=True, axis_...]
    ppermute x6 -> x5, waiting for transfers between devices: 9.45 us -> 12.8 us  [fetch(): lax.ppermute(value, 'dap', [(d, d ^ 2 * apart) for d in range(devices)])]
    ppermute x6 -> x5, starting transfers between devices: 8.01 us -> 8.76 us  [fetch(): lax.ppermute(value, 'dap', [(d, d ^ 2 * apart) for d in range(devices)])]
    unnamed x45 -> x44, local copies, waits for them, and re-layouts: 1.79 us -> 1.78 us
  transfers between devices with their start and end apart: 12 -> 11, of which waited for: 10 -> 10; matrix products, arithmetic and copies ran while one was open for 1% -> 1% of each run, Pallas kernels for 2% -> 3%
where the time goes in v6:
time: 71.4 us; the launch traced here: 70.9 us
  waiting for transfers between devices  28.1 us (39%)
  starting transfers between devices  22.6 us (32%)
  Pallas kernels  17.1 us (24%)
  local copies, waits for them, and re-layouts  2.17 us (3%)
  between operations  0.96 us (1%)
    ppermute x5, waiting for transfers between devices, fetch(): lax.ppermute(value, 'dap', [(d, d ^ 2 * apart) for d in range(devices)])  12.8 us
    ppermute x5, starting transfers between devices, fetch(): lax.ppermute(value, 'dap', [(d, d ^ 2 * apart) for d in range(devices)])  8.76 us
    all_to_all x1, starting transfers between devices, paired_shards(): lax.all_to_all(block, 'dap', split_axis=0, concat_axis=0, tiled=True)  7.33 us
    all_to_all x1, waiting for transfers between devices, paired_shards(): lax.all_to_all(sent, 'dap', split_axis=0, concat_axis=0, tiled=True)  7.08 us
    all_to_all x1, waiting for transfers between devices, paired_shards(): lax.all_to_all(block, 'dap', split_axis=0, concat_axis=0, tiled=True)  6 us
    pallas_call x1, Pallas kernels, paired_shards(): vmem_call(outgoing_body, (shape((lanes, channels), f32), shape((chips, la...  3.67 us
    all_to_all x1, starting transfers between devices, paired_shards(): lax.all_to_all(opm, 'dap', split_axis=0, concat_axis=0, tiled=True, axis_...  3.66 us
    pallas_call x1, Pallas kernels, paired_shards(): vmem_call(functools.partial(opm_body, len(couples)), (shape(stack, f32),...  3.57 us
  transfers between devices with their start and end apart: 11, of which 10 were waited for; matrix products, arithmetic and copies ran while one was open for 1% of the time, Pallas kernels for 3%

profile of v6, /device:TPU:0, one launch (start us, length us, event | category | flops | bytes accessed | tf_op | source)
XLA Modules:
  0.0 70.9 jit_solution(4071132706361683488)
XLA Ops:
  0.6 1.9 %shard_map.221 = (bf16[32,16,128]{2,1,0:T(8,128)(2,1)}, bf16[1,128,128]{2,1,0:T(8,128)(2,1)}) custom-call(f32[128,128]{1,0:T(8,128)} %bitcast.19, f32[1,128]{1,0:T(1,128)} %bitcast.31, bf16[8,128]{1,0:T(8,128)(2,1)} %bitcast.25, s32[2,64]{1,0:T(2,128)} %refs_3_.4), custom_call_target="tpu_custom_call" | custom-call | tf_op jit(solution)/shard_map/pallas_call | solution.py:812
  2.5 0.0 copy-start.2
  2.5 0.0 copy-start.10
  2.5 7.3 %all-to-all-start = ((bf16[32,16,128]{2,1,0:T(8,128)(2,1)}), bf16[32,16,128]{2,1,0:T(8,128)(2,1)S(1)}, u32[]{:S(2)}, u32[]{:S(2)}) async-start(bf16[32,16,128]{2,1,0:T(8,128)(2,1)} %get-tuple-element.21), calls=%async_computation | async-start | bytes 262144 | tf_op jit(solution)/shard_map/all_to_all | solution.py:826
  9.9 0.0 copy-start.17
  9.9 0.0 copy-start.18
  9.9 0.0 copy-start.19
  9.9 0.0 copy-start.15
  10.0 0.6 copy-done.17
  10.6 0.0 copy-done.18
  10.6 0.0 copy-done.19
  10.6 0.0 copy-done.15
  10.6 0.0 copy-done.16
  10.7 1.0 %copy-done.3 = bf16[256,768]{1,0:T(8,128)(2,1)S(1)} copy-done((bf16[256,768]{1,0:T(8,128)(2,1)S(1)}, bf16[256,768]{1,0:T(8,128)(2,1)}, u32[]{:S(2)}) %copy-start.3) | copy-done | bytes 393240
  11.7 0.4 shard_map.222
  12.1 6.0 %all-to-all-done.refs_0_.refs_1_.refs_6_ = bf16[32,16,128]{2,1,0:T(8,128)(2,1)S(1)} async-done(((bf16[32,16,128]{2,1,0:T(8,128)(2,1)}), bf16[32,16,128]{2,1,0:T(8,128)(2,1)S(1)}, u32[]{:S(2)}, u32[]{:S(2)}) %all-to-all-start) | async-done | bytes 131104 | tf_op jit(solution)/shard_map/all_to_all | solution.py:826
  18.1 2.3 %shard_map.223 = bf16[32,8,128]{2,1,0:T(8,128)(2,1)} custom-call(bf16[32,16,128]{2,1,0:T(8,128)(2,1)S(1)} %all-to-all-done.refs_0_.refs_1_.refs_6_, f32[128,256]{1,0:T(8,128)S(1)} %bitcast.18, f32[2,128,128]{2,1,0:T(8,128)S(1)} %get-tuple-element.22.refs_2_, bf16[128,256]{1,0:T(8,128)(2,1)S(1)} %get-tuple-element.23.refs_3_, ...), custom_call_target="tpu_custom_call" | custom-call | tf_op jit(solution)/shard_map/pallas_call | solution.py:854
  20.4 2.6 %all-to-all-start.1 = ((bf16[32,8,128]{2,1,0:T(8,128)(2,1)}), bf16[32,8,128]{2,1,0:T(8,128)(2,1)S(1)}, u32[]{:S(2)}, u32[]{:S(2)}) async-start(bf16[32,8,128]{2,1,0:T(8,128)(2,1)} %shard_map.223), calls=%async_computation.1 | async-start | bytes 131072 | tf_op jit(solution)/shard_map/all_to_all | solution.py:864
  23.0 0.0 copy-start.9
  23.0 0.0 copy-start.12
  23.0 0.1 copy.27
  23.1 0.1 copy.28.refs_7_
  23.3 7.1 %all-to-all-done.1.refs_0_ = bf16[32,8,128]{2,1,0:T(8,128)(2,1)S(1)} async-done(((bf16[32,8,128]{2,1,0:T(8,128)(2,1)}), bf16[32,8,128]{2,1,0:T(8,128)(2,1)S(1)}, u32[]{:S(2)}, u32[]{:S(2)}) %all-to-all-start.1) | async-done | bytes 65568 | tf_op jit(solution)/shard_map/all_to_all | solution.py:864
  30.4 2.4 %shard_map.224 = (f32[64,512]{1,0:T(8,128)S(1)}, bf16[16,64,128]{2,1,0:T(8,128)(2,1)}) custom-call(bf16[32,8,128]{2,1,0:T(8,128)(2,1)S(1)} %all-to-all-done.1.refs_0_, bf16[32,16,128]{2,1,0:T(8,128)(2,1)S(1)} %all-to-all-done.refs_0_.refs_1_.refs_6_, f32[8,256]{1,0:T(8,128)S(1)} %concatenate.10.refs_1_.refs_2_.refs_8_.refs_5_.refs_3_.refs_4_, ...), custom_call_target="tpu_custom_call" | custom-call | tf_op jit(solution)/shard_map/pallas_call | solution.py:865
  32.8 3.7 %all-to-all-start.2 = ((bf16[16,64,128]{2,1,0:T(8,128)(2,1)}), bf16[16,64,128]{2,1,0:T(8,128)(2,1)S(1)}, u32[]{:S(2)}, u32[]{:S(2)}) async-start(bf16[16,64,128]{2,1,0:T(8,128)(2,1)} %get-tuple-element.27), calls=%async_computation.2 | async-start | bytes 524288 | tf_op jit(solution)/shard_map/all_to_all | solution.py:886
  36.5 1.9 %collective-permute-start.1 = (bf16[1,128,128]{2,1,0:T(8,128)(2,1)S(1)}, bf16[1,128,128]{2,1,0:T(8,128)(2,1)S(1)}, u32[]{:S(2)}, u32[]{:S(2)}) collective-permute-start(bf16[1,128,128]{2,1,0:T(8,128)(2,1)S(1)} %copy-done.14), channel_id=1, source_target_pairs={{0,8},{1,9},{2,10},{3,11},{4,12},{5,13},{6,14},{7,15},{8,0},{9,1},... | collective-permute-start | bytes 98312 | tf_op jit(solution)/shard_map/ppermute | solution.py:763
  38.4 4.9 %collective-permute-done.1 = bf16[1,128,128]{2,1,0:T(8,128)(2,1)S(1)} collective-permute-done((bf16[1,128,128]{2,1,0:T(8,128)(2,1)S(1)}, bf16[1,128,128]{2,1,0:T(8,128)(2,1)S(1)}, u32[]{:S(2)}, u32[]{:S(2)}) %collective-permute-start.1) | collective-permute-done | bytes 32800 | tf_op jit(solution)/shard_map/ppermute | solution.py:763
  43.3 3.3 %collective-permute-start.2 = (bf16[2,128,128]{2,1,0:T(8,128)(2,1)S(1)}, bf16[2,128,128]{2,1,0:T(8,128)(2,1)S(1)}, u32[]{:S(2)}, u32[]{:S(2)}) collective-permute-start(bf16[2,128,128]{2,1,0:T(8,128)(2,1)S(1)} %pad_maximum_fusion), channel_id=1, source_target_pairs={{0,16},{1,17},{2,18},{3,19},{4,20},{5,21},{6,22},{7,23},{8,24},{9,... | collective-permute-start | bytes 196616 | tf_op jit(solution)/shard_map/ppermute | solution.py:763
  46.6 0.2 all-to-all-done.2.refs_0_
  46.8 2.7 %collective-permute-done.2 = bf16[2,128,128]{2,1,0:T(8,128)(2,1)S(1)} collective-permute-done((bf16[2,128,128]{2,1,0:T(8,128)(2,1)S(1)}, bf16[2,128,128]{2,1,0:T(8,128)(2,1)S(1)}, u32[]{:S(2)}, u32[]{:S(2)}) %collective-permute-start.2) | collective-permute-done | bytes 65568 | tf_op jit(solution)/shard_map/ppermute | solution.py:763
  49.6 1.5 %collective-permute-start.3 = (bf16[4,128,128]{2,1,0:T(8,128)(2,1)S(1)}, bf16[4,128,128]{2,1,0:T(8,128)(2,1)S(1)}, u32[]{:S(2)}, u32[]{:S(2)}) collective-permute-start(bf16[4,128,128]{2,1,0:T(8,128)(2,1)S(1)} %constant_dynamic-update-slice_fusion.refs_2_), channel_id=1, source_target_pairs={{0,2},{1,3},{2,0},{3,1},{4,6},{5,7},{6,4},{7,5},{8,10},{9,11},{10,... | collective-permute-start | bytes 393224 | tf_op jit(solution)/shard_map/ppermute | solution.py:763
  51.1 1.5 %collective-permute-start.4 = (bf16[4,128,128]{2,1,0:T(8,128)(2,1)S(1)}, bf16[4,128,128]{2,1,0:T(8,128)(2,1)S(1)}, u32[]{:S(2)}, u32[]{:S(2)}) collective-permute-start(bf16[4,128,128]{2,1,0:T(8,128)(2,1)S(1)} %constant_dynamic-update-slice_fusion.refs_2_), channel_id=1, source_target_pairs={{0,4},{1,5},{2,6},{3,7},{4,0},{5,1},{6,2},{7,3},{8,12},{9,13},{10,... | collective-permute-start | bytes 393224 | tf_op jit(solution)/shard_map/ppermute | solution.py:763
  52.6 0.5 collective-permute-start.5
  53.1 0.1 reshape.54.refs_10_
  53.2 0.0 copy-start.7
  53.2 2.6 %collective-permute-done.3.refs_3_ = bf16[4,128,128]{2,1,0:T(8,128)(2,1)S(1)} collective-permute-done((bf16[4,128,128]{2,1,0:T(8,128)(2,1)S(1)}, bf16[4,128,128]{2,1,0:T(8,128)(2,1)S(1)}, u32[]{:S(2)}, u32[]{:S(2)}) %collective-permute-start.3) | collective-permute-done | bytes 131104 | tf_op jit(solution)/shard_map/ppermute | solution.py:763
  55.8 1.2 %collective-permute-done.4.refs_4_ = bf16[4,128,128]{2,1,0:T(8,128)(2,1)S(1)} collective-permute-done((bf16[4,128,128]{2,1,0:T(8,128)(2,1)S(1)}, bf16[4,128,128]{2,1,0:T(8,128)(2,1)S(1)}, u32[]{:S(2)}, u32[]{:S(2)}) %collective-permute-start.4) | collective-permute-done | bytes 131104 | tf_op jit(solution)/shard_map/ppermute | solution.py:763
  57.0 1.5 %collective-permute-done.5.refs_5_ = bf16[4,128,128]{2,1,0:T(8,128)(2,1)S(1)} collective-permute-done((bf16[4,128,128]{2,1,0:T(8,128)(2,1)S(1)}, bf16[4,128,128]{2,1,0:T(8,128)(2,1)S(1)}, u32[]{:S(2)}, u32[]{:S(2)}) %collective-permute-start.5) | collective-permute-done | bytes 131104 | tf_op jit(solution)/shard_map/ppermute | solution.py:763
  58.5 3.6 %shard_map.225 = (f32[16,128,128]{2,1,0:T(8,128)S(1)}, bf16[16,128,128]{2,1,0:T(8,128)(2,1)S(1)}, bf16[16,128,128]{2,1,0:T(8,128)(2,1)S(1)}) custom-call(bf16[16,64,128]{2,1,0:T(8,128)(2,1)S(1)} %all-to-all-done.2.refs_0_, bf16[16,64,128]{2,1,0:T(8,128)(2,1)S(1)} %collective-permute-done.refs_1_, ...), custom_call_target="tpu_custom_call" | custom-call | tf_op jit(solution)/shard_map/pallas_call | solution.py:892
  62.0 0.1 collective-permute-start.6
  62.1 0.0 copy-start.5
  62.1 1.3 %shard_map.226 = (bf16[4096,128]{1,0:T(8,128)(2,1)S(1)}, bf16[4096,128]{1,0:T(8,128)(2,1)S(1)}, f32[16,128,128]{2,1,0:T(8,128)S(1)}) custom-call(bf16[16,128,128]{2,1,0:T(8,128)(2,1)S(1)} %get-tuple-element.30.refs_0_, bf16[16,128,128]{2,1,0:T(8,128)(2,1)S(1)} %get-tuple-element.31.refs_1_, ...), custom_call_target="tpu_custom_call" | custom-call | tf_op jit(solution)/shard_map/pallas_call | solution.py:917
  63.4 0.6 collective-permute-done.6.refs_4_
  64.0 3.7 %shard_map.227 = (f32[128,128]{1,0:T(8,128)S(1)}, bf16[16,144,128]{2,1,0:T(8,128)(2,1)S(1)}) custom-call(f32[16,128,128]{2,1,0:T(8,128)S(1)} %get-tuple-element.29.refs_0_, bf16[4096,128]{1,0:T(8,128)(2,1)S(1)} %get-tuple-element.32.refs_1_, bf16[4096,128]{1,0:T(8,128)(2,1)S(1)} %get-tuple-element.33.refs_2_, f32[16,128,128]{2,1,0:T(8,128)S(1)} %get-tuple-element.34.refs_3_, ...), custom_call_target="tpu_custom_call" | custom-call | tf_op jit(solution)/shard_map/pallas_call | solution.py:927
  67.7 0.2 collective-permute-start.7
  67.9 0.5 shard_map.228
  68.4 1.4 %collective-permute-done.7.refs_0_ = bf16[16,144,128]{2,1,0:T(8,128)(2,1)S(1)} collective-permute-done((bf16[16,144,128]{2,1,0:T(8,128)(2,1)S(1)}, bf16[16,144,128]{2,1,0:T(8,128)(2,1)S(1)}, u32[]{:S(2)}, u32[]{:S(2)}) %collective-permute-start.7) | collective-permute-done | bytes 589856 | tf_op jit(solution)/shard_map/ppermute | solution.py:949
  69.8 1.1 %shard_map.229 = f32[128,128]{1,0:T(8,128)} custom-call(bf16[16,144,128]{2,1,0:T(8,128)(2,1)S(1)} %collective-permute-done.7.refs_0_, f32[128,128]{1,0:T(8,128)S(1)} %get-tuple-element.37.refs_1_, f32[128,128]{1,0:T(8,128)S(1)} %get-tuple-element.38.refs_2_, f32[128,128]{1,0:T(8,128)S(1)} %get-tuple-element.39.refs_3_, ...), custom_call_target="tpu_custom_call" | custom-call | tf_op jit(solution)/shard_map/pallas_call | solution.py:955
  (36 shorter events, 0.1 us)
Async XLA Ops:
  0.6 9.2 %copy-start.20 = (s32[64]{0:T(128)S(1)}, s32[64]{0:T(128)}, u32[]{:S(2)}) copy-start(s32[64]{0:T(128)} %param.25) | copy-start | bytes 772
  2.5 8.2 %copy-start.2 = (f32[2,64,256]{2,1,0:T(8,128)S(1)}, f32[2,64,256]{2,1,0:T(8,128)}, u32[]{:S(2)}) copy-start(f32[2,64,256]{2,1,0:T(8,128)} %param.22) | copy-start | bytes 393220
  2.5 8.2 %copy-start.10 = (bf16[256,256]{1,0:T(8,128)(2,1)S(1)}, bf16[256,256]{1,0:T(8,128)(2,1)}, u32[]{:S(2)}) copy-start(bf16[256,256]{1,0:T(8,128)(2,1)} %refs_2_.1) | copy-start | bytes 393220
  2.5 15.5 %all-to-all-start = ((bf16[32,16,128]{2,1,0:T(8,128)(2,1)}), bf16[32,16,128]{2,1,0:T(8,128)(2,1)S(1)}, u32[]{:S(2)}, u32[]{:S(2)}) async-start(bf16[32,16,128]{2,1,0:T(8,128)(2,1)} %get-tuple-element.21), calls=%async_computation | async-start | bytes 262144 | tf_op jit(solution)/shard_map/all_to_all | solution.py:826
  9.9 0.7 copy-start.17
  9.9 0.7 copy-start.18
  9.9 0.7 copy-start.19
  9.9 0.7 copy-start.15
  10.0 0.7 copy-start.16
  10.7 1.0 %copy-start.3 = (bf16[256,768]{1,0:T(8,128)(2,1)S(1)}, bf16[256,768]{1,0:T(8,128)(2,1)}, u32[]{:S(2)}) copy-start(bf16[256,768]{1,0:T(8,128)(2,1)} %refs_3_.5) | copy-start | bytes 1179652
  11.7 6.4 %copy-start.11 = (bf16[256,256]{1,0:T(8,128)(2,1)S(1)}, bf16[256,256]{1,0:T(8,128)(2,1)}, u32[]{:S(2)}) copy-start(bf16[256,256]{1,0:T(8,128)(2,1)} %refs_6_.2) | copy-start | bytes 393220
  18.1 4.9 %copy-start.13 = (bf16[1024,128]{1,0:T(8,128)(2,1)S(1)}, bf16[1024,128]{1,0:T(8,128)(2,1)}, u32[]{:S(2)}) copy-start(bf16[1024,128]{1,0:T(8,128)(2,1)} %param.38) | copy-start | bytes 786436
  20.4 10.0 %all-to-all-start.1 = ((bf16[32,8,128]{2,1,0:T(8,128)(2,1)}), bf16[32,8,128]{2,1,0:T(8,128)(2,1)S(1)}, u32[]{:S(2)}, u32[]{:S(2)}) async-start(bf16[32,8,128]{2,1,0:T(8,128)(2,1)} %shard_map.223), calls=%async_computation.1 | async-start | bytes 131072 | tf_op jit(solution)/shard_map/all_to_all | solution.py:864
  23.0 7.4 %copy-start.9 = (bf16[256,256]{1,0:T(8,128)(2,1)S(1)}, bf16[256,256]{1,0:T(8,128)(2,1)}, u32[]{:S(2)}) copy-start(bf16[256,256]{1,0:T(8,128)(2,1)} %refs_5_.2) | copy-start | bytes 393220
  23.0 7.4 %copy-start.12 = (bf16[256,64]{0,1:T(8,128)(2,1)S(1)}, bf16[256,64]{0,1:T(8,128)(2,1)}, u32[]{:S(2)}) copy-start(bf16[256,64]{0,1:T(8,128)(2,1)} %param.37) | copy-start | bytes 98308
  23.1 7.3 %copy-start.4 = (bf16[256,768]{1,0:T(8,128)(2,1)S(1)}, bf16[256,768]{1,0:T(8,128)(2,1)}, u32[]{:S(2)}) copy-start(bf16[256,768]{1,0:T(8,128)(2,1)} %refs_4_.3) | copy-start | bytes 1179652
  23.1 7.3 %copy-start.8 = (bf16[256,256]{1,0:T(8,128)(2,1)S(1)}, bf16[256,256]{1,0:T(8,128)(2,1)}, u32[]{:S(2)}) copy-start(bf16[256,256]{1,0:T(8,128)(2,1)} %refs_3_.6) | copy-start | bytes 393220
  32.8 3.7 %copy-start.14 = (bf16[1,128,128]{2,1,0:T(8,128)(2,1)S(1)}, bf16[1,128,128]{2,1,0:T(8,128)(2,1)}, u32[]{:S(2)}) copy-start(bf16[1,128,128]{2,1,0:T(8,128)(2,1)} %get-tuple-element.28) | copy-start | bytes 98308
  32.8 14.0 %all-to-all-start.2 = ((bf16[16,64,128]{2,1,0:T(8,128)(2,1)}), bf16[16,64,128]{2,1,0:T(8,128)(2,1)S(1)}, u32[]{:S(2)}, u32[]{:S(2)}) async-start(bf16[16,64,128]{2,1,0:T(8,128)(2,1)} %get-tuple-element.27), calls=%async_computation.2 | async-start | bytes 524288 | tf_op jit(solution)/shard_map/all_to_all | solution.py:886
  36.5 6.8 %collective-permute-start.1 = (bf16[1,128,128]{2,1,0:T(8,128)(2,1)S(1)}, bf16[1,128,128]{2,1,0:T(8,128)(2,1)S(1)}, u32[]{:S(2)}, u32[]{:S(2)}) collective-permute-start(bf16[1,128,128]{2,1,0:T(8,128)(2,1)S(1)} %copy-done.14), channel_id=1, source_target_pairs={{0,8},{1,9},{2,10},{3,11},{4,12},{5,13},{6,14},{7,15},{8,0},{9,1},... | collective-permute-start | bytes 98312 | tf_op jit(solution)/shard_map/ppermute | solution.py:763
  43.3 15.2 %copy-start = (bf16[2,128,512]{2,1,0:T(8,128)(2,1)S(1)}, bf16[2,128,512]{2,1,0:T(8,128)(2,1)}, u32[]{:S(2)}) copy-start(bf16[2,128,512]{2,1,0:T(8,128)(2,1)} %refs_7_.1) | copy-start | bytes 786436
  43.3 6.3 %collective-permute-start.2 = (bf16[2,128,128]{2,1,0:T(8,128)(2,1)S(1)}, bf16[2,128,128]{2,1,0:T(8,128)(2,1)S(1)}, u32[]{:S(2)}, u32[]{:S(2)}) collective-permute-start(bf16[2,128,128]{2,1,0:T(8,128)(2,1)S(1)} %pad_maximum_fusion), channel_id=1, source_target_pairs={{0,16},{1,17},{2,18},{3,19},{4,20},{5,21},{6,22},{7,23},{8,24},{9,... | collective-permute-start | bytes 196616 | tf_op jit(solution)/shard_map/ppermute | solution.py:763
  46.8 11.6 %collective-permute-start = (bf16[16,64,128]{2,1,0:T(8,128)(2,1)S(1)}, bf16[16,64,128]{2,1,0:T(8,128)(2,1)S(1)}, u32[]{:S(2)}, u32[]{:S(2)}) collective-permute-start(bf16[16,64,128]{2,1,0:T(8,128)(2,1)S(1)} %all-to-all-done.2.refs_0_), channel_id=1, source_target_pairs={{0,1},{1,0},{2,3},{3,2},{4,5},{5,4},{6,7},{7,6},{8,9},{9,8},{10,11... | collective-permute-start | bytes 786440 | tf_op jit(solution)/shard_map/ppermute | solution.py:889
  49.6 6.2 %collective-permute-start.3 = (bf16[4,128,128]{2,1,0:T(8,128)(2,1)S(1)}, bf16[4,128,128]{2,1,0:T(8,128)(2,1)S(1)}, u32[]{:S(2)}, u32[]{:S(2)}) collective-permute-start(bf16[4,128,128]{2,1,0:T(8,128)(2,1)S(1)} %constant_dynamic-update-slice_fusion.refs_2_), channel_id=1, source_target_pairs={{0,2},{1,3},{2,0},{3,1},{4,6},{5,7},{6,4},{7,5},{8,10},{9,11},{10,... | collective-permute-start | bytes 393224 | tf_op jit(solution)/shard_map/ppermute | solution.py:763
  51.1 5.9 %collective-permute-start.4 = (bf16[4,128,128]{2,1,0:T(8,128)(2,1)S(1)}, bf16[4,128,128]{2,1,0:T(8,128)(2,1)S(1)}, u32[]{:S(2)}, u32[]{:S(2)}) collective-permute-start(bf16[4,128,128]{2,1,0:T(8,128)(2,1)S(1)} %constant_dynamic-update-slice_fusion.refs_2_), channel_id=1, source_target_pairs={{0,4},{1,5},{2,6},{3,7},{4,0},{5,1},{6,2},{7,3},{8,12},{9,13},{10,... | collective-permute-start | bytes 393224 | tf_op jit(solution)/shard_map/ppermute | solution.py:763
  52.6 5.9 %collective-permute-start.5 = (bf16[4,128,128]{2,1,0:T(8,128)(2,1)S(1)}, bf16[4,128,128]{2,1,0:T(8,128)(2,1)S(1)}, u32[]{:S(2)}, u32[]{:S(2)}) collective-permute-start(bf16[4,128,128]{2,1,0:T(8,128)(2,1)S(1)} %constant_dynamic-update-slice_fusion.refs_2_), channel_id=1, source_target_pairs={{0,6},{1,7},{2,4},{3,5},{4,2},{5,3},{6,0},{7,1},{8,14},{9,15},{10,... | collective-permute-start | bytes 393224 | tf_op jit(solution)/shard_map/ppermute | solution.py:763
  53.2 8.8 %copy-start.1 = (f32[64,2,256]{2,1,0:T(2,128)}, f32[64,2,256]{2,1,0:T(2,128)S(1)}, u32[]{:S(2)}) copy-start(f32[64,2,256]{2,1,0:T(2,128)S(1)} %reshape.54.refs_10_) | copy-start | bytes 393220
  53.2 8.9 %copy-start.7 = (bf16[2,128,128]{2,1,0:T(8,128)(2,1)S(1)}, bf16[2,128,128]{2,1,0:T(8,128)(2,1)}, u32[]{:S(2)}) copy-start(bf16[2,128,128]{2,1,0:T(8,128)(2,1)} %refs_4_.5) | copy-start | bytes 196612
  62.0 2.0 %collective-permute-start.6 = (bf16[16,128,128]{2,1,0:T(8,128)(2,1)S(1)}, bf16[16,128,128]{2,1,0:T(8,128)(2,1)S(1)}, u32[]{:S(2)}, u32[]{:S(2)}) collective-permute-start(bf16[16,128,128]{2,1,0:T(8,128)(2,1)S(1)} %get-tuple-element.31.refs_1_), channel_id=1, source_target_pairs={{0,1},{1,0},{2,3},{3,2},{4,5},{5,4},{6,7},{7,6},{8,9},{9,8},{10,11... | collective-permute-start | bytes 1572872 | tf_op jit(solution)/shard_map/ppermute | solution.py:915
  62.1 1.9 %copy-start.5 = (bf16[2,128,128]{2,1,0:T(8,128)(2,1)S(1)}, bf16[2,128,128]{2,1,0:T(8,128)(2,1)}, u32[]{:S(2)}) copy-start(bf16[2,128,128]{2,1,0:T(8,128)(2,1)} %refs_5_.3) | copy-start | bytes 196612
  64.0 3.9 %copy-start.6 = (f32[2,64,128]{2,1,0:T(8,128)S(1)}, f32[2,64,128]{2,1,0:T(8,128)}, u32[]{:S(2)}) copy-start(f32[2,64,128]{2,1,0:T(8,128)} %param.23) | copy-start | bytes 196612
  67.7 2.1 %collective-permute-start.7 = (bf16[16,144,128]{2,1,0:T(8,128)(2,1)S(1)}, bf16[16,144,128]{2,1,0:T(8,128)(2,1)S(1)}, u32[]{:S(2)}, u32[]{:S(2)}) collective-permute-start(bf16[16,144,128]{2,1,0:T(8,128)(2,1)S(1)} %get-tuple-element.35.refs_0_), channel_id=1, source_target_pairs={{0,1},{1,0},{2,3},{3,2},{4,5},{5,4},{6,7},{7,6},{8,9},{9,8},{10,11... | collective-permute-start | bytes 1769480 | tf_op jit(solution)/shard_map/ppermute | solution.py:949

commit v7 on v6

--- a/solution.py
+++ b/solution.py
@@ -367,8 +367,10 @@
     ).astype(jnp.bfloat16)
 
 
-def attend_heads(q, k, v, offset):
-    scores = dot_nt(head_spread(q), k) + offset
+def attend_heads(q, k, v, *offsets):
+    scores = dot_nt(head_spread(q), k)
+    for offset in offsets:
+        scores = scores + offset
     scores = scores - jnp.max(scores, axis=-1, keepdims=True)
     raised = jnp.exp(scores)
     shares = (raised / jnp.sum(raised, axis=-1, keepdims=True)).astype(jnp.bfloat16)
@@ -397,7 +399,9 @@
         for r in range(2):
             rows = pl.ds(s * per_seq + r, devices, stride=2)
             bias = jnp.concatenate([b[:, r * half : (r + 1) * half] for b in heads], axis=0)
-            mixed = attend_heads(rows_of(q_ref, rows), keys, values, bias + penalty[:, s * half : (s + 1) * half])
+            mixed = attend_heads(
+                rows_of(q_ref, rows), keys, values, bias, penalty[:, s * half : (s + 1) * half]
+            )
             y = (mixed * rows_of(g_ref, rows)).astype(jnp.bfloat16)
             updated = rows_of(x_parts, rows) + dot_nn(y, final_ref[...])
             for part in range(updated.shape[1] // (2 * half)):
@@ -607,7 +611,7 @@
             left_ref[chip * channels : (chip + 1) * channels, :] = jnp.transpose(left[rows])
             side[chip * channels : (chip + 1) * channels, :] = own_ref[chip].astype(jnp.float32)
     low = lane_iota((chips, lanes)) < half
-    per_step = 64
+    per_step = channels
 
     @pl.loop(0, channels // per_step)
     def _(step):
@@ -636,7 +640,7 @@
     my_chip = me // 2
 
     side[...] = oth_ref[...].astype(jnp.float32).reshape(side.shape)
-    per_step = 64
+    per_step = channels
 
     @pl.loop(0, channels // per_step)
     def _(step):

time: 71.4 us -> 71.1 us (level)
  no operation moved by 1% of the time
where the time goes in v7:
time: 71.1 us; the launch traced here: 70.7 us
  waiting for transfers between devices  28.3 us (40%)
  starting transfers between devices  22.6 us (32%)
  Pallas kernels  16.6 us (23%)
  local copies, waits for them, and re-layouts  2.17 us (3%)
  between operations  0.96 us (1%)
    ppermute x5, waiting for transfers between devices, fetch(): lax.ppermute(value, 'dap', [(d, d ^ 2 * apart) for d in range(devices)])  12.8 us
    ppermute x5, starting transfers between devices, fetch(): lax.ppermute(value, 'dap', [(d, d ^ 2 * apart) for d in range(devices)])  8.58 us
    all_to_all x1, starting transfers between devices, paired_shards(): lax.all_to_all(block, 'dap', split_axis=0, concat_axis=0, tiled=True)  7.33 us
    all_to_all x1, waiting for transfers between devices, paired_shards(): lax.all_to_all(sent, 'dap', split_axis=0, concat_axis=0, tiled=True)  7.08 us
    all_to_all x1, waiting for transfers between devices, paired_shards(): lax.all_to_all(block, 'dap', split_axis=0, concat_axis=0, tiled=True)  6 us
    all_to_all x1, starting transfers between devices, paired_shards(): lax.all_to_all(opm, 'dap', split_axis=0, concat_axis=0, tiled=True, axis_...  3.84 us
    pallas_call x1, Pallas kernels, paired_shards(): vmem_call(functools.partial(opm_body, len(couples)), (shape(stack, f32),...  3.57 us
    pallas_call x1, Pallas kernels, paired_shards(): vmem_call(outgoing_body, (shape((lanes, channels), f32), shape((chips, la...  3.44 us
  transfers between devices with their start and end apart: 11, of which 10 were waited for; matrix products, arithmetic and copies ran while one was open for 1% of the time, Pallas kernels for 3%

profile of v7, /device:TPU:0, one launch (start us, length us, event | category | flops | bytes accessed | tf_op | source)
XLA Modules:
  0.0 70.7 jit_solution(11451685218812950849)
XLA Ops:
  0.6 1.9 %shard_map.221 = (bf16[32,16,128]{2,1,0:T(8,128)(2,1)}, bf16[1,128,128]{2,1,0:T(8,128)(2,1)}) custom-call(f32[128,128]{1,0:T(8,128)} %bitcast.19, f32[1,128]{1,0:T(1,128)} %bitcast.31, bf16[8,128]{1,0:T(8,128)(2,1)} %bitcast.25, s32[2,64]{1,0:T(2,128)} %refs_3_.4), custom_call_target="tpu_custom_call" | custom-call | tf_op jit(solution)/shard_map/pallas_call | solution.py:816
  2.5 0.0 copy-start.2
  2.5 0.0 copy-start.10
  2.5 7.3 %all-to-all-start = ((bf16[32,16,128]{2,1,0:T(8,128)(2,1)}), bf16[32,16,128]{2,1,0:T(8,128)(2,1)S(1)}, u32[]{:S(2)}, u32[]{:S(2)}) async-start(bf16[32,16,128]{2,1,0:T(8,128)(2,1)} %get-tuple-element.21), calls=%async_computation | async-start | bytes 262144 | tf_op jit(solution)/shard_map/all_to_all | solution.py:830
  9.9 0.0 copy-start.18
  9.9 0.0 copy-start.19
  10.0 0.6 copy-done.17
  10.6 0.0 copy-done.18
  10.6 0.0 copy-done.19
  10.6 0.0 copy-done.15
  10.6 0.0 copy-done.16
  10.7 0.0 copy-start.3
  10.7 1.0 %copy-done.3 = bf16[256,768]{1,0:T(8,128)(2,1)S(1)} copy-done((bf16[256,768]{1,0:T(8,128)(2,1)S(1)}, bf16[256,768]{1,0:T(8,128)(2,1)}, u32[]{:S(2)}) %copy-start.3) | copy-done | bytes 393240
  11.7 0.4 shard_map.222
  12.1 6.0 %all-to-all-done.refs_0_.refs_1_.refs_6_ = bf16[32,16,128]{2,1,0:T(8,128)(2,1)S(1)} async-done(((bf16[32,16,128]{2,1,0:T(8,128)(2,1)}), bf16[32,16,128]{2,1,0:T(8,128)(2,1)S(1)}, u32[]{:S(2)}, u32[]{:S(2)}) %all-to-all-start) | async-done | bytes 131104 | tf_op jit(solution)/shard_map/all_to_all | solution.py:830
  18.1 2.3 %shard_map.223 = bf16[32,8,128]{2,1,0:T(8,128)(2,1)} custom-call(bf16[32,16,128]{2,1,0:T(8,128)(2,1)S(1)} %all-to-all-done.refs_0_.refs_1_.refs_6_, f32[128,256]{1,0:T(8,128)S(1)} %bitcast.18, f32[2,128,128]{2,1,0:T(8,128)S(1)} %get-tuple-element.22.refs_2_, bf16[128,256]{1,0:T(8,128)(2,1)S(1)} %get-tuple-element.23.refs_3_, ...), custom_call_target="tpu_custom_call" | custom-call | tf_op jit(solution)/shard_map/pallas_call | solution.py:858
  20.4 2.6 %all-to-all-start.1 = ((bf16[32,8,128]{2,1,0:T(8,128)(2,1)}), bf16[32,8,128]{2,1,0:T(8,128)(2,1)S(1)}, u32[]{:S(2)}, u32[]{:S(2)}) async-start(bf16[32,8,128]{2,1,0:T(8,128)(2,1)} %shard_map.223), calls=%async_computation.1 | async-start | bytes 131072 | tf_op jit(solution)/shard_map/all_to_all | solution.py:868
  23.0 0.0 copy-start.9
  23.0 0.1 copy.27
  23.1 0.0 copy-start.8
  23.1 0.1 copy.28.refs_7_
  23.3 7.1 %all-to-all-done.1.refs_0_ = bf16[32,8,128]{2,1,0:T(8,128)(2,1)S(1)} async-done(((bf16[32,8,128]{2,1,0:T(8,128)(2,1)}), bf16[32,8,128]{2,1,0:T(8,128)(2,1)S(1)}, u32[]{:S(2)}, u32[]{:S(2)}) %all-to-all-start.1) | async-done | bytes 65568 | tf_op jit(solution)/shard_map/all_to_all | solution.py:868
  30.4 2.4 %shard_map.224 = (f32[64,512]{1,0:T(8,128)S(1)}, bf16[16,64,128]{2,1,0:T(8,128)(2,1)}) custom-call(bf16[32,8,128]{2,1,0:T(8,128)(2,1)S(1)} %all-to-all-done.1.refs_0_, bf16[32,16,128]{2,1,0:T(8,128)(2,1)S(1)} %all-to-all-done.refs_0_.refs_1_.refs_6_, f32[8,256]{1,0:T(8,128)S(1)} %concatenate.10.refs_1_.refs_2_.refs_8_.refs_5_.refs_3_.refs_4_, ...), custom_call_target="tpu_custom_call" | custom-call | tf_op jit(solution)/shard_map/pallas_call | solution.py:869
  32.8 3.8 %all-to-all-start.2 = ((bf16[16,64,128]{2,1,0:T(8,128)(2,1)}), bf16[16,64,128]{2,1,0:T(8,128)(2,1)S(1)}, u32[]{:S(2)}, u32[]{:S(2)}) async-start(bf16[16,64,128]{2,1,0:T(8,128)(2,1)} %get-tuple-element.27), calls=%async_computation.2 | async-start | bytes 524288 | tf_op jit(solution)/shard_map/all_to_all | solution.py:890
  36.7 1.7 %collective-permute-start.1 = (bf16[1,128,128]{2,1,0:T(8,128)(2,1)S(1)}, bf16[1,128,128]{2,1,0:T(8,128)(2,1)S(1)}, u32[]{:S(2)}, u32[]{:S(2)}) collective-permute-start(bf16[1,128,128]{2,1,0:T(8,128)(2,1)S(1)} %copy-done.14), channel_id=1, source_target_pairs={{0,8},{1,9},{2,10},{3,11},{4,12},{5,13},{6,14},{7,15},{8,0},{9,1},... | collective-permute-start | bytes 98312 | tf_op jit(solution)/shard_map/ppermute | solution.py:767
  38.4 4.9 %collective-permute-done.1 = bf16[1,128,128]{2,1,0:T(8,128)(2,1)S(1)} collective-permute-done((bf16[1,128,128]{2,1,0:T(8,128)(2,1)S(1)}, bf16[1,128,128]{2,1,0:T(8,128)(2,1)S(1)}, u32[]{:S(2)}, u32[]{:S(2)}) %collective-permute-start.1) | collective-permute-done | bytes 32800 | tf_op jit(solution)/shard_map/ppermute | solution.py:767
  43.3 0.0 copy-start
  43.3 3.3 %collective-permute-start.2 = (bf16[2,128,128]{2,1,0:T(8,128)(2,1)S(1)}, bf16[2,128,128]{2,1,0:T(8,128)(2,1)S(1)}, u32[]{:S(2)}, u32[]{:S(2)}) collective-permute-start(bf16[2,128,128]{2,1,0:T(8,128)(2,1)S(1)} %pad_maximum_fusion), channel_id=1, source_target_pairs={{0,16},{1,17},{2,18},{3,19},{4,20},{5,21},{6,22},{7,23},{8,24},{9,... | collective-permute-start | bytes 196616 | tf_op jit(solution)/shard_map/ppermute | solution.py:767
  46.6 0.2 all-to-all-done.2.refs_0_
  46.8 2.7 %collective-permute-done.2 = bf16[2,128,128]{2,1,0:T(8,128)(2,1)S(1)} collective-permute-done((bf16[2,128,128]{2,1,0:T(8,128)(2,1)S(1)}, bf16[2,128,128]{2,1,0:T(8,128)(2,1)S(1)}, u32[]{:S(2)}, u32[]{:S(2)}) %collective-permute-start.2) | collective-permute-done | bytes 65568 | tf_op jit(solution)/shard_map/ppermute | solution.py:767
  49.6 1.5 %collective-permute-start.3 = (bf16[4,128,128]{2,1,0:T(8,128)(2,1)S(1)}, bf16[4,128,128]{2,1,0:T(8,128)(2,1)S(1)}, u32[]{:S(2)}, u32[]{:S(2)}) collective-permute-start(bf16[4,128,128]{2,1,0:T(8,128)(2,1)S(1)} %constant_dynamic-update-slice_fusion.refs_2_), channel_id=1, source_target_pairs={{0,2},{1,3},{2,0},{3,1},{4,6},{5,7},{6,4},{7,5},{8,10},{9,11},{10,... | collective-permute-start | bytes 393224 | tf_op jit(solution)/shard_map/ppermute | solution.py:767
  51.1 1.5 %collective-permute-start.4 = (bf16[4,128,128]{2,1,0:T(8,128)(2,1)S(1)}, bf16[4,128,128]{2,1,0:T(8,128)(2,1)S(1)}, u32[]{:S(2)}, u32[]{:S(2)}) collective-permute-start(bf16[4,128,128]{2,1,0:T(8,128)(2,1)S(1)} %constant_dynamic-update-slice_fusion.refs_2_), channel_id=1, source_target_pairs={{0,4},{1,5},{2,6},{3,7},{4,0},{5,1},{6,2},{7,3},{8,12},{9,13},{10,... | collective-permute-start | bytes 393224 | tf_op jit(solution)/shard_map/ppermute | solution.py:767
  52.6 0.5 collective-permute-start.5
  53.1 0.1 reshape.54.refs_10_
  53.2 0.0 copy-start.1
  53.2 2.6 %collective-permute-done.3.refs_3_ = bf16[4,128,128]{2,1,0:T(8,128)(2,1)S(1)} collective-permute-done((bf16[4,128,128]{2,1,0:T(8,128)(2,1)S(1)}, bf16[4,128,128]{2,1,0:T(8,128)(2,1)S(1)}, u32[]{:S(2)}, u32[]{:S(2)}) %collective-permute-start.3) | collective-permute-done | bytes 131104 | tf_op jit(solution)/shard_map/ppermute | solution.py:767
  55.8 1.2 %collective-permute-done.4.refs_4_ = bf16[4,128,128]{2,1,0:T(8,128)(2,1)S(1)} collective-permute-done((bf16[4,128,128]{2,1,0:T(8,128)(2,1)S(1)}, bf16[4,128,128]{2,1,0:T(8,128)(2,1)S(1)}, u32[]{:S(2)}, u32[]{:S(2)}) %collective-permute-start.4) | collective-permute-done | bytes 131104 | tf_op jit(solution)/shard_map/ppermute | solution.py:767
  57.0 1.5 %collective-permute-done.5.refs_5_ = bf16[4,128,128]{2,1,0:T(8,128)(2,1)S(1)} collective-permute-done((bf16[4,128,128]{2,1,0:T(8,128)(2,1)S(1)}, bf16[4,128,128]{2,1,0:T(8,128)(2,1)S(1)}, u32[]{:S(2)}, u32[]{:S(2)}) %collective-permute-start.5) | collective-permute-done | bytes 131104 | tf_op jit(solution)/shard_map/ppermute | solution.py:767
  58.5 3.6 %shard_map.225 = (f32[16,128,128]{2,1,0:T(8,128)S(1)}, bf16[16,128,128]{2,1,0:T(8,128)(2,1)S(1)}, bf16[16,128,128]{2,1,0:T(8,128)(2,1)S(1)}) custom-call(bf16[16,64,128]{2,1,0:T(8,128)(2,1)S(1)} %all-to-all-done.2.refs_0_, bf16[16,64,128]{2,1,0:T(8,128)(2,1)S(1)} %collective-permute-done.refs_1_, ...), custom_call_target="tpu_custom_call" | custom-call | tf_op jit(solution)/shard_map/pallas_call | solution.py:896
  62.0 0.1 collective-permute-start.6
  62.1 0.0 copy-start.5
  62.1 1.0 %shard_map.226 = (bf16[4096,128]{1,0:T(8,128)(2,1)S(1)}, bf16[4096,128]{1,0:T(8,128)(2,1)S(1)}, f32[16,128,128]{2,1,0:T(8,128)S(1)}) custom-call(bf16[16,128,128]{2,1,0:T(8,128)(2,1)S(1)} %get-tuple-element.30.refs_0_, bf16[16,128,128]{2,1,0:T(8,128)(2,1)S(1)} %get-tuple-element.31.refs_1_, ...), custom_call_target="tpu_custom_call" | custom-call | tf_op jit(solution)/shard_map/pallas_call | solution.py:921
  63.2 0.8 %collective-permute-done.6.refs_4_ = bf16[16,128,128]{2,1,0:T(8,128)(2,1)S(1)} collective-permute-done((bf16[16,128,128]{2,1,0:T(8,128)(2,1)S(1)}, bf16[16,128,128]{2,1,0:T(8,128)(2,1)S(1)}, u32[]{:S(2)}, u32[]{:S(2)}) %collective-permute-start.6) | collective-permute-done | bytes 524320 | tf_op jit(solution)/shard_map/ppermute | solution.py:919
  64.0 3.4 %shard_map.227 = (f32[128,128]{1,0:T(8,128)S(1)}, bf16[16,144,128]{2,1,0:T(8,128)(2,1)S(1)}) custom-call(f32[16,128,128]{2,1,0:T(8,128)S(1)} %get-tuple-element.29.refs_0_, bf16[4096,128]{1,0:T(8,128)(2,1)S(1)} %get-tuple-element.32.refs_1_, bf16[4096,128]{1,0:T(8,128)(2,1)S(1)} %get-tuple-element.33.refs_2_, f32[16,128,128]{2,1,0:T(8,128)S(1)} %get-tuple-element.34.refs_3_, ...), custom_call_target="tpu_custom_call" | custom-call | tf_op jit(solution)/shard_map/pallas_call | solution.py:931
  67.5 0.2 collective-permute-start.7
  67.7 0.5 shard_map.228
  68.2 1.4 %collective-permute-done.7.refs_0_ = bf16[16,144,128]{2,1,0:T(8,128)(2,1)S(1)} collective-permute-done((bf16[16,144,128]{2,1,0:T(8,128)(2,1)S(1)}, bf16[16,144,128]{2,1,0:T(8,128)(2,1)S(1)}, u32[]{:S(2)}, u32[]{:S(2)}) %collective-permute-start.7) | collective-permute-done | bytes 589856 | tf_op jit(solution)/shard_map/ppermute | solution.py:953
  69.5 1.1 %shard_map.229 = f32[128,128]{1,0:T(8,128)} custom-call(bf16[16,144,128]{2,1,0:T(8,128)(2,1)S(1)} %collective-permute-done.7.refs_0_, f32[128,128]{1,0:T(8,128)S(1)} %get-tuple-element.37.refs_1_, f32[128,128]{1,0:T(8,128)S(1)} %get-tuple-element.38.refs_2_, f32[128,128]{1,0:T(8,128)S(1)} %get-tuple-element.39.refs_3_, ...), custom_call_target="tpu_custom_call" | custom-call | tf_op jit(solution)/shard_map/pallas_call | solution.py:959
  (36 shorter events, 0.1 us)
Async XLA Ops:
  0.6 9.2 %copy-start.20 = (s32[64]{0:T(128)S(1)}, s32[64]{0:T(128)}, u32[]{:S(2)}) copy-start(s32[64]{0:T(128)} %param.25) | copy-start | bytes 772
  2.5 8.2 %copy-start.2 = (f32[2,64,256]{2,1,0:T(8,128)S(1)}, f32[2,64,256]{2,1,0:T(8,128)}, u32[]{:S(2)}) copy-start(f32[2,64,256]{2,1,0:T(8,128)} %param.22) | copy-start | bytes 393220
  2.5 8.2 %copy-start.10 = (bf16[256,256]{1,0:T(8,128)(2,1)S(1)}, bf16[256,256]{1,0:T(8,128)(2,1)}, u32[]{:S(2)}) copy-start(bf16[256,256]{1,0:T(8,128)(2,1)} %refs_2_.1) | copy-start | bytes 393220
  2.5 15.5 %all-to-all-start = ((bf16[32,16,128]{2,1,0:T(8,128)(2,1)}), bf16[32,16,128]{2,1,0:T(8,128)(2,1)S(1)}, u32[]{:S(2)}, u32[]{:S(2)}) async-start(bf16[32,16,128]{2,1,0:T(8,128)(2,1)} %get-tuple-element.21), calls=%async_computation | async-start | bytes 262144 | tf_op jit(solution)/shard_map/all_to_all | solution.py:830
  9.9 0.7 copy-start.17
  9.9 0.7 copy-start.18
  9.9 0.7 copy-start.19
  9.9 0.7 copy-start.15
  10.0 0.7 copy-start.16
  10.7 1.0 %copy-start.3 = (bf16[256,768]{1,0:T(8,128)(2,1)S(1)}, bf16[256,768]{1,0:T(8,128)(2,1)}, u32[]{:S(2)}) copy-start(bf16[256,768]{1,0:T(8,128)(2,1)} %refs_3_.5) | copy-start | bytes 1179652
  11.7 6.4 %copy-start.11 = (bf16[256,256]{1,0:T(8,128)(2,1)S(1)}, bf16[256,256]{1,0:T(8,128)(2,1)}, u32[]{:S(2)}) copy-start(bf16[256,256]{1,0:T(8,128)(2,1)} %refs_6_.2) | copy-start | bytes 393220
  18.1 4.9 %copy-start.13 = (bf16[1024,128]{1,0:T(8,128)(2,1)S(1)}, bf16[1024,128]{1,0:T(8,128)(2,1)}, u32[]{:S(2)}) copy-start(bf16[1024,128]{1,0:T(8,128)(2,1)} %param.38) | copy-start | bytes 786436
  20.4 10.0 %all-to-all-start.1 = ((bf16[32,8,128]{2,1,0:T(8,128)(2,1)}), bf16[32,8,128]{2,1,0:T(8,128)(2,1)S(1)}, u32[]{:S(2)}, u32[]{:S(2)}) async-start(bf16[32,8,128]{2,1,0:T(8,128)(2,1)} %shard_map.223), calls=%async_computation.1 | async-start | bytes 131072 | tf_op jit(solution)/shard_map/all_to_all | solution.py:868
  23.0 7.4 %copy-start.9 = (bf16[256,256]{1,0:T(8,128)(2,1)S(1)}, bf16[256,256]{1,0:T(8,128)(2,1)}, u32[]{:S(2)}) copy-start(bf16[256,256]{1,0:T(8,128)(2,1)} %refs_5_.2) | copy-start | bytes 393220
  23.0 7.4 %copy-start.12 = (bf16[256,64]{0,1:T(8,128)(2,1)S(1)}, bf16[256,64]{0,1:T(8,128)(2,1)}, u32[]{:S(2)}) copy-start(bf16[256,64]{0,1:T(8,128)(2,1)} %param.37) | copy-start | bytes 98308
  23.1 7.3 %copy-start.4 = (bf16[256,768]{1,0:T(8,128)(2,1)S(1)}, bf16[256,768]{1,0:T(8,128)(2,1)}, u32[]{:S(2)}) copy-start(bf16[256,768]{1,0:T(8,128)(2,1)} %refs_4_.3) | copy-start | bytes 1179652
  23.1 7.3 %copy-start.8 = (bf16[256,256]{1,0:T(8,128)(2,1)S(1)}, bf16[256,256]{1,0:T(8,128)(2,1)}, u32[]{:S(2)}) copy-start(bf16[256,256]{1,0:T(8,128)(2,1)} %refs_3_.6) | copy-start | bytes 393220
  32.8 3.9 %copy-start.14 = (bf16[1,128,128]{2,1,0:T(8,128)(2,1)S(1)}, bf16[1,128,128]{2,1,0:T(8,128)(2,1)}, u32[]{:S(2)}) copy-start(bf16[1,128,128]{2,1,0:T(8,128)(2,1)} %get-tuple-element.28) | copy-start | bytes 98308
  32.8 14.0 %all-to-all-start.2 = ((bf16[16,64,128]{2,1,0:T(8,128)(2,1)}), bf16[16,64,128]{2,1,0:T(8,128)(2,1)S(1)}, u32[]{:S(2)}, u32[]{:S(2)}) async-start(bf16[16,64,128]{2,1,0:T(8,128)(2,1)} %get-tuple-element.27), calls=%async_computation.2 | async-start | bytes 524288 | tf_op jit(solution)/shard_map/all_to_all | solution.py:890
  36.7 6.6 %collective-permute-start.1 = (bf16[1,128,128]{2,1,0:T(8,128)(2,1)S(1)}, bf16[1,128,128]{2,1,0:T(8,128)(2,1)S(1)}, u32[]{:S(2)}, u32[]{:S(2)}) collective-permute-start(bf16[1,128,128]{2,1,0:T(8,128)(2,1)S(1)} %copy-done.14), channel_id=1, source_target_pairs={{0,8},{1,9},{2,10},{3,11},{4,12},{5,13},{6,14},{7,15},{8,0},{9,1},... | collective-permute-start | bytes 98312 | tf_op jit(solution)/shard_map/ppermute | solution.py:767
  43.3 15.2 %copy-start = (bf16[2,128,512]{2,1,0:T(8,128)(2,1)S(1)}, bf16[2,128,512]{2,1,0:T(8,128)(2,1)}, u32[]{:S(2)}) copy-start(bf16[2,128,512]{2,1,0:T(8,128)(2,1)} %refs_7_.1) | copy-start | bytes 786436
  43.3 6.3 %collective-permute-start.2 = (bf16[2,128,128]{2,1,0:T(8,128)(2,1)S(1)}, bf16[2,128,128]{2,1,0:T(8,128)(2,1)S(1)}, u32[]{:S(2)}, u32[]{:S(2)}) collective-permute-start(bf16[2,128,128]{2,1,0:T(8,128)(2,1)S(1)} %pad_maximum_fusion), channel_id=1, source_target_pairs={{0,16},{1,17},{2,18},{3,19},{4,20},{5,21},{6,22},{7,23},{8,24},{9,... | collective-permute-start | bytes 196616 | tf_op jit(solution)/shard_map/ppermute | solution.py:767
  46.8 11.6 %collective-permute-start = (bf16[16,64,128]{2,1,0:T(8,128)(2,1)S(1)}, bf16[16,64,128]{2,1,0:T(8,128)(2,1)S(1)}, u32[]{:S(2)}, u32[]{:S(2)}) collective-permute-start(bf16[16,64,128]{2,1,0:T(8,128)(2,1)S(1)} %all-to-all-done.2.refs_0_), channel_id=1, source_target_pairs={{0,1},{1,0},{2,3},{3,2},{4,5},{5,4},{6,7},{7,6},{8,9},{9,8},{10,11... | collective-permute-start | bytes 786440 | tf_op jit(solution)/shard_map/ppermute | solution.py:893
  49.6 6.2 %collective-permute-start.3 = (bf16[4,128,128]{2,1,0:T(8,128)(2,1)S(1)}, bf16[4,128,128]{2,1,0:T(8,128)(2,1)S(1)}, u32[]{:S(2)}, u32[]{:S(2)}) collective-permute-start(bf16[4,128,128]{2,1,0:T(8,128)(2,1)S(1)} %constant_dynamic-update-slice_fusion.refs_2_), channel_id=1, source_target_pairs={{0,2},{1,3},{2,0},{3,1},{4,6},{5,7},{6,4},{7,5},{8,10},{9,11},{10,... | collective-permute-start | bytes 393224 | tf_op jit(solution)/shard_map/ppermute | solution.py:767
  51.1 5.9 %collective-permute-start.4 = (bf16[4,128,128]{2,1,0:T(8,128)(2,1)S(1)}, bf16[4,128,128]{2,1,0:T(8,128)(2,1)S(1)}, u32[]{:S(2)}, u32[]{:S(2)}) collective-permute-start(bf16[4,128,128]{2,1,0:T(8,128)(2,1)S(1)} %constant_dynamic-update-slice_fusion.refs_2_), channel_id=1, source_target_pairs={{0,4},{1,5},{2,6},{3,7},{4,0},{5,1},{6,2},{7,3},{8,12},{9,13},{10,... | collective-permute-start | bytes 393224 | tf_op jit(solution)/shard_map/ppermute | solution.py:767
  52.6 5.9 %collective-permute-start.5 = (bf16[4,128,128]{2,1,0:T(8,128)(2,1)S(1)}, bf16[4,128,128]{2,1,0:T(8,128)(2,1)S(1)}, u32[]{:S(2)}, u32[]{:S(2)}) collective-permute-start(bf16[4,128,128]{2,1,0:T(8,128)(2,1)S(1)} %constant_dynamic-update-slice_fusion.refs_2_), channel_id=1, source_target_pairs={{0,6},{1,7},{2,4},{3,5},{4,2},{5,3},{6,0},{7,1},{8,14},{9,15},{10,... | collective-permute-start | bytes 393224 | tf_op jit(solution)/shard_map/ppermute | solution.py:767
  53.2 8.8 %copy-start.1 = (f32[64,2,256]{2,1,0:T(2,128)}, f32[64,2,256]{2,1,0:T(2,128)S(1)}, u32[]{:S(2)}) copy-start(f32[64,2,256]{2,1,0:T(2,128)S(1)} %reshape.54.refs_10_) | copy-start | bytes 393220
  53.2 8.9 %copy-start.7 = (bf16[2,128,128]{2,1,0:T(8,128)(2,1)S(1)}, bf16[2,128,128]{2,1,0:T(8,128)(2,1)}, u32[]{:S(2)}) copy-start(bf16[2,128,128]{2,1,0:T(8,128)(2,1)} %refs_4_.5) | copy-start | bytes 196612
  62.0 2.0 %collective-permute-start.6 = (bf16[16,128,128]{2,1,0:T(8,128)(2,1)S(1)}, bf16[16,128,128]{2,1,0:T(8,128)(2,1)S(1)}, u32[]{:S(2)}, u32[]{:S(2)}) collective-permute-start(bf16[16,128,128]{2,1,0:T(8,128)(2,1)S(1)} %get-tuple-element.31.refs_1_), channel_id=1, source_target_pairs={{0,1},{1,0},{2,3},{3,2},{4,5},{5,4},{6,7},{7,6},{8,9},{9,8},{10,11... | collective-permute-start | bytes 1572872 | tf_op jit(solution)/shard_map/ppermute | solution.py:919
  62.1 1.9 %copy-start.5 = (bf16[2,128,128]{2,1,0:T(8,128)(2,1)S(1)}, bf16[2,128,128]{2,1,0:T(8,128)(2,1)}, u32[]{:S(2)}) copy-start(bf16[2,128,128]{2,1,0:T(8,128)(2,1)} %refs_5_.3) | copy-start | bytes 196612
  64.0 3.7 %copy-start.6 = (f32[2,64,128]{2,1,0:T(8,128)S(1)}, f32[2,64,128]{2,1,0:T(8,128)}, u32[]{:S(2)}) copy-start(f32[2,64,128]{2,1,0:T(8,128)} %param.23) | copy-start | bytes 196612
  67.5 2.1 %collective-permute-start.7 = (bf16[16,144,128]{2,1,0:T(8,128)(2,1)S(1)}, bf16[16,144,128]{2,1,0:T(8,128)(2,1)S(1)}, u32[]{:S(2)}, u32[]{:S(2)}) collective-permute-start(bf16[16,144,128]{2,1,0:T(8,128)(2,1)S(1)} %get-tuple-element.35.refs_0_), channel_id=1, source_target_pairs={{0,1},{1,0},{2,3},{3,2},{4,5},{5,4},{6,7},{7,6},{8,9},{9,8},{10,11... | collective-permute-start | bytes 1769480 | tf_op jit(solution)/shard_map/ppermute | solution.py:953
